TPU v7x, 256 devices: a whole 4x4x8 slice. The times are simulated.
256 devices in a mesh: dp: 8 (over x, core), seq: 32 (over z, y).
Axes of the slice: x: 4, y: 4, z: 8, core: 2. Of those that a mesh axis runs over, the one named last changes fastest.
Arguments:
- layer_input: bfloat16 [8, 4096, 4096], P('dp', 'seq'), may hold values from -6 to 6
- proj_weight: bfloat16 [4096, 256], replicated, may hold values from -0.0078125 to 0.0078125
- inputs: bfloat16 [8, 4096, 2048], P('dp', 'seq'), may hold values from -6 to 6
- step_size: float32 [8, 32, 4096], P('dp', None, 'seq'), may hold values from 0.02 to 0.2
- log_decay: float32 [8, 32, 4096], P('dp', None, 'seq'), may hold values from -0.8 to 0, as said below
- skip_gain: float32 [32], replicated, may hold values from 0.1 to 1.9
- grad_out: bfloat16 [8, 4096, 2048], P('dp', 'seq'), may hold values from -6 to 6
Outputs:
- grad_inputs: bfloat16 [8, 4096, 2048], P('dp', 'seq')
- grad_weight: float32 [4096, 256], P(('dp', 'seq'))
Inputs may be any that keep to these rules, and one draw needn't show every extreme that they name: `log_decay`: every entry is negative.
All inputs are finite; a program needn't handle non-finite values.
Results may differ from a plain program's by a relative error of at most 0.0069.
Values sent between devices are 32-bit elements; how exact they have to be, the bound alone decides.
A program may use at most 192 MiB of HBM per device.

v0:
```python
import jax
import jax.numpy as jnp
from jax import lax
from jax.sharding import PartitionSpec as P

SHARD_CHANNELS = 32
HEAD_DIM = 64
STATE = 128
SPAN = 128


def prefix(value, axis, combine, identity, reverse):
    length, position = (lax.axis_size(axis), lax.axis_index(axis))
    everything = jax.tree.map(lambda part: lax.all_gather(part, axis), value)
    start = jax.tree.map(
        lambda part, zero: jnp.broadcast_to(jnp.asarray(zero, part.dtype), part.shape),
        value,
        identity,
    )

    def step(k, before):
        at = length - 1 - k if reverse else k
        reached = at > position if reverse else at < position
        new = combine(before, jax.tree.map(lambda part: part[at], everything))
        return jax.tree.map(lambda a, b: jnp.where(reached, a, b), new, before)

    return lax.fori_loop(0, length, step, start)


def span_inputs(proj, inputs, grad_out, step_size, log_decay):
    length = inputs.shape[0]
    spans = length // SPAN
    b_cols = proj[:, :STATE].reshape(spans, SPAN, STATE)
    c_cols = proj[:, STATE:].reshape(spans, SPAN, STATE)
    inputs_c = inputs.reshape(spans, SPAN, SHARD_CHANNELS, HEAD_DIM)
    grad_rows = grad_out.reshape(spans, SPAN, SHARD_CHANNELS, HEAD_DIM)
    step_rows = step_size.reshape(SHARD_CHANNELS, spans, SPAN).transpose(1, 0, 2)
    decay_sum = jnp.cumsum(
        log_decay.reshape(SHARD_CHANNELS, spans, SPAN).transpose(1, 0, 2), axis=2
    )
    span_total = decay_sum[:, :, -1]
    to_end = jnp.exp(span_total[:, :, None] - decay_sum)
    weighted = (
        inputs_c.astype(jnp.float32) * jnp.transpose(step_rows * to_end, (0, 2, 1))[..., None]
    ).astype(jnp.bfloat16)
    scaled = (
        grad_rows.astype(jnp.float32) * jnp.transpose(jnp.exp(decay_sum), (0, 2, 1))[..., None]
    ).astype(jnp.bfloat16)
    own_state = jnp.einsum("cqhp,cqn->chpn", weighted, b_cols, preferred_element_type=jnp.float32)
    own_grad = jnp.einsum("cqhp,cqn->chpn", scaled, c_cols, preferred_element_type=jnp.float32)
    return (
        b_cols,
        c_cols,
        inputs_c,
        grad_rows,
        step_rows,
        decay_sum,
        span_total,
        weighted,
        scaled,
        own_state,
        own_grad,
    )


def span_grads(
    b_cols,
    c_cols,
    inputs_c,
    grad_rows,
    step_rows,
    decay_sum,
    span_total,
    weighted,
    scaled,
    start,
    after,
    skip_gain,
):
    start_bf = start.astype(jnp.bfloat16)
    after_bf = after.astype(jnp.bfloat16)
    row_ids = lax.broadcasted_iota(jnp.int32, (SPAN, SPAN), 0)
    col_ids = lax.broadcasted_iota(jnp.int32, (SPAN, SPAN), 1)
    causal = row_ids >= col_ids
    log_gap = decay_sum[:, :, None] - decay_sum[:, None, :]
    decay_mat = jnp.exp(jnp.where(causal[None], log_gap, -jnp.inf))
    kernel = jnp.dot(c_cols, b_cols.T, preferred_element_type=jnp.float32)
    weights = (decay_mat * kernel[None]).astype(jnp.bfloat16)
    within = jnp.einsum("hsj,shp->jhp", weights, grad_rows, preferred_element_type=jnp.float32)
    carried = jnp.einsum("hpn,jn->jhp", after_bf, b_cols, preferred_element_type=jnp.float32)
    to_end = jnp.exp(span_total[:, None] - decay_sum)
    grad_x = step_rows.T[:, :, None] * (within + to_end.T[:, :, None] * carried) + skip_gain[
        None, :, None
    ] * grad_rows.astype(jnp.float32)
    intersection = jnp.einsum(
        "shp,jhp->hsj", grad_rows, inputs_c, preferred_element_type=jnp.float32
    )
    mixing = jnp.sum(decay_mat * step_rows[:, None, :] * intersection, axis=0).astype(jnp.bfloat16)
    grad_c = jnp.dot(mixing, b_cols, preferred_element_type=jnp.float32) + jnp.dot(
        scaled.reshape(SPAN, -1), start_bf.reshape(-1, STATE), preferred_element_type=jnp.float32
    )
    grad_b = jnp.dot(mixing.T, c_cols, preferred_element_type=jnp.float32) + jnp.dot(
        weighted.reshape(SPAN, -1), after_bf.reshape(-1, STATE), preferred_element_type=jnp.float32
    )
    grad_proj = jnp.concatenate([grad_b, grad_c], axis=1).astype(jnp.bfloat16)
    return (grad_x.astype(jnp.bfloat16).reshape(SPAN, -1), grad_proj)


def chain_step(earlier, later_part):
    return (earlier[0] * later_part[0], later_part[0][:, None, None] * earlier[1] + later_part[1])


def on_device(layer_input, proj_weight, inputs, step_size, log_decay, skip_gain, grad_out):
    tokens = layer_input[0]
    length = tokens.shape[0]
    proj = jnp.dot(tokens, proj_weight, preferred_element_type=jnp.float32).astype(jnp.bfloat16)
    pieces = span_inputs(proj, inputs[0], grad_out[0], step_size[0], log_decay[0])
    own_state, own_grad, span_total = (pieces[9], pieces[10], pieces[6])
    empty_state = jnp.zeros((SHARD_CHANNELS, HEAD_DIM, STATE), jnp.float32)
    unit_decay = jnp.ones((SHARD_CHANNELS,), jnp.float32)

    def advance(state_carry, piece):
        return (jnp.exp(piece[1])[:, None, None] * state_carry + piece[0], state_carry)

    last_state, local_starts = lax.scan(advance, empty_state, (own_state, span_total))
    last_grad, local_afters = lax.scan(advance, empty_state, (own_grad, span_total), reverse=True)
    device_decay = jnp.exp(jnp.sum(span_total, axis=0))
    _, state_entry = prefix(
        (device_decay, last_state), "seq", chain_step, (unit_decay, empty_state), False
    )
    _, grad_entry = prefix(
        (device_decay, last_grad), "seq", chain_step, (unit_decay, empty_state), True
    )
    running = jnp.cumsum(span_total, axis=0)
    before = running - span_total
    behind = jnp.sum(span_total, axis=0)[None] - running
    starts = local_starts + jnp.exp(before)[:, :, None, None] * state_entry[None]
    afters = local_afters + jnp.exp(behind)[:, :, None, None] * grad_entry[None]

    def finish(parts):
        return span_grads(*parts, skip_gain)

    grad_x, grad_proj = lax.map(finish, pieces[:9] + (starts, afters))
    grad_proj = grad_proj.reshape(length, 2 * STATE)
    scale_factor = 1.0 / (length * lax.axis_size("seq"))
    grad_weight = lax.psum_scatter(
        jnp.einsum("ld,ln->dn", tokens, grad_proj, preferred_element_type=jnp.float32)
        * scale_factor,
        ("dp", "seq"),
        scatter_dimension=0,
        tiled=True,
    )
    return (grad_x, grad_weight)


def solution(mesh):
    return jax.shard_map(
        on_device,
        mesh=mesh,
        in_specs=(
            P("dp", "seq", None),
            P(),
            P("dp", "seq", None),
            P("dp", None, "seq"),
            P("dp", None, "seq"),
            P(),
            P("dp", "seq", None),
        ),
        out_specs=(P("dp", "seq", None), P(("dp", "seq"), None)),
        check_vma=False,
    )
```

profile of v0, /device:TPU:32, one launch (start us, length us, event | category | flops | bytes accessed | tf_op | source)
XLA Modules:
  0.0 1813.6 jit_solution(11749552611717270648)
XLA Ops:
  11.3 1.7 convolution_convert_fusion
  15.9 40.3 %all-gather = f32[32,32,1]{1,2,0:T(1,128)S(1)} all-gather(f32[1,32,1]{1,2,0:T(1,128)S(1)} %exp.70), channel_id=2, replica_groups=mesh['dp'=8,'seq'=32] {'seq'}, dimensions={0}, use_global_device_ids=true | all-gather | bytes 4224 | tf_op jit(solution)/shard_map/all_gather | solution.py:14
  57.8 191.0 %all-gather.8.cloned.1.call-done = f32[1024,64,128]{2,1,0:T(8,128)} async-done(((f32[32,64,128]{2,1,0:T(8,128)}), f32[1024,64,128]{2,1,0:T(8,128)}) %all-gather.8.cloned.1.call-update) | async-done | bytes 33554448 | tf_op jit(solution)/shard_map/all_gather | solution.py:14
  248.8 48.5 %while.21 = (s32[]{:T(128)}, f32[32,64,128]{2,1,0:T(8,128)S(1)}, s32[]{:T(128)}, f32[32,32]{1,0:T(8,128)S(1)}, f32[32,32,64,128]{3,2,1,0:T(8,128)}, /*index=5*/s32[]{:T(128)}, s32[]{:T(128)}) while((s32[]{:T(128)}, f32[32,64,128]{2,1,0:T(8,128)S(1)}, s32[]{:T(128)}, f32[32,32]{1,0:T(8,128)S(1)}, f32[32,32,64,128]{3,2,1,0:T(8,128)}, ...), condition=%wide.region_5.6_spmd.clone, body=%wide.region_4.5_spmd.clone.sunk | while | flops 1048580 | bytes 3146217 | solution.py:27
  250.3 1.5 fusion.56
  251.8 1.5 fusion.56
  253.3 1.5 fusion.56
  254.8 1.5 fusion.56
  256.3 1.5 fusion.56
  260.8 1.5 fusion.56
  262.3 1.6 fusion.56
  264.0 1.5 fusion.56
  273.0 1.5 fusion.56
  274.6 1.5 fusion.56
  276.1 1.5 fusion.56
  277.6 1.5 fusion.56
  279.1 1.5 fusion.56
  280.6 1.5 fusion.56
  282.1 1.5 fusion.56
  283.7 1.5 fusion.56
  285.2 1.5 fusion.56
  286.7 1.5 fusion.56
  288.2 1.5 fusion.56
  289.7 1.5 fusion.56
  291.2 1.5 fusion.56
  292.7 1.5 fusion.56
  294.3 1.5 fusion.56
  295.8 1.5 fusion.56
  297.3 184.5 %all-gather.6.cloned.1.call-done = f32[1024,64,128]{2,1,0:T(8,128)} async-done(((f32[32,64,128]{2,1,0:T(8,128)}), f32[1024,64,128]{2,1,0:T(8,128)}) %all-gather.6.cloned.1.call-update) | async-done | bytes 33554448 | tf_op jit(solution)/shard_map/all_gather | solution.py:14
  481.7 48.5 %while.20 = (s32[]{:T(128)}, f32[32,64,128]{2,1,0:T(8,128)S(1)}, s32[]{:T(128)}, f32[32,32]{1,0:T(8,128)S(1)}, f32[32,32,64,128]{3,2,1,0:T(8,128)}, /*index=5*/s32[]{:T(128)}, s32[]{:T(128)}, s32[]{:T(128)}, s32[]{:T(128)}) while((s32[]{:T(128)}, f32[32,64,128]{2,1,0:T(8,128)S(1)}, s32[]{:T(128)}, f32[32,32]{1,0:T(8,128)S(1)}, ...), condition=%wide.region_2.3_spmd.clone, body=%wide.region_1.2_spmd.clone.sunk | while | flops 1048584 | bytes 3146279 | solution.py:27
  483.3 1.5 fusion.55
  484.8 1.5 fusion.55
  486.3 1.5 fusion.55
  487.8 1.5 fusion.55
  489.3 1.5 fusion.55
  490.8 1.5 fusion.55
  492.4 1.5 fusion.55
  493.9 1.5 fusion.55
  495.4 1.5 fusion.55
  496.9 1.5 fusion.55
  498.4 1.5 fusion.55
  500.0 1.5 fusion.55
  501.5 1.5 fusion.55
  503.0 1.5 fusion.55
  504.5 1.5 fusion.55
  506.0 1.5 fusion.55
  507.5 1.5 fusion.55
  509.1 1.5 fusion.55
  510.6 1.5 fusion.55
  512.1 1.5 fusion.55
  513.6 1.5 fusion.55
  515.1 1.5 fusion.55
  516.6 1.5 fusion.55
  518.2 1.5 fusion.55
  519.7 1.5 fusion.55
  521.2 1.5 fusion.55
  522.7 1.5 fusion.55
  524.2 1.5 fusion.55
  525.7 1.5 fusion.55
  527.3 1.5 fusion.55
  528.8 1.5 fusion.55
  531.5 2.6 fusion.2
  534.1 5.6 copy.37
  542.6 1264.5 %reduce-scatter.4.cloned.1.call-done = f32[16,256]{1,0:T(8,128)} async-done(((f32[4096,256]{1,0:T(8,128)}), f32[16,256]{1,0:T(8,128)}) %reduce-scatter.4.cloned.1.call-update) | async-done | bytes 16400
  (113 shorter events, 26.2 us)
Async XLA Ops:
  7.2 4.1 copy-start
  7.2 4.0 copy-start.3
  7.2 241.6 %all-gather.8.cloned.1.call-start = ((), (), s32[]{:S(2)}) async-start(), calls=%async_computation.2 | async-start | bytes 34603008 | tf_op jit(solution)/shard_map/all_gather | solution.py:14
  14.5 467.3 %all-gather.6.cloned.1.call-start = ((), (), s32[]{:S(2)}) async-start(), calls=%async_computation.1 | async-start | bytes 34603008 | tf_op jit(solution)/shard_map/all_gather | solution.py:14
  15.8 1791.3 %reduce-scatter.4.cloned.1.call-start = ((), (), s32[]{:S(2)}) async-start(), calls=%async_computation.3 | async-start | bytes 4210688
  530.3 1.2 copy-start.2
  539.8 0.7 copy-start.4
  540.4 1266.7 %copy-start.1 = (bf16[4096,256]{1,0:T(8,128)(2,1)S(1)}, bf16[4096,256]{1,0:T(8,128)(2,1)}, u32[]{:S(2)}) copy-start(bf16[4096,256]{1,0:T(8,128)(2,1)} %param.12) | copy-start | bytes 6291460
Sparse Core Ops, SparseCore 0:
  14.6 234.1 all-gather.7
  251.4 230.3 all-gather.5
  539.9 1267.1 reduce-scatter.3
where the time goes:
time: 1820 us; the launch traced here: 1810 us
  waiting for transfers between devices  1640 us (90%)
  other arithmetic  95.6 us (5%)
  blocking collectives  40.3 us (2%)
    unnamed x4, waiting for transfers between devices  1260 us
    all_gather x2, waiting for transfers between devices, prefix(): everything = jax.tree.map(lambda part: lax.all_gather(part, axis), value)  375 us
    select_n x64, other arithmetic, step(): return jax.tree.map(lambda a, b: jnp.where(reached, a, b), new, before)  94 us
    all_gather x1, blocking collectives, prefix(): everything = jax.tree.map(lambda part: lax.all_gather(part, axis), value)  40.3 us
  transfers between devices with their start and end apart: 3, of which 3 were waited for; matrix products, arithmetic and copies ran while one was open for 3% of the time, Pallas kernels for 0%

commit v1 on v0

--- a/solution.py
+++ b/solution.py
@@ -7,24 +7,6 @@
 HEAD_DIM = 64
 STATE = 128
 SPAN = 128
-
-
-def prefix(value, axis, combine, identity, reverse):
-    length, position = (lax.axis_size(axis), lax.axis_index(axis))
-    everything = jax.tree.map(lambda part: lax.all_gather(part, axis), value)
-    start = jax.tree.map(
-        lambda part, zero: jnp.broadcast_to(jnp.asarray(zero, part.dtype), part.shape),
-        value,
-        identity,
-    )
-
-    def step(k, before):
-        at = length - 1 - k if reverse else k
-        reached = at > position if reverse else at < position
-        new = combine(before, jax.tree.map(lambda part: part[at], everything))
-        return jax.tree.map(lambda a, b: jnp.where(reached, a, b), new, before)
-
-    return lax.fori_loop(0, length, step, start)
 
 
 def span_inputs(proj, inputs, grad_out, step_size, log_decay):
@@ -106,8 +88,42 @@
     return (grad_x.astype(jnp.bfloat16).reshape(SPAN, -1), grad_proj)
 
 
-def chain_step(earlier, later_part):
-    return (earlier[0] * later_part[0], later_part[0][:, None, None] * earlier[1] + later_part[1])
+def exchange(own_state, own_grad, device_total):
+    count = lax.axis_size("seq")
+    heads, rows, cols = own_state.shape
+    marks = jnp.broadcast_to(device_total[:, None, None], (heads, 8, cols))
+    payload = jnp.stack(
+        [
+            jnp.concatenate([own_state, marks], axis=1),
+            jnp.concatenate([own_grad, marks], axis=1),
+        ]
+    )
+    mine = lax.all_to_all(payload, "seq", 1, 1, tiled=True)
+    totals = mine[0, :, rows, 0]
+    ends = mine[:, :, :rows, :].reshape(2, count, rows * cols)
+    ids = jnp.arange(count)
+    target, source, between = ids[:, None, None], ids[None, :, None], ids[None, None, :]
+    fwd_span = (source < between) & (between < target)
+    bwd_span = (target < between) & (between < source)
+    fwd_log = jnp.sum(jnp.where(fwd_span, totals[None, None, :], 0.0), axis=2)
+    bwd_log = jnp.sum(jnp.where(bwd_span, totals[None, None, :], 0.0), axis=2)
+    fwd_w = jnp.where(ids[None, :] < ids[:, None], jnp.exp(fwd_log), 0.0)
+    bwd_w = jnp.where(ids[None, :] > ids[:, None], jnp.exp(bwd_log), 0.0)
+    weights = jnp.stack([fwd_w, bwd_w])
+    entries = jnp.einsum(
+        "ktj,kjx->ktx", weights, ends, precision=lax.Precision.HIGHEST,
+        preferred_element_type=jnp.float32,
+    ).reshape(2, count, rows, cols)
+    back = lax.all_to_all(entries, "seq", 1, 1, tiled=True)
+    return back[0], back[1]
+
+
+def scatter_rows(term):
+    dp, seq = lax.axis_size("dp"), lax.axis_size("seq")
+    rows, cols = term.shape
+    part = lax.all_to_all(term.reshape(dp, rows // dp, cols), "dp", 0, 0, tiled=True).sum(0)
+    part = lax.all_to_all(part.reshape(seq, rows // dp // seq, cols), "seq", 0, 0, tiled=True)
+    return part.sum(0)
 
 
 def on_device(layer_input, proj_weight, inputs, step_size, log_decay, skip_gain, grad_out):
@@ -117,20 +133,13 @@
     pieces = span_inputs(proj, inputs[0], grad_out[0], step_size[0], log_decay[0])
     own_state, own_grad, span_total = (pieces[9], pieces[10], pieces[6])
     empty_state = jnp.zeros((SHARD_CHANNELS, HEAD_DIM, STATE), jnp.float32)
-    unit_decay = jnp.ones((SHARD_CHANNELS,), jnp.float32)
 
     def advance(state_carry, piece):
         return (jnp.exp(piece[1])[:, None, None] * state_carry + piece[0], state_carry)
 
     last_state, local_starts = lax.scan(advance, empty_state, (own_state, span_total))
     last_grad, local_afters = lax.scan(advance, empty_state, (own_grad, span_total), reverse=True)
-    device_decay = jnp.exp(jnp.sum(span_total, axis=0))
-    _, state_entry = prefix(
-        (device_decay, last_state), "seq", chain_step, (unit_decay, empty_state), False
-    )
-    _, grad_entry = prefix(
-        (device_decay, last_grad), "seq", chain_step, (unit_decay, empty_state), True
-    )
+    state_entry, grad_entry = exchange(last_state, last_grad, jnp.sum(span_total, axis=0))
     running = jnp.cumsum(span_total, axis=0)
     before = running - span_total
     behind = jnp.sum(span_total, axis=0)[None] - running
@@ -143,13 +152,8 @@
     grad_x, grad_proj = lax.map(finish, pieces[:9] + (starts, afters))
     grad_proj = grad_proj.reshape(length, 2 * STATE)
     scale_factor = 1.0 / (length * lax.axis_size("seq"))
-    grad_weight = lax.psum_scatter(
-        jnp.einsum("ld,ln->dn", tokens, grad_proj, preferred_element_type=jnp.float32)
-        * scale_factor,
-        ("dp", "seq"),
-        scatter_dimension=0,
-        tiled=True,
-    )
+    term = jnp.einsum("ld,ln->dn", tokens, grad_proj, preferred_element_type=jnp.float32)
+    grad_weight = scatter_rows(term) * scale_factor
     return (grad_x, grad_weight)
 
 

time: 1820 us -> 237 us (0.13)
  waiting for transfers between devices: 1640 us -> 115 us
  other arithmetic: 95.6 us -> 11.4 us
  starting transfers between devices: 0.12 us -> 24.6 us
    unnamed x4 -> x0, waiting for transfers between devices: 1260 us -> none
    all_gather x2 -> x0, waiting for transfers between devices: 375 us -> none  [prefix(): everything = jax.tree.map(lambda part: lax.all_gather(part, axis), value)]
    all_to_all x0 -> x3, waiting for transfers between devices: none -> 115 us  [the longest x1 55.3 us: exchange(): mine = lax.all_to_all(payload, 'seq', 1, 1, tiled=True)]
    select_n x64 -> x2, other arithmetic: 94 us -> 0.02 us  [the longest x1 0.01 us: exchange(): fwd_w = jnp.where(ids[None, :] < ids[:, None], jnp.exp(fwd_log), 0.0)]
    all_to_all x0 -> x1, blocking collectives: none -> 54.5 us  [scatter_rows(): lax.all_to_all(term.reshape(dp, rows // dp, cols), 'dp', 0, 0, tiled=True)]
    all_gather x1 -> x0, blocking collectives: 40.3 us -> none  [prefix(): everything = jax.tree.map(lambda part: lax.all_gather(part, axis), value)]
    all_to_all x0 -> x3, starting transfers between devices: none -> 24.6 us  [the longest x1 11.4 us: exchange(): mine = lax.all_to_all(payload, 'seq', 1, 1, tiled=True)]
  transfers between devices with their start and end apart: 3 -> 3, of which waited for: 3 -> 3; matrix products, arithmetic and copies ran while one was open for 3% -> 2% of each run, Pallas kernels for 0% -> 0%
where the time goes in v1:
time: 237 us; the launch traced here: 236 us
  waiting for transfers between devices  115 us (49%)
  blocking collectives  54.5 us (23%)
  starting transfers between devices  24.6 us (10%)
  local copies, waits for them, and re-layouts  17.8 us (8%)
  other arithmetic  11.4 us (5%)
  matrix products  11.3 us (5%)
    all_to_all x1, waiting for transfers between devices, exchange(): mine = lax.all_to_all(payload, 'seq', 1, 1, tiled=True)  55.3 us
    all_to_all x1, blocking collectives, scatter_rows(): lax.all_to_all(term.reshape(dp, rows // dp, cols), 'dp', 0, 0, tiled=True)  54.5 us
    all_to_all x1, waiting for transfers between devices, exchange(): back = lax.all_to_all(entries, 'seq', 1, 1, tiled=True)  45.9 us
    all_to_all x1, waiting for transfers between devices, scatter_rows(): lax.all_to_all(part.reshape(seq, rows // dp // seq, cols), 'seq', 0, 0, t...  14.2 us
    all_to_all x1, starting transfers between devices, exchange(): mine = lax.all_to_all(payload, 'seq', 1, 1, tiled=True)  11.4 us
    all_to_all x1, starting transfers between devices, exchange(): back = lax.all_to_all(entries, 'seq', 1, 1, tiled=True)  6.64 us
    all_to_all x1, starting transfers between devices, scatter_rows(): lax.all_to_all(part.reshape(seq, rows // dp // seq, cols), 'seq', 0, 0, t...  6.52 us
  transfers between devices with their start and end apart: 3, of which 3 were waited for; matrix products, arithmetic and copies ran while one was open for 2% of the time, Pallas kernels for 0%

profile of v1, /device:TPU:32, one launch (start us, length us, event | category | flops | bytes accessed | tf_op | source)
XLA Modules:
  0.0 235.9 jit_solution(15632578017909510652)
XLA Ops:
  0.6 0.0 copy-start
  0.6 1.1 reduce_window_sum.17
  1.8 0.2 slice_reduce_fusion.1
  2.0 0.8 multiply_bitcast_fusion
  2.8 1.3 copy.43
  4.1 1.3 copy.42
  5.4 0.0 copy-done
  5.4 1.7 convolution_convert_fusion
  7.1 0.2 fusion.13
  7.3 0.3 convolution_add_fusion.1
  7.6 0.3 convolution_add_fusion
  7.9 0.1 broadcast_in_dim.100
  8.0 0.2 fusion.6
  8.2 0.2 pad_maximum_fusion
  8.4 1.6 copy.45
  9.9 11.4 %all-to-all-start = ((f32[2,32,72,128]{3,2,0,1:T(8,128)}), f32[2,32,72,128]{3,2,0,1:T(8,128)}, u32[]{:S(2)}, u32[]{:S(2)}) async-start(f32[2,32,72,128]{3,2,0,1:T(8,128)} %copy.45), calls=%async_computation | async-start | bytes 4718592 | tf_op jit(solution)/shard_map/all_to_all | solution.py:101
  21.4 55.3 %all-to-all-done = f32[2,32,72,128]{3,2,0,1:T(8,128)} async-done(((f32[2,32,72,128]{3,2,0,1:T(8,128)}), f32[2,32,72,128]{3,2,0,1:T(8,128)}, u32[]{:S(2)}, u32[]{:S(2)}) %all-to-all-start) | async-done | bytes 2359328 | tf_op jit(solution)/shard_map/all_to_all | solution.py:101
  76.7 3.2 %slice.32 = f32[2,32,64,128]{3,2,0,1:T(8,128)} slice(f32[2,32,72,128]{3,2,0,1:T(8,128)} %all-to-all-done), slice={[0:2], [0:32], [0:64], [0:128]} | slice | bytes 4194304 | tf_op jit(solution)/shard_map/slice | solution.py:103
  79.9 3.4 %reshape.335 = f32[2,32,8192]{2,0,1:T(2,128)} reshape(f32[2,32,64,128]{3,2,0,1:T(8,128)} %slice.32) | data formatting | bytes 4194304 | tf_op jit(solution)/shard_map/reshape | solution.py:103
  83.3 1.2 slice_reduce_fusion
  84.5 0.3 select_reduce_fusion.1
  84.9 4.5 %fusion = f32[2,32,8192]{2,1,0:T(8,128)S(1)} fusion(f32[2,32,8192]{2,0,1:T(2,128)} %reshape.335, f32[1,32,32]{2,1,0:T(8,128)S(1)} %bitcast_select_fusion, f32[1,32,32]{2,1,0:T(8,128)S(1)} %bitcast_select_fusion.1), kind=kOutput, calls=%fused_computation.2 | convolution fusion | flops 201328640 | bytes 4202496 | tf_op jit(solution)/shard_map/ktj,kjx->ktx/dot_general | solution.py:113
  89.4 0.4 copy.56
  89.8 1.4 copy.47
  91.3 0.0 copy-start.4
  91.3 6.6 %all-to-all-start.1 = ((f32[2,32,64,128]{3,2,0,1:T(8,128)}), f32[2,32,64,128]{3,2,0,1:T(8,128)}, u32[]{:S(2)}, u32[]{:S(2)}) async-start(f32[2,32,64,128]{3,2,0,1:T(8,128)} %copy.47), calls=%async_computation.1 | async-start | bytes 4194304 | tf_op jit(solution)/shard_map/all_to_all | solution.py:117
  97.9 0.0 copy-done.4
  97.9 1.1 multiply_reduce_fusion
  99.1 0.2 fusion.39
  99.3 0.2 fusion.33
  99.5 1.3 fusion.10
  100.8 45.9 %all-to-all-done.1 = f32[2,32,64,128]{3,2,0,1:T(8,128)} async-done(((f32[2,32,64,128]{3,2,0,1:T(8,128)}), f32[2,32,64,128]{3,2,0,1:T(8,128)}, u32[]{:S(2)}, u32[]{:S(2)}) %all-to-all-start.1) | async-done | bytes 2097184 | tf_op jit(solution)/shard_map/all_to_all | solution.py:117
  146.7 0.0 copy-start.3
  146.7 0.0 copy-start.2
  146.7 0.0 copy-start.1
  146.7 1.9 fusion.11
  148.6 0.0 copy-done.3
  148.6 0.3 fusion.9
  149.0 0.0 copy-done.2
  149.0 0.4 fusion.8
  149.4 0.0 copy-done.1
  149.4 0.7 fusion.15
  150.1 0.6 copy.60
  150.7 54.5 %all_to_all.20 = f32[8,512,256]{1,2,0:T(8,128)} all-to-all(f32[8,512,256]{1,2,0:T(8,128)S(1)} %bitcast.93), channel_id=1, replica_groups=mesh['dp'=8,'seq'=32] {'dp'}, dimensions={0} | all-to-all | bytes 8388608 | tf_op jit(solution)/shard_map/all_to_all | solution.py:124
  205.2 3.5 %reduce_sum.57 = f32[512,256]{0,1:T(8,128)} reduce(f32[8,512,256]{1,2,0:T(8,128)} %all_to_all.20, f32[]{:T(128)} %constant.57.clone.1), dimensions={0}, to_apply=%region_4.5 | reduce | flops 917504 | bytes 4718596 | tf_op jit(solution)/shard_map/reduce_sum | solution.py:124
  208.7 0.0 copy-start.5
  208.7 2.1 copy.51
  210.8 6.5 %all-to-all-start.3 = ((f32[32,16,256]{2,1,0:T(8,128)}), f32[32,16,256]{2,1,0:T(8,128)}, u32[]{:S(2)}, u32[]{:S(2)}) async-start(f32[32,16,256]{2,1,0:T(8,128)} %bitcast.102), calls=%async_computation.3 | async-start | bytes 1048576 | tf_op jit(solution)/shard_map/all_to_all | solution.py:125
  217.3 0.1 exponential_bitcast_fusion.1
  217.4 0.1 fusion.36
  217.5 0.3 convolution_multiply_fusion
  217.8 0.0 copy-done.5
  217.8 1.2 fusion.5
  219.0 1.0 copy.52
  220.0 14.2 %all-to-all-done.3 = f32[32,16,256]{2,1,0:T(8,128)} async-done(((f32[32,16,256]{2,1,0:T(8,128)}), f32[32,16,256]{2,1,0:T(8,128)}, u32[]{:S(2)}, u32[]{:S(2)}) %all-to-all-start.3) | async-done | bytes 524320 | tf_op jit(solution)/shard_map/all_to_all | solution.py:125
  234.2 1.1 reduce_sum.58
  235.3 0.6 broadcast_multiply_fusion
  (5 shorter events, 0.1 us)
Async XLA Ops:
  0.6 4.8 %copy-start = (bf16[4096,256]{1,0:T(8,128)(2,1)S(1)}, bf16[4096,256]{1,0:T(8,128)(2,1)}, u32[]{:S(2)}) copy-start(bf16[4096,256]{1,0:T(8,128)(2,1)} %param.8) | copy-start | bytes 6291460
  9.9 66.7 %all-to-all-start = ((f32[2,32,72,128]{3,2,0,1:T(8,128)}), f32[2,32,72,128]{3,2,0,1:T(8,128)}, u32[]{:S(2)}, u32[]{:S(2)}) async-start(f32[2,32,72,128]{3,2,0,1:T(8,128)} %copy.45), calls=%async_computation | async-start | bytes 4718592 | tf_op jit(solution)/shard_map/all_to_all | solution.py:101
  91.3 6.7 %copy-start.4 = (f32[1,32,128]{2,1,0:T(8,128)S(1)}, f32[1,32,128]{2,1,0:T(8,128)}, u32[]{:S(2)}) copy-start(f32[1,32,128]{2,1,0:T(8,128)} %param.10) | copy-start | bytes 49156
  91.3 55.4 %all-to-all-start.1 = ((f32[2,32,64,128]{3,2,0,1:T(8,128)}), f32[2,32,64,128]{3,2,0,1:T(8,128)}, u32[]{:S(2)}, u32[]{:S(2)}) async-start(f32[2,32,64,128]{3,2,0,1:T(8,128)} %copy.47), calls=%async_computation.1 | async-start | bytes 4194304 | tf_op jit(solution)/shard_map/all_to_all | solution.py:117
  146.7 1.9 copy-start.3
  146.7 2.3 copy-start.2
  146.7 2.7 %copy-start.1 = (bf16[1,128,4096]{2,1,0:T(8,128)(2,1)S(1)}, bf16[1,128,4096]{2,1,0:T(8,128)(2,1)}, u32[]{:S(2)}) copy-start(bf16[1,128,4096]{2,1,0:T(8,128)(2,1)} %param.7) | copy-start | bytes 3145732
  208.7 9.1 %copy-start.5 = (f32[32]{0:T(128)S(1)}, f32[32]{0:T(128)}, u32[]{:S(2)}) copy-start(f32[32]{0:T(128)} %param.12) | copy-start | bytes 388
  210.8 23.4 %all-to-all-start.3 = ((f32[32,16,256]{2,1,0:T(8,128)}), f32[32,16,256]{2,1,0:T(8,128)}, u32[]{:S(2)}, u32[]{:S(2)}) async-start(f32[32,16,256]{2,1,0:T(8,128)} %bitcast.102), calls=%async_computation.3 | async-start | bytes 1048576 | tf_op jit(solution)/shard_map/all_to_all | solution.py:125

commit v2 on v1

--- a/solution.py
+++ b/solution.py
@@ -1,7 +1,7 @@
 import jax
 import jax.numpy as jnp
 from jax import lax
-from jax.sharding import PartitionSpec as P
+from jax.sharding import Mesh, PartitionSpec as P
 
 SHARD_CHANNELS = 32
 HEAD_DIM = 64
@@ -89,7 +89,7 @@
 
 
 def exchange(own_state, own_grad, device_total):
-    count = lax.axis_size("seq")
+    count = lax.axis_size("z") * lax.axis_size("y")
     heads, rows, cols = own_state.shape
     marks = jnp.broadcast_to(device_total[:, None, None], (heads, 8, cols))
     payload = jnp.stack(
@@ -98,7 +98,7 @@
             jnp.concatenate([own_grad, marks], axis=1),
         ]
     )
-    mine = lax.all_to_all(payload, "seq", 1, 1, tiled=True)
+    mine = lax.all_to_all(payload, ("z", "y"), 1, 1, tiled=True)
     totals = mine[0, :, rows, 0]
     ends = mine[:, :, :rows, :].reshape(2, count, rows * cols)
     ids = jnp.arange(count)
@@ -114,15 +114,18 @@
         "ktj,kjx->ktx", weights, ends, precision=lax.Precision.HIGHEST,
         preferred_element_type=jnp.float32,
     ).reshape(2, count, rows, cols)
-    back = lax.all_to_all(entries, "seq", 1, 1, tiled=True)
+    back = lax.all_to_all(entries, ("z", "y"), 1, 1, tiled=True)
     return back[0], back[1]
 
 
 def scatter_rows(term):
-    dp, seq = lax.axis_size("dp"), lax.axis_size("seq")
+    cores, chips = lax.axis_size("core"), lax.axis_size("x")
+    seq = lax.axis_size("z") * lax.axis_size("y")
     rows, cols = term.shape
-    part = lax.all_to_all(term.reshape(dp, rows // dp, cols), "dp", 0, 0, tiled=True).sum(0)
-    part = lax.all_to_all(part.reshape(seq, rows // dp // seq, cols), "seq", 0, 0, tiled=True)
+    part = term.reshape(chips, cores, rows // (chips * cores), cols)
+    part = lax.all_to_all(part, "core", 1, 1, tiled=True).sum(1)
+    part = lax.all_to_all(part, "x", 0, 0, tiled=True).sum(0)
+    part = lax.all_to_all(part.reshape(seq, -1, cols), ("z", "y"), 0, 0, tiled=True)
     return part.sum(0)
 
 
@@ -151,25 +154,35 @@
 
     grad_x, grad_proj = lax.map(finish, pieces[:9] + (starts, afters))
     grad_proj = grad_proj.reshape(length, 2 * STATE)
-    scale_factor = 1.0 / (length * lax.axis_size("seq"))
+    scale_factor = 1.0 / (length * lax.axis_size("z") * lax.axis_size("y"))
     term = jnp.einsum("ld,ln->dn", tokens, grad_proj, preferred_element_type=jnp.float32)
     grad_weight = scatter_rows(term) * scale_factor
     return (grad_x, grad_weight)
 
 
+def physical_mesh(mesh):
+    grid = mesh.devices
+    cores = len({d.core_on_chip for d in grid.flat})
+    rows = len({d.coords[1] for d in grid.flat})
+    dp, seq = grid.shape
+    return Mesh(grid.reshape(dp // cores, cores, seq // rows, rows), ("x", "core", "z", "y"))
+
+
 def solution(mesh):
+    fine = physical_mesh(mesh)
+    dp, seq = ("x", "core"), ("z", "y")
     return jax.shard_map(
         on_device,
-        mesh=mesh,
+        mesh=fine,
         in_specs=(
-            P("dp", "seq", None),
+            P(dp, seq, None),
             P(),
-            P("dp", "seq", None),
-            P("dp", None, "seq"),
-            P("dp", None, "seq"),
+            P(dp, seq, None),
+            P(dp, None, seq),
+            P(dp, None, seq),
             P(),
-            P("dp", "seq", None),
+            P(dp, seq, None),
         ),
-        out_specs=(P("dp", "seq", None), P(("dp", "seq"), None)),
+        out_specs=(P(dp, seq, None), P(dp + seq, None)),
         check_vma=False,
     )

time: 237 us -> 238 us (level)
  blocking collectives: 54.5 us -> 39 us
  local copies, waits for them, and re-layouts: 17.8 us -> 29.3 us
  other arithmetic: 11.4 us -> 15.7 us
    all_to_all x1 -> x2, blocking collectives: 54.5 us -> 39 us  [the longest x1 30.8 us: scatter_rows(): part = lax.all_to_all(part, 'x', 0, 0, tiled=True).sum(0)]
    reshape x1 -> x2, local copies, waits for them, and re-layouts: 0.62 us -> 9.84 us  [scatter_rows(): part = term.reshape(chips, cores, rows // (chips * cores), cols)]
    reduce_sum x1 -> x2, other arithmetic: 3.49 us -> 7.73 us  [the longest x1 5.07 us: scatter_rows(): part = lax.all_to_all(part, 'core', 1, 1, tiled=True).sum(1)]
where the time goes in v2:
time: 238 us; the launch traced here: 237 us
  waiting for transfers between devices  115 us (48%)
  blocking collectives  39 us (16%)
  local copies, waits for them, and re-layouts  29.3 us (12%)
  starting transfers between devices  24.6 us (10%)
  other arithmetic  15.7 us (7%)
  matrix products  13.2 us (6%)
    all_to_all x1, waiting for transfers between devices, exchange(): mine = lax.all_to_all(payload, ('z', 'y'), 1, 1, tiled=True)  55.3 us
    all_to_all x1, waiting for transfers between devices, exchange(): back = lax.all_to_all(entries, ('z', 'y'), 1, 1, tiled=True)  45.9 us
    all_to_all x1, blocking collectives, scatter_rows(): part = lax.all_to_all(part, 'x', 0, 0, tiled=True).sum(0)  30.8 us
    all_to_all x1, waiting for transfers between devices, scatter_rows(): lax.all_to_all(part.reshape(seq, -1, cols), ('z', 'y'), 0, 0, tiled=True)  13.5 us
    all_to_all x1, starting transfers between devices, exchange(): mine = lax.all_to_all(payload, ('z', 'y'), 1, 1, tiled=True)  11.4 us
    reshape x2, local copies, waits for them, and re-layouts, scatter_rows(): part = term.reshape(chips, cores, rows // (chips * cores), cols)  9.84 us
    all_to_all x1, blocking collectives, scatter_rows(): part = lax.all_to_all(part, 'core', 1, 1, tiled=True).sum(1)  8.17 us
    all_to_all x1, starting transfers between devices, exchange(): back = lax.all_to_all(entries, ('z', 'y'), 1, 1, tiled=True)  6.66 us
  transfers between devices with their start and end apart: 3, of which 3 were waited for; matrix products, arithmetic and copies ran while one was open for 2% of the time, Pallas kernels for 0%

profile of v2, /device:TPU:32, one launch (start us, length us, event | category | flops | bytes accessed | tf_op | source)
XLA Modules:
  0.0 237.3 jit_solution(9138814663797119742)
XLA Ops:
  0.6 0.0 copy-start
  0.6 1.1 reduce_window_sum.17
  1.8 0.2 slice_reduce_fusion.1
  2.0 0.8 multiply_bitcast_fusion
  2.8 1.3 copy.57
  4.1 1.3 copy.56
  5.4 0.0 copy-done
  5.4 1.7 convolution_convert_fusion
  7.1 0.2 fusion.13
  7.3 0.3 convolution_add_fusion.1
  7.6 0.3 convolution_add_fusion
  7.9 0.1 broadcast_in_dim.100
  8.0 0.2 fusion.6
  8.2 0.2 pad_maximum_fusion
  8.4 1.6 copy.59
  9.9 11.4 %all-to-all-start = ((f32[2,32,72,128]{3,2,0,1:T(8,128)}), f32[2,32,72,128]{3,2,0,1:T(8,128)}, u32[]{:S(2)}, u32[]{:S(2)}) async-start(f32[2,32,72,128]{3,2,0,1:T(8,128)} %copy.59), calls=%async_computation | async-start | bytes 4718592 | tf_op jit(solution)/shard_map/all_to_all | solution.py:101
  21.4 55.3 %all-to-all-done = f32[2,32,72,128]{3,2,0,1:T(8,128)} async-done(((f32[2,32,72,128]{3,2,0,1:T(8,128)}), f32[2,32,72,128]{3,2,0,1:T(8,128)}, u32[]{:S(2)}, u32[]{:S(2)}) %all-to-all-start) | async-done | bytes 2359328 | tf_op jit(solution)/shard_map/all_to_all | solution.py:101
  76.7 3.2 %slice.32 = f32[2,32,64,128]{3,2,0,1:T(8,128)} slice(f32[2,32,72,128]{3,2,0,1:T(8,128)} %all-to-all-done), slice={[0:2], [0:32], [0:64], [0:128]} | slice | bytes 4194304 | tf_op jit(solution)/shard_map/slice | solution.py:103
  79.9 3.4 %reshape.335 = f32[2,32,8192]{2,0,1:T(2,128)} reshape(f32[2,32,64,128]{3,2,0,1:T(8,128)} %slice.32) | data formatting | bytes 4194304 | tf_op jit(solution)/shard_map/reshape | solution.py:103
  83.3 1.2 slice_reduce_fusion
  84.5 0.3 select_reduce_fusion.1
  84.9 4.5 %fusion = f32[2,32,8192]{2,1,0:T(8,128)S(1)} fusion(f32[2,32,8192]{2,0,1:T(2,128)} %reshape.335, f32[1,32,32]{2,1,0:T(8,128)S(1)} %bitcast_select_fusion, f32[1,32,32]{2,1,0:T(8,128)S(1)} %bitcast_select_fusion.1), kind=kOutput, calls=%fused_computation.2 | convolution fusion | flops 201328640 | bytes 4202496 | tf_op jit(solution)/shard_map/ktj,kjx->ktx/dot_general | solution.py:113
  89.4 0.4 copy.72
  89.8 1.4 copy.61
  91.3 0.0 copy-start.4
  91.3 6.7 %all-to-all-start.1 = ((f32[2,32,64,128]{3,2,0,1:T(8,128)}), f32[2,32,64,128]{3,2,0,1:T(8,128)}, u32[]{:S(2)}, u32[]{:S(2)}) async-start(f32[2,32,64,128]{3,2,0,1:T(8,128)} %copy.61), calls=%async_computation.1 | async-start | bytes 4194304 | tf_op jit(solution)/shard_map/all_to_all | solution.py:117
  97.9 0.0 copy-done.4
  98.0 1.1 multiply_reduce_fusion
  99.1 0.2 fusion.38
  99.3 0.2 fusion.32
  99.5 1.3 fusion.10
  100.8 45.9 %all-to-all-done.1 = f32[2,32,64,128]{3,2,0,1:T(8,128)} async-done(((f32[2,32,64,128]{3,2,0,1:T(8,128)}), f32[2,32,64,128]{3,2,0,1:T(8,128)}, u32[]{:S(2)}, u32[]{:S(2)}) %all-to-all-start.1) | async-done | bytes 2097184 | tf_op jit(solution)/shard_map/all_to_all | solution.py:117
  146.7 0.0 copy-start.3
  146.7 0.0 copy-start.2
  146.7 0.0 copy-start.1
  146.7 1.9 fusion.11
  148.6 0.0 copy-done.3
  148.6 0.3 fusion.9
  149.0 0.0 copy-done.2
  149.0 0.4 fusion.8
  149.4 0.0 copy-done.1
  149.4 2.6 %convolution_bitcast_fusion = f32[4096,256]{0,1:T(8,128)} fusion(bf16[1,128,4096]{2,1,0:T(8,128)(2,1)S(1)} %copy-done.1, bf16[128,128]{0,1:T(8,128)(2,1)S(1)} %fusion.9, bf16[128,128]{0,1:T(8,128)(2,1)S(1)} %fusion.8), kind=kOutput, calls=%fused_computation | convolution fusion | flops 268566528 | bytes 5308416 | tf_op jit(solution)/shard_map/ld,ln->dn/dot_general | solution.py:158
  152.0 6.6 %reshape.331 = f32[4,2,512,256]{2,1,0,3:T(2,128)} reshape(f32[4096,256]{0,1:T(8,128)} %convolution_bitcast_fusion) | data formatting | bytes 8388608 | tf_op jit(solution)/shard_map/reshape | solution.py:125
  158.6 3.3 %copy.63 = f32[4,2,512,256]{2,0,3,1:T(4,128)S(1)} copy(f32[4,2,512,256]{2,1,0,3:T(2,128)} %reshape.331) | data formatting | bytes 8388608 | tf_op jit(solution)/shard_map/reshape | solution.py:125
  161.8 8.2 %all_to_all.25 = f32[4,2,512,256]{2,0,3,1:T(4,128)} all-to-all(f32[4,2,512,256]{2,0,3,1:T(4,128)S(1)} %copy.63), channel_id=1, replica_groups=mesh['x'=4,'core'=2,'z'=8,'y'=4] {'core'}, dimensions={1} | all-to-all | bytes 8388608 | tf_op jit(solution)/shard_map/all_to_all | solution.py:126
  170.0 5.1 %reduce_sum.66 = f32[4,512,256]{1,0,2:T(4,128)} reduce(f32[4,2,512,256]{2,0,3,1:T(4,128)} %all_to_all.25, f32[]{:T(128)} %constant.57.clone.1), dimensions={1}, to_apply=%region_4.5 | reduce | flops 524288 | bytes 6291460 | tf_op jit(solution)/shard_map/reduce_sum | solution.py:126
  175.1 2.3 copy.65
  177.4 30.8 %all_to_all.26 = f32[4,512,256]{1,2,0:T(8,128)} all-to-all(f32[4,512,256]{1,2,0:T(8,128)S(1)} %copy.65), channel_id=1, replica_groups=mesh['x'=4,'core'=2,'z'=8,'y'=4] {'x'}, dimensions={0} | all-to-all | bytes 4194304 | tf_op jit(solution)/shard_map/all_to_all | solution.py:127
  208.2 2.7 %reduce_sum.67 = f32[512,256]{0,1:T(8,128)} reduce(f32[4,512,256]{1,2,0:T(8,128)} %all_to_all.26, f32[]{:T(128)} %constant.57.clone.1), dimensions={0}, to_apply=%region_5.6 | reduce | flops 393216 | bytes 2621444 | tf_op jit(solution)/shard_map/reduce_sum | solution.py:127
  210.8 0.0 copy-start.5
  210.8 2.1 copy.67
  212.9 6.5 %all-to-all-start.4 = ((f32[32,16,256]{2,1,0:T(8,128)}), f32[32,16,256]{2,1,0:T(8,128)}, u32[]{:S(2)}, u32[]{:S(2)}) async-start(f32[32,16,256]{2,1,0:T(8,128)} %bitcast.99), calls=%async_computation.4 | async-start | bytes 1048576 | tf_op jit(solution)/shard_map/all_to_all | solution.py:128
  219.4 0.1 exponential_bitcast_fusion.1
  219.5 0.1 fusion.35
  219.6 0.3 convolution_multiply_fusion
  220.0 0.0 copy-done.5
  220.0 1.2 fusion.5
  221.1 1.0 copy.68
  222.2 13.5 %all-to-all-done.4 = f32[32,16,256]{2,1,0:T(8,128)} async-done(((f32[32,16,256]{2,1,0:T(8,128)}), f32[32,16,256]{2,1,0:T(8,128)}, u32[]{:S(2)}, u32[]{:S(2)}) %all-to-all-start.4) | async-done | bytes 524320 | tf_op jit(solution)/shard_map/all_to_all | solution.py:128
  235.6 1.1 reduce_sum.68
  236.7 0.6 broadcast_multiply_fusion
  (5 shorter events, 0.1 us)
Async XLA Ops:
  0.6 4.8 %copy-start = (bf16[4096,256]{1,0:T(8,128)(2,1)S(1)}, bf16[4096,256]{1,0:T(8,128)(2,1)}, u32[]{:S(2)}) copy-start(bf16[4096,256]{1,0:T(8,128)(2,1)} %param.8) | copy-start | bytes 6291460
  9.9 66.7 %all-to-all-start = ((f32[2,32,72,128]{3,2,0,1:T(8,128)}), f32[2,32,72,128]{3,2,0,1:T(8,128)}, u32[]{:S(2)}, u32[]{:S(2)}) async-start(f32[2,32,72,128]{3,2,0,1:T(8,128)} %copy.59), calls=%async_computation | async-start | bytes 4718592 | tf_op jit(solution)/shard_map/all_to_all | solution.py:101
  91.3 6.7 %copy-start.4 = (f32[1,32,128]{2,1,0:T(8,128)S(1)}, f32[1,32,128]{2,1,0:T(8,128)}, u32[]{:S(2)}) copy-start(f32[1,32,128]{2,1,0:T(8,128)} %param.10) | copy-start | bytes 49156
  91.3 55.4 %all-to-all-start.1 = ((f32[2,32,64,128]{3,2,0,1:T(8,128)}), f32[2,32,64,128]{3,2,0,1:T(8,128)}, u32[]{:S(2)}, u32[]{:S(2)}) async-start(f32[2,32,64,128]{3,2,0,1:T(8,128)} %copy.61), calls=%async_computation.1 | async-start | bytes 4194304 | tf_op jit(solution)/shard_map/all_to_all | solution.py:117
  146.7 1.9 copy-start.3
  146.7 2.3 copy-start.2
  146.7 2.7 %copy-start.1 = (bf16[1,128,4096]{2,1,0:T(8,128)(2,1)S(1)}, bf16[1,128,4096]{2,1,0:T(8,128)(2,1)}, u32[]{:S(2)}) copy-start(bf16[1,128,4096]{2,1,0:T(8,128)(2,1)} %param.7) | copy-start | bytes 3145732
  210.8 9.1 %copy-start.5 = (f32[32]{0:T(128)S(1)}, f32[32]{0:T(128)}, u32[]{:S(2)}) copy-start(f32[32]{0:T(128)} %param.12) | copy-start | bytes 388
  212.9 22.7 %all-to-all-start.4 = ((f32[32,16,256]{2,1,0:T(8,128)}), f32[32,16,256]{2,1,0:T(8,128)}, u32[]{:S(2)}, u32[]{:S(2)}) async-start(f32[32,16,256]{2,1,0:T(8,128)} %bitcast.99), calls=%async_computation.4 | async-start | bytes 1048576 | tf_op jit(solution)/shard_map/all_to_all | solution.py:128

commit v3 on v2

--- a/solution.py
+++ b/solution.py
@@ -1,6 +1,8 @@
 import jax
 import jax.numpy as jnp
 from jax import lax
+from jax.experimental import pallas as pl
+from jax.experimental.pallas import tpu as pltpu
 from jax.sharding import Mesh, PartitionSpec as P
 
 SHARD_CHANNELS = 32
@@ -88,6 +90,57 @@
     return (grad_x.astype(jnp.bfloat16).reshape(SPAN, -1), grad_proj)
 
 
+def group_all_to_all(payload):
+    width = lax.axis_size("y")
+    count = lax.axis_size("z") * width
+
+    def kernel(src_ref, out_ref, land, send_sems, recv_sems, local_sem):
+        chip, core = lax.axis_index("x"), lax.axis_index("core")
+        me = lax.axis_index("z") * width + lax.axis_index("y")
+        local = pltpu.make_async_copy(src_ref.at[me], land.at[me], local_sem)
+        local.start()
+        outgoing = []
+        for step in range(1, count):
+            dest = (me + step) % count
+            copy = pltpu.make_async_remote_copy(
+                src_ref=src_ref.at[dest],
+                dst_ref=land.at[me],
+                send_sem=send_sems.at[step - 1],
+                recv_sem=recv_sems.at[step - 1],
+                device_id=(chip, core, dest // width, dest % width),
+                device_id_type=pl.DeviceIdType.MESH,
+            )
+            copy.start()
+            outgoing.append(copy)
+        local.wait()
+        for step in range(1, count):
+            outgoing[step - 1].wait_send()
+            origin = (me + count - step) % count
+            pltpu.make_async_remote_copy(
+                src_ref=src_ref.at[origin],
+                dst_ref=land.at[origin],
+                send_sem=send_sems.at[step - 1],
+                recv_sem=recv_sems.at[step - 1],
+                device_id=(chip, core, origin // width, origin % width),
+                device_id_type=pl.DeviceIdType.MESH,
+            ).wait_recv()
+        out_ref[...] = land[...]
+
+    return pl.pallas_call(
+        kernel,
+        out_shape=jax.ShapeDtypeStruct(payload.shape, payload.dtype),
+        in_specs=[pl.BlockSpec(memory_space=pltpu.VMEM)],
+        out_specs=pl.BlockSpec(memory_space=pltpu.VMEM),
+        scratch_shapes=[
+            pltpu.VMEM(payload.shape, payload.dtype),
+            pltpu.SemaphoreType.DMA((count - 1,)),
+            pltpu.SemaphoreType.DMA((count - 1,)),
+            pltpu.SemaphoreType.DMA(()),
+        ],
+        compiler_params=pltpu.CompilerParams(has_side_effects=True, vmem_limit_bytes=48 * 1024 * 1024),
+    )(payload)
+
+
 def exchange(own_state, own_grad, device_total):
     count = lax.axis_size("z") * lax.axis_size("y")
     heads, rows, cols = own_state.shape
@@ -96,11 +149,12 @@
         [
             jnp.concatenate([own_state, marks], axis=1),
             jnp.concatenate([own_grad, marks], axis=1),
-        ]
-    )
-    mine = lax.all_to_all(payload, ("z", "y"), 1, 1, tiled=True)
-    totals = mine[0, :, rows, 0]
-    ends = mine[:, :, :rows, :].reshape(2, count, rows * cols)
+        ],
+        axis=1,
+    )
+    mine = group_all_to_all(payload)
+    totals = mine[:, 0, rows, 0]
+    ends = mine[:, :, :rows, :].reshape(count, 2, rows * cols)
     ids = jnp.arange(count)
     target, source, between = ids[:, None, None], ids[None, :, None], ids[None, None, :]
     fwd_span = (source < between) & (between < target)
@@ -111,11 +165,11 @@
     bwd_w = jnp.where(ids[None, :] > ids[:, None], jnp.exp(bwd_log), 0.0)
     weights = jnp.stack([fwd_w, bwd_w])
     entries = jnp.einsum(
-        "ktj,kjx->ktx", weights, ends, precision=lax.Precision.HIGHEST,
+        "ktj,jkx->tkx", weights, ends, precision=lax.Precision.HIGHEST,
         preferred_element_type=jnp.float32,
-    ).reshape(2, count, rows, cols)
-    back = lax.all_to_all(entries, ("z", "y"), 1, 1, tiled=True)
-    return back[0], back[1]
+    ).reshape(count, 2, rows, cols)
+    back = group_all_to_all(entries)
+    return back[:, 0], back[:, 1]
 
 
 def scatter_rows(term):

time: 238 us -> 247 us (1.038)
  Pallas kernels: 0 us -> 129 us
  waiting for transfers between devices: 115 us -> 10.4 us
  starting transfers between devices: 24.6 us -> 14.4 us
  local copies, waits for them, and re-layouts: 29.3 us -> 25.3 us
  other arithmetic: 15.7 us -> 12.1 us
    pallas_call x0 -> x2, Pallas kernels: none -> 129 us  [group_all_to_all(): pl.pallas_call(kernel, out_shape=jax.ShapeDtypeStruct(payload.shape, payl...]
    all_to_all x2 -> x0, waiting for transfers between devices: 101 us -> none  [the longest x1 55.3 us: exchange(): mine = lax.all_to_all(payload, ('z', 'y'), 1, 1, tiled=True)]
    all_to_all x2 -> x0, starting transfers between devices: 18.1 us -> none  [the longest x1 11.4 us: exchange(): mine = lax.all_to_all(payload, ('z', 'y'), 1, 1, tiled=True)]
    all_to_all x1, starting transfers between devices: 6.51 us -> 14.4 us  [scatter_rows(): lax.all_to_all(part.reshape(seq, -1, cols), ('z', 'y'), 0, 0, tiled=True)]
    all_to_all x1, waiting for transfers between devices: 13.5 us -> 10.4 us  [scatter_rows(): lax.all_to_all(part.reshape(seq, -1, cols), ('z', 'y'), 0, 0, tiled=True)]
    slice x2, local copies, waits for them, and re-layouts: 4.42 us -> 1.94 us  [the longest x1 1.62 us: exchange(): ends = mine[:, :, :rows, :].reshape(count, 2, rows * cols)]
    unnamed x16 -> x18, local copies, waits for them, and re-layouts: 4.04 us -> 6.4 us
  transfers between devices with their start and end apart: 3 -> 1, of which waited for: 3 -> 1; matrix products, arithmetic and copies ran while one was open for 2% -> 2% of each run, Pallas kernels for 0% -> 0%
where the time goes in v3:
time: 247 us; the launch traced here: 246 us
  Pallas kernels  129 us (52%)
  blocking collectives  38.6 us (16%)
  local copies, waits for them, and re-layouts  25.3 us (10%)
  matrix products  15.4 us (6%)
  starting transfers between devices  14.4 us (6%)
  other arithmetic  12.1 us (5%)
  waiting for transfers between devices  10.4 us (4%)
    pallas_call x2, Pallas kernels, group_all_to_all(): pl.pallas_call(kernel, out_shape=jax.ShapeDtypeStruct(payload.shape, payl...  129 us
    all_to_all x1, blocking collectives, scatter_rows(): part = lax.all_to_all(part, 'x', 0, 0, tiled=True).sum(0)  30.4 us
    all_to_all x1, starting transfers between devices, scatter_rows(): lax.all_to_all(part.reshape(seq, -1, cols), ('z', 'y'), 0, 0, tiled=True)  14.4 us
    all_to_all x1, waiting for transfers between devices, scatter_rows(): lax.all_to_all(part.reshape(seq, -1, cols), ('z', 'y'), 0, 0, tiled=True)  10.4 us
    reshape x2, local copies, waits for them, and re-layouts, scatter_rows(): part = term.reshape(chips, cores, rows // (chips * cores), cols)  9.84 us
    all_to_all x1, blocking collectives, scatter_rows(): part = lax.all_to_all(part, 'core', 1, 1, tiled=True).sum(1)  8.17 us
    unnamed x18, local copies, waits for them, and re-layouts  6.4 us
    reduce_sum x1, other arithmetic, scatter_rows(): part = lax.all_to_all(part, 'core', 1, 1, tiled=True).sum(1)  5.07 us
  transfers between devices with their start and end apart: 1, of which 1 were waited for; matrix products, arithmetic and copies ran while one was open for 2% of the time, Pallas kernels for 0%

profile of v3, /device:TPU:32, one launch (start us, length us, event | category | flops | bytes accessed | tf_op | source)
XLA Modules:
  0.0 246.1 jit_solution(14283815933509579060)
XLA Ops:
  0.6 0.0 copy-start
  0.7 1.1 reduce_window_sum.17
  1.8 0.2 slice_reduce_fusion
  2.0 0.8 multiply_bitcast_fusion
  2.8 1.3 copy.63
  4.1 0.0 copy-start.5
  4.2 1.3 copy.62
  5.5 0.0 copy-done
  5.5 1.7 convolution_convert_fusion
  7.2 0.0 copy-done.5
  7.2 1.1 multiply_reduce_fusion
  8.3 0.2 fusion.38
  8.5 0.2 fusion.32
  8.7 1.3 fusion.10
  10.0 0.2 fusion.12
  10.2 0.3 convolution_add_fusion.1
  10.5 0.3 convolution_add_fusion
  10.8 0.1 broadcast_in_dim.100
  10.9 0.2 fusion.6
  11.1 0.2 pad_maximum_fusion.src_ref
  11.3 65.6 %shard_map.86 = f32[32,2,72,128]{3,2,1,0:T(8,128)S(1)} custom-call(f32[32,2,72,128]{3,2,1,0:T(8,128)S(1)} %pad_maximum_fusion.src_ref), custom_call_target="tpu_custom_call" | custom-call | tf_op jit(solution)/shard_map/pallas_call | solution.py:129
  76.9 0.3 slice_reduce_fusion.1
  77.2 1.6 slice.24
  78.8 3.4 %reshape.348 = f32[32,2,8192]{2,1,0:T(2,128)} reshape(f32[32,2,64,128]{3,2,1,0:T(8,128)} %slice.24) | data formatting | bytes 4194304 | tf_op jit(solution)/shard_map/reshape | solution.py:157
  82.2 0.3 select_reduce_fusion.1
  82.6 4.7 %fusion = f32[2,8192,32]{1,2,0:T(8,128)S(1)} fusion(f32[32,2,8192]{2,1,0:T(2,128)} %reshape.348, f32[1,32,32]{2,1,0:T(8,128)S(1)} %bitcast_select_fusion, f32[1,32,32]{2,1,0:T(8,128)S(1)} %bitcast_select_fusion.1), kind=kOutput, calls=%fused_computation.2 | convolution fusion | flops 201328640 | bytes 4202496 | tf_op jit(solution)/shard_map/ktj,jkx->tkx/dot_general | solution.py:167
  87.3 0.4 copy.78
  87.7 0.1 copy.75.src_ref
  87.9 63.5 %shard_map.87 = f32[32,2,64,128]{3,2,1,0:T(8,128)S(1)} custom-call(f32[32,2,64,128]{3,2,1,0:T(8,128)S(1)} %copy.75.src_ref), custom_call_target="tpu_custom_call" | custom-call | tf_op jit(solution)/shard_map/pallas_call | solution.py:129
  151.3 0.0 copy-start.1
  151.3 0.0 copy-start.4
  151.4 0.0 copy-start.3
  151.4 0.0 copy-start.2
  151.4 0.2 multiply_convert_fusion.3
  151.6 1.1 copy-done.4
  152.8 0.3 fusion.8
  153.1 0.0 copy-done.1
  153.1 0.2 copy-done.3
  153.3 0.3 fusion.9
  153.7 0.0 copy-done.2
  153.7 2.6 %convolution_bitcast_fusion = f32[4096,256]{0,1:T(8,128)} fusion(bf16[1,128,4096]{2,1,0:T(8,128)(2,1)S(1)} %copy-done.2, bf16[128,128]{0,1:T(8,128)(2,1)S(1)} %fusion.9, bf16[128,128]{0,1:T(8,128)(2,1)S(1)} %fusion.8), kind=kOutput, calls=%fused_computation | convolution fusion | flops 268566528 | bytes 5308416 | tf_op jit(solution)/shard_map/ld,ln->dn/dot_general | solution.py:212
  156.3 6.6 %reshape.350 = f32[4,2,512,256]{2,1,0,3:T(2,128)} reshape(f32[4096,256]{0,1:T(8,128)} %convolution_bitcast_fusion) | data formatting | bytes 8388608 | tf_op jit(solution)/shard_map/reshape | solution.py:179
  162.9 3.3 %copy.69 = f32[4,2,512,256]{2,0,3,1:T(4,128)S(1)} copy(f32[4,2,512,256]{2,1,0,3:T(2,128)} %reshape.350) | data formatting | bytes 8388608 | tf_op jit(solution)/shard_map/reshape | solution.py:179
  166.1 8.2 %all_to_all.15 = f32[4,2,512,256]{2,0,3,1:T(4,128)} all-to-all(f32[4,2,512,256]{2,0,3,1:T(4,128)S(1)} %copy.69), channel_id=1, replica_groups=mesh['x'=4,'core'=2,'z'=8,'y'=4] {'core'}, dimensions={1} | all-to-all | bytes 8388608 | tf_op jit(solution)/shard_map/all_to_all | solution.py:180
  174.3 5.1 %reduce_sum.66 = f32[4,512,256]{1,0,2:T(4,128)} reduce(f32[4,2,512,256]{2,0,3,1:T(4,128)} %all_to_all.15, f32[]{:T(128)} %constant.57.clone.1), dimensions={1}, to_apply=%region_4.5 | reduce | flops 524288 | bytes 6291460 | tf_op jit(solution)/shard_map/reduce_sum | solution.py:180
  179.4 2.3 copy.71
  181.6 30.4 %all_to_all.16 = f32[4,512,256]{1,2,0:T(8,128)} all-to-all(f32[4,512,256]{1,2,0:T(8,128)S(1)} %copy.71), channel_id=1, replica_groups=mesh['x'=4,'core'=2,'z'=8,'y'=4] {'x'}, dimensions={0} | all-to-all | bytes 4194304 | tf_op jit(solution)/shard_map/all_to_all | solution.py:181
  212.0 1.9 reduce_sum.67
  213.9 0.0 copy-start.6
  213.9 1.0 copy.73
  214.9 14.4 %all-to-all-start.2 = ((f32[32,16,256]{2,1,0:T(8,128)}), f32[32,16,256]{2,1,0:T(8,128)S(1)}, u32[]{:S(2)}, u32[]{:S(2)}) async-start(f32[32,16,256]{2,1,0:T(8,128)} %bitcast.103), calls=%async_computation.2 | async-start | bytes 1048576 | tf_op jit(solution)/shard_map/all_to_all | solution.py:182
  229.3 0.1 exponential_bitcast_fusion.1
  229.4 0.1 fusion.35
  229.5 1.6 convolution_multiply_fusion
  231.2 0.0 copy-done.6
  231.2 1.9 fusion.5
  233.0 2.0 copy.74
  235.1 10.4 %all-to-all-done.2 = f32[32,16,256]{2,1,0:T(8,128)S(1)} async-done(((f32[32,16,256]{2,1,0:T(8,128)}), f32[32,16,256]{2,1,0:T(8,128)S(1)}, u32[]{:S(2)}, u32[]{:S(2)}) %all-to-all-start.2) | async-done | bytes 524320 | tf_op jit(solution)/shard_map/all_to_all | solution.py:182
  245.5 0.6 broadcast_multiply_fusion
  (6 shorter events, 0.1 us)
Async XLA Ops:
  0.6 4.9 %copy-start = (bf16[4096,256]{1,0:T(8,128)(2,1)S(1)}, bf16[4096,256]{1,0:T(8,128)(2,1)}, u32[]{:S(2)}) copy-start(bf16[4096,256]{1,0:T(8,128)(2,1)} %param.8) | copy-start | bytes 6291460
  4.1 3.0 %copy-start.5 = (f32[1,32,128]{2,1,0:T(8,128)S(1)}, f32[1,32,128]{2,1,0:T(8,128)}, u32[]{:S(2)}) copy-start(f32[1,32,128]{2,1,0:T(8,128)} %param.10) | copy-start | bytes 49156
  151.3 1.8 copy-start.1
  151.3 1.4 copy-start.4
  151.4 1.9 copy-start.3
  151.4 2.3 copy-start.2
  213.9 17.2 %copy-start.6 = (f32[32]{0:T(128)S(1)}, f32[32]{0:T(128)}, u32[]{:S(2)}) copy-start(f32[32]{0:T(128)} %param.12) | copy-start | bytes 388
  214.9 30.6 %all-to-all-start.2 = ((f32[32,16,256]{2,1,0:T(8,128)}), f32[32,16,256]{2,1,0:T(8,128)S(1)}, u32[]{:S(2)}, u32[]{:S(2)}) async-start(f32[32,16,256]{2,1,0:T(8,128)} %bitcast.103), calls=%async_computation.2 | async-start | bytes 1048576 | tf_op jit(solution)/shard_map/all_to_all | solution.py:182

commit v4 on v3

--- a/solution.py
+++ b/solution.py
@@ -172,15 +172,82 @@
     return back[:, 0], back[:, 1]
 
 
-def scatter_rows(term):
-    cores, chips = lax.axis_size("core"), lax.axis_size("x")
-    seq = lax.axis_size("z") * lax.axis_size("y")
-    rows, cols = term.shape
-    part = term.reshape(chips, cores, rows // (chips * cores), cols)
-    part = lax.all_to_all(part, "core", 1, 1, tiled=True).sum(1)
-    part = lax.all_to_all(part, "x", 0, 0, tiled=True).sum(0)
-    part = lax.all_to_all(part.reshape(seq, -1, cols), ("z", "y"), 0, 0, tiled=True)
-    return part.sum(0)
+def weight_grad_sum(tokens, grad_proj, scale):
+    chips, cores = lax.axis_size("x"), lax.axis_size("core")
+    width = lax.axis_size("y")
+    count = lax.axis_size("z") * width
+    length, depth = tokens.shape
+    cols = grad_proj.shape[1]
+    slab = depth // (chips * cores)
+    piece = slab // count
+    by_owner = tokens.T.reshape(chips, cores, slab, length)
+
+    def kernel(tok_ref, gp_ref, out_ref, send1, land1, acc1, land2, acc2, land3, sems):
+        chip, core = lax.axis_index("x"), lax.axis_index("core")
+        z, y = lax.axis_index("z"), lax.axis_index("y")
+        me = z * width + y
+        other = 1 - core
+        gp = gp_ref[...]
+        for c in range(chips):
+            send1[c] = jnp.dot(tok_ref[c, other], gp, preferred_element_type=jnp.float32)
+        first = pltpu.make_async_remote_copy(
+            src_ref=send1, dst_ref=land1, send_sem=sems.at[0, 0], recv_sem=sems.at[1, 0],
+            device_id=(chip, other, z, y), device_id_type=pl.DeviceIdType.MESH,
+        )
+        first.start()
+        for c in range(chips):
+            acc1[c] = jnp.dot(tok_ref[c, core], gp, preferred_element_type=jnp.float32)
+        first.wait()
+        acc1[...] = acc1[...] + land1[...]
+        second = []
+        for step in range(1, chips):
+            dest = (chip + step) % chips
+            copy = pltpu.make_async_remote_copy(
+                src_ref=acc1.at[dest], dst_ref=land2.at[step - 1], send_sem=sems.at[0, step],
+                recv_sem=sems.at[1, step], device_id=(dest, core, z, y),
+                device_id_type=pl.DeviceIdType.MESH,
+            )
+            copy.start()
+            second.append(copy)
+        for copy in second:
+            copy.wait()
+        total = acc1[chip]
+        for step in range(1, chips):
+            total = total + land2[step - 1]
+        acc2[...] = total.reshape(count, piece, cols)
+        third = []
+        for step in range(1, count):
+            dest = (me + step) % count
+            copy = pltpu.make_async_remote_copy(
+                src_ref=acc2.at[dest], dst_ref=land3.at[step - 1], send_sem=sems.at[0, chips + step],
+                recv_sem=sems.at[1, chips + step], device_id=(chip, core, dest // width, dest % width),
+                device_id_type=pl.DeviceIdType.MESH,
+            )
+            copy.start()
+            third.append(copy)
+        for copy in third:
+            copy.wait()
+        total = acc2[me]
+        for step in range(1, count):
+            total = total + land3[step - 1]
+        out_ref[...] = total * scale
+
+    return pl.pallas_call(
+        kernel,
+        out_shape=jax.ShapeDtypeStruct((piece, cols), jnp.float32),
+        in_specs=[pl.BlockSpec(memory_space=pltpu.VMEM)] * 2,
+        out_specs=pl.BlockSpec(memory_space=pltpu.VMEM),
+        scratch_shapes=[
+            pltpu.VMEM((chips, slab, cols), jnp.float32),
+            pltpu.VMEM((chips, slab, cols), jnp.float32),
+            pltpu.VMEM((chips, slab, cols), jnp.float32),
+            pltpu.VMEM((chips - 1, slab, cols), jnp.float32),
+            pltpu.VMEM((count, piece, cols), jnp.float32),
+            pltpu.VMEM((count - 1, piece, cols), jnp.float32),
+            pltpu.SemaphoreType.DMA((2, chips + count)),
+        ],
+        compiler_params=pltpu.CompilerParams(has_side_effects=True, vmem_limit_bytes=48 * 1024 * 1024),
+    )(by_owner, grad_proj)
 
 
 def on_device(layer_input, proj_weight, inputs, step_size, log_decay, skip_gain, grad_out):
@@ -209,8 +276,7 @@
     grad_x, grad_proj = lax.map(finish, pieces[:9] + (starts, afters))
     grad_proj = grad_proj.reshape(length, 2 * STATE)
     scale_factor = 1.0 / (length * lax.axis_size("z") * lax.axis_size("y"))
-    term = jnp.einsum("ld,ln->dn", tokens, grad_proj, preferred_element_type=jnp.float32)
-    grad_weight = scatter_rows(term) * scale_factor
+    grad_weight = weight_grad_sum(tokens, grad_proj, scale_factor)
     return (grad_x, grad_weight)
 
 

time: 247 us -> 228 us (0.923); the launches traced: 246 us -> 225 us
  Pallas kernels: 129 us -> 192 us
  blocking collectives: 38.6 us -> 0 us
  starting transfers between devices: 14.4 us -> 0 us
  local copies, waits for them, and re-layouts: 25.3 us -> 13.7 us
  waiting for transfers between devices: 10.4 us -> 0 us
  other arithmetic: 12.1 us -> 5.83 us
  matrix products: 15.4 us -> 12 us
    pallas_call x0 -> x1, Pallas kernels: none -> 63.1 us  [weight_grad_sum(): pl.pallas_call(kernel, out_shape=jax.ShapeDtypeStruct((piece, cols), jnp....]
    all_to_all x2 -> x0, blocking collectives: 38.6 us -> none  [the longest x1 30.4 us: scatter_rows(): part = lax.all_to_all(part, 'x', 0, 0, tiled=True).sum(0)]
    all_to_all x1 -> x0, starting transfers between devices: 14.4 us -> none  [scatter_rows(): lax.all_to_all(part.reshape(seq, -1, cols), ('z', 'y'), 0, 0, tiled=True)]
    all_to_all x1 -> x0, waiting for transfers between devices: 10.4 us -> none  [scatter_rows(): lax.all_to_all(part.reshape(seq, -1, cols), ('z', 'y'), 0, 0, tiled=True)]
    reshape x2 -> x0, local copies, waits for them, and re-layouts: 9.84 us -> none  [scatter_rows(): part = term.reshape(chips, cores, rows // (chips * cores), cols)]
    reduce_sum x3 -> x0, other arithmetic: 6.99 us -> none  [the longest x1 5.07 us: scatter_rows(): part = lax.all_to_all(part, 'core', 1, 1, tiled=True).sum(1)]
    reduce_sum x2 -> x0, local copies, waits for them, and re-layouts: 3.26 us -> none  [the longest x1 2.27 us: scatter_rows(): part = lax.all_to_all(part, 'core', 1, 1, tiled=True).sum(1)]
    dot_general x1 -> x0, matrix products: 2.62 us -> none  [on_device(): jnp.einsum('ld,ln->dn', tokens, grad_proj, preferred_element_type=jnp.flo...]
  transfers between devices with their start and end apart: 1 -> 0, of which waited for: 1 -> 0; matrix products, arithmetic and copies ran while one was open for 2% -> 0% of each run, Pallas kernels for 0% -> 0%
where the time goes in v4:
time: 228 us; the launch traced here: 225 us
  Pallas kernels  192 us (84%)
  local copies, waits for them, and re-layouts  13.7 us (6%)
  matrix products  12 us (5%)
  other arithmetic  5.83 us (3%)
    pallas_call x2, Pallas kernels, group_all_to_all(): pl.pallas_call(kernel, out_shape=jax.ShapeDtypeStruct(payload.shape, payl...  129 us
    pallas_call x1, Pallas kernels, weight_grad_sum(): pl.pallas_call(kernel, out_shape=jax.ShapeDtypeStruct((piece, cols), jnp....  63.1 us
    unnamed x35, local copies, waits for them, and re-layouts  6.29 us
    dot_general x1, matrix products, exchange(): jnp.einsum('ktj,jkx->tkx', weights, ends, precision=lax.Precision.HIGHEST...  4.72 us

profile of v4, /device:TPU:32, one launch (start us, length us, event | category | flops | bytes accessed | tf_op | source)
XLA Modules:
  0.0 224.6 jit_solution(2938172722978355270)
XLA Ops:
  0.6 0.0 copy-start
  0.6 0.0 copy-start.8
  0.7 1.2 reduce_window_sum.17
  1.8 0.2 slice_reduce_fusion
  2.0 0.0 copy-start.10
  2.1 0.1 exponential_bitcast_fusion.1
  2.1 0.8 multiply_bitcast_fusion
  2.9 0.0 copy-done
  2.9 0.0 copy-start.12
  3.0 1.7 convolution_convert_fusion
  4.6 0.8 fusion.31
  5.4 0.1 broadcast_in_dim.100
  5.5 0.0 copy-done.8
  5.5 0.3 copy.38
  5.8 0.0 copy-start.4
  5.8 1.5 copy.37
  7.3 0.0 copy-start.1
  7.3 0.0 copy-done.10
  7.3 0.0 copy-done.12
  7.3 1.1 multiply_reduce_fusion
  8.5 0.0 copy-done.4
  8.5 0.0 copy-done.1
  8.5 0.1 fusion.34
  8.6 0.2 fusion.28
  8.8 1.6 copy.43
  10.4 0.0 copy-start.2
  10.4 0.0 copy-start.5
  10.4 2.6 %fusion.10 = (bf16[128,32,64]{0,2,1:T(8,128)(2,1)}, bf16[128,32,64]{0,2,1:T(8,128)(2,1)}) fusion(bf16[128,32,64]{0,2,1:T(8,128)(2,1)} %bitcast.96, f32[128,32]{0,1:T(8,128)S(1)} %get-tuple-element.75, f32[128,32]{0,1:T(8,128)S(1)} %get-tuple-element.74, bf16[128,32,64]{0,2,1:T(8,128)(2,1)} %bitcast.99), kind=kLoop, calls=%fused_computation.25 | loop fusion | flops 1572864 | bytes 2129920 | tf_op jit(solution)/shard_map/convert_element_type | solution.py:32
  13.1 0.0 copy-done.2
  13.1 0.0 copy-done.5
  13.1 0.2 fusion.12
  13.3 0.3 convolution_add_fusion.1
  13.6 0.3 convolution_add_fusion
  13.8 0.2 fusion.6
  14.0 0.2 pad_maximum_fusion.src_ref
  14.2 65.6 %shard_map.86 = f32[32,2,72,128]{3,2,1,0:T(8,128)S(1)} custom-call(f32[32,2,72,128]{3,2,1,0:T(8,128)S(1)} %pad_maximum_fusion.src_ref), custom_call_target="tpu_custom_call" | custom-call | tf_op jit(solution)/shard_map/pallas_call | solution.py:129
  79.8 0.3 slice_reduce_fusion.1
  80.1 1.6 slice.24
  81.7 3.4 %reshape.345 = f32[32,2,8192]{2,1,0:T(2,128)} reshape(f32[32,2,64,128]{3,2,1,0:T(8,128)} %slice.24) | data formatting | bytes 4194304 | tf_op jit(solution)/shard_map/reshape | solution.py:157
  85.1 0.3 select_reduce_fusion.1
  85.5 4.7 %fusion = f32[2,8192,32]{1,2,0:T(8,128)S(1)} fusion(f32[32,2,8192]{2,1,0:T(2,128)} %reshape.345, f32[1,32,32]{2,1,0:T(8,128)S(1)} %bitcast_select_fusion, f32[1,32,32]{2,1,0:T(8,128)S(1)} %bitcast_select_fusion.1), kind=kOutput, calls=%fused_computation.1 | convolution fusion | flops 201328640 | bytes 4202496 | tf_op jit(solution)/shard_map/ktj,jkx->tkx/dot_general | solution.py:167
  90.2 0.4 copy.55
  90.6 0.1 copy.54.src_ref
  90.8 63.4 %shard_map.87 = f32[32,2,64,128]{3,2,1,0:T(8,128)S(1)} custom-call(f32[32,2,64,128]{3,2,1,0:T(8,128)S(1)} %copy.54.src_ref), custom_call_target="tpu_custom_call" | custom-call | tf_op jit(solution)/shard_map/pallas_call | solution.py:129
  154.2 0.0 copy-start.3
  154.2 0.0 copy-start.9
  154.2 0.0 copy-start.11
  154.2 0.0 copy-start.13
  154.2 0.0 copy-start.14
  154.3 0.4 convolution_multiply_fusion
  154.6 0.6 copy-done.3
  155.2 0.0 copy-done.9
  155.2 0.0 copy-done.11
  155.3 0.0 copy-done.13
  155.3 0.0 copy-done.14
  155.3 1.8 fusion.5
  157.1 0.2 multiply_convert_fusion.3
  157.3 0.8 copy-done.7
  158.1 0.3 fusion.8
  158.5 0.0 copy-done.6
  158.5 0.3 fusion.9
  158.8 63.1 %shard_map.88 = f32[16,256]{1,0:T(8,128)S(1)} custom-call(bf16[4,2,512,128]{3,2,1,0:T(8,128)(2,1)S(1)} %bitcast.92, bf16[128,256]{1,0:T(8,128)(2,1)S(1)} %pad_maximum_fusion.3.gp_ref), custom_call_target="tpu_custom_call" | custom-call | tf_op jit(solution)/shard_map/pallas_call | solution.py:235
  221.9 2.0 copy.49
  224.0 0.6 copy.59
  (8 shorter events, 0.1 us)
Async XLA Ops:
  0.6 2.3 %copy-start = (bf16[4096,256]{1,0:T(8,128)(2,1)S(1)}, bf16[4096,256]{1,0:T(8,128)(2,1)}, u32[]{:S(2)}) copy-start(bf16[4096,256]{1,0:T(8,128)(2,1)} %param.8) | copy-start | bytes 6291460
  0.6 4.9 %copy-start.8 = (bf16[1,128,2048]{2,1,0:T(8,128)(2,1)S(1)}, bf16[1,128,2048]{2,1,0:T(8,128)(2,1)}, u32[]{:S(2)}) copy-start(bf16[1,128,2048]{2,1,0:T(8,128)(2,1)} %param.9) | copy-start | bytes 1572868
  2.0 5.3 %copy-start.10 = (pred[128,128]{1,0:T(8,128)(4,1)}, pred[128,128]{1,0:T(8,128)(4,1)S(1)}, u32[]{:S(2)}) copy-start(pred[128,128]{1,0:T(8,128)(4,1)S(1)} %iota_compare_fusion) | copy-start | bytes 49156
  2.9 4.4 %copy-start.12 = (f32[1,32,128]{2,1,0:T(8,128)S(1)}, f32[1,32,128]{2,1,0:T(8,128)}, u32[]{:S(2)}) copy-start(f32[1,32,128]{2,1,0:T(8,128)} %param.10) | copy-start | bytes 49156
  5.8 2.7 %copy-start.4 = (bf16[1,128,2048]{1,2,0:T(8,128)(2,1)}, bf16[1,128,2048]{1,2,0:T(8,128)(2,1)S(1)}, u32[]{:S(2)}) copy-start(bf16[1,128,2048]{1,2,0:T(8,128)(2,1)S(1)} %copy.38) | copy-start | bytes 1572868
  7.3 1.2 copy-start.1
  10.4 2.6 %copy-start.2 = (bf16[1,128,2048]{1,2,0:T(8,128)(2,1)S(1)}, bf16[1,128,2048]{1,2,0:T(8,128)(2,1)}, u32[]{:S(2)}) copy-start(bf16[1,128,2048]{1,2,0:T(8,128)(2,1)} %copy-done.1) | copy-start | bytes 1572868
  10.4 2.6 %copy-start.5 = (bf16[1,128,2048]{1,2,0:T(8,128)(2,1)S(1)}, bf16[1,128,2048]{1,2,0:T(8,128)(2,1)}, u32[]{:S(2)}) copy-start(bf16[1,128,2048]{1,2,0:T(8,128)(2,1)} %copy-done.4) | copy-start | bytes 1572868
  154.2 1.0 copy-start.3
  154.2 1.0 copy-start.9
  154.2 1.0 copy-start.11
  154.2 1.0 copy-start.13
  154.2 1.0 copy-start.14
  157.1 1.0 copy-start.7
  157.1 1.4 copy-start.6

commit v5 on v4

--- a/solution.py
+++ b/solution.py
@@ -152,7 +152,7 @@
         ],
         axis=1,
     )
-    mine = group_all_to_all(payload)
+    mine = lax.all_to_all(payload, ("z", "y"), 0, 0, tiled=True)
     totals = mine[:, 0, rows, 0]
     ends = mine[:, :, :rows, :].reshape(count, 2, rows * cols)
     ids = jnp.arange(count)
@@ -168,7 +168,7 @@
         "ktj,jkx->tkx", weights, ends, precision=lax.Precision.HIGHEST,
         preferred_element_type=jnp.float32,
     ).reshape(count, 2, rows, cols)
-    back = group_all_to_all(entries)
+    back = lax.all_to_all(entries, ("z", "y"), 0, 0, tiled=True)
     return back[:, 0], back[:, 1]
 
 

time: 228 us -> 214 us (0.939)
  Pallas kernels: 192 us -> 55.5 us
  waiting for transfers between devices: 0 us -> 98.3 us
  starting transfers between devices: 0 us -> 17.9 us
  local copies, waits for them, and re-layouts: 13.7 us -> 17.6 us
    pallas_call x2 -> x0, Pallas kernels: 129 us -> none  [group_all_to_all(): pl.pallas_call(kernel, out_shape=jax.ShapeDtypeStruct(payload.shape, payl...]
    all_to_all x0 -> x2, waiting for transfers between devices: none -> 98.3 us  [the longest x1 55.3 us: exchange(): mine = lax.all_to_all(payload, ('z', 'y'), 0, 0, tiled=True)]
    all_to_all x0 -> x2, starting transfers between devices: none -> 17.9 us  [the longest x1 11.4 us: exchange(): mine = lax.all_to_all(payload, ('z', 'y'), 0, 0, tiled=True)]
    pallas_call x1, Pallas kernels: 63.1 us -> 55.5 us  [weight_grad_sum(): pl.pallas_call(kernel, out_shape=jax.ShapeDtypeStruct((piece, cols), jnp....]
    unnamed x35 -> x25, local copies, waits for them, and re-layouts: 6.29 us -> 4.88 us
  transfers between devices with their start and end apart: 0 -> 2, of which waited for: 0 -> 2; matrix products, arithmetic and copies ran while one was open for 0% -> 3% of each run, Pallas kernels for 0% -> 0%
where the time goes in v5:
time: 214 us; the launch traced here: 210 us
  waiting for transfers between devices  98.3 us (46%)
  Pallas kernels  55.5 us (26%)
  starting transfers between devices  17.9 us (8%)
  local copies, waits for them, and re-layouts  17.6 us (8%)
  matrix products  13.2 us (6%)
  other arithmetic  6.17 us (3%)
    pallas_call x1, Pallas kernels, weight_grad_sum(): pl.pallas_call(kernel, out_shape=jax.ShapeDtypeStruct((piece, cols), jnp....  55.5 us
    all_to_all x1, waiting for transfers between devices, exchange(): mine = lax.all_to_all(payload, ('z', 'y'), 0, 0, tiled=True)  55.3 us
    all_to_all x1, waiting for transfers between devices, exchange(): back = lax.all_to_all(entries, ('z', 'y'), 0, 0, tiled=True)  43 us
    all_to_all x1, starting transfers between devices, exchange(): mine = lax.all_to_all(payload, ('z', 'y'), 0, 0, tiled=True)  11.4 us
    all_to_all x1, starting transfers between devices, exchange(): back = lax.all_to_all(entries, ('z', 'y'), 0, 0, tiled=True)  6.52 us
    unnamed x25, local copies, waits for them, and re-layouts  4.88 us
    dot_general x1, matrix products, exchange(): jnp.einsum('ktj,jkx->tkx', weights, ends, precision=lax.Precision.HIGHEST...  4.72 us
  transfers between devices with their start and end apart: 2, of which 2 were waited for; matrix products, arithmetic and copies ran while one was open for 3% of the time, Pallas kernels for 0%

profile of v5, /device:TPU:32, one launch (start us, length us, event | category | flops | bytes accessed | tf_op | source)
XLA Modules:
  0.0 209.7 jit_solution(8245834634377338408)
XLA Ops:
  0.6 0.0 copy-start
  0.6 1.1 reduce_window_sum.17
  1.8 0.2 slice_reduce_fusion.1
  2.0 0.8 multiply_bitcast_fusion
  2.8 1.3 copy.45
  4.1 0.0 copy-start.4
  4.1 1.5 copy.44
  5.6 0.0 copy-done
  5.6 0.0 copy-start.1
  5.7 1.9 convolution_convert_fusion
  7.5 0.0 copy-done.4
  7.5 0.2 fusion.13
  7.7 0.0 copy-done.1
  7.8 0.3 convolution_add_fusion.1
  8.0 0.3 convolution_add_fusion
  8.3 0.1 broadcast_in_dim.100
  8.4 0.2 fusion.6
  8.6 0.2 pad_maximum_fusion
  8.8 1.6 copy.47
  10.4 11.4 %all-to-all-start = ((f32[32,2,72,128]{3,2,1,0:T(8,128)}), f32[32,2,72,128]{3,2,1,0:T(8,128)}, u32[]{:S(2)}, u32[]{:S(2)}) async-start(f32[32,2,72,128]{3,2,1,0:T(8,128)} %copy.47), calls=%async_computation | async-start | bytes 4718592 | tf_op jit(solution)/shard_map/all_to_all | solution.py:155
  21.8 55.3 %all-to-all-done = f32[32,2,72,128]{3,2,1,0:T(8,128)} async-done(((f32[32,2,72,128]{3,2,1,0:T(8,128)}), f32[32,2,72,128]{3,2,1,0:T(8,128)}, u32[]{:S(2)}, u32[]{:S(2)}) %all-to-all-start) | async-done | bytes 2359328 | tf_op jit(solution)/shard_map/all_to_all | solution.py:155
  77.1 3.2 %slice.31 = f32[32,2,64,128]{3,2,1,0:T(8,128)} slice(f32[32,2,72,128]{3,2,1,0:T(8,128)} %all-to-all-done), slice={[0:32], [0:2], [0:64], [0:128]} | slice | bytes 4194304 | tf_op jit(solution)/shard_map/slice | solution.py:157
  80.3 3.4 %reshape.350 = f32[32,2,8192]{2,1,0:T(2,128)} reshape(f32[32,2,64,128]{3,2,1,0:T(8,128)} %slice.31) | data formatting | bytes 4194304 | tf_op jit(solution)/shard_map/reshape | solution.py:157
  83.7 1.2 slice_reduce_fusion
  85.0 0.3 select_reduce_fusion.1
  85.3 4.7 %fusion = f32[2,8192,32]{1,2,0:T(8,128)S(1)} fusion(f32[32,2,8192]{2,1,0:T(2,128)} %reshape.350, f32[1,32,32]{2,1,0:T(8,128)S(1)} %bitcast_select_fusion, f32[1,32,32]{2,1,0:T(8,128)S(1)} %bitcast_select_fusion.1), kind=kOutput, calls=%fused_computation.1 | convolution fusion | flops 201328640 | bytes 4202496 | tf_op jit(solution)/shard_map/ktj,jkx->tkx/dot_general | solution.py:167
  90.1 0.4 copy.62
  90.4 1.4 copy.49
  91.9 6.5 %all-to-all-start.1 = ((f32[32,2,64,128]{3,2,1,0:T(8,128)}), f32[32,2,64,128]{3,2,1,0:T(8,128)}, u32[]{:S(2)}, u32[]{:S(2)}) async-start(f32[32,2,64,128]{3,2,1,0:T(8,128)} %copy.49), calls=%async_computation.1 | async-start | bytes 4194304 | tf_op jit(solution)/shard_map/all_to_all | solution.py:171
  98.4 0.0 copy-start.8
  98.4 1.6 copy.50
  100.1 0.1 exponential_bitcast_fusion.1
  100.1 0.1 fusion.32
  100.3 0.0 copy-done.8
  100.3 0.0 copy-start.2
  100.3 0.0 copy-start.5
  100.3 2.2 %multiply_reduce_fusion = bf16[128,128]{1,0:T(8,128)(2,1)S(1)} fusion(bf16[128,32,64]{0,2,1:T(8,128)(2,1)} %bitcast.93, bf16[128,32,64]{0,2,1:T(8,128)(2,1)} %bitcast.96, f32[32,128]{1,0:T(8,128)S(1)} %bitcast.108, f32[32,128]{1,0:T(8,128)S(1)} %bitcast.106, pred[128,128]{1,0:T(8,128)(4,1)S(1)} %iota_compare_fusion), kind=kOutput, calls=%fused_computation.3 | convolution fusion | flops 69713920 | bytes 1130496 | tf_op jit(solution)/shard_map/while/body/eval_jaxpr/shp,jhp->hsj/dot_general | solution.py:79
  102.6 0.1 fusion.35
  102.7 0.2 fusion.29
  102.9 0.0 copy-done.2
  102.9 0.0 copy-done.5
  102.9 1.3 fusion.10
  104.2 43.0 %all-to-all-done.1 = f32[32,2,64,128]{3,2,1,0:T(8,128)} async-done(((f32[32,2,64,128]{3,2,1,0:T(8,128)}), f32[32,2,64,128]{3,2,1,0:T(8,128)}, u32[]{:S(2)}, u32[]{:S(2)}) %all-to-all-start.1) | async-done | bytes 2097184 | tf_op jit(solution)/shard_map/all_to_all | solution.py:171
  147.2 0.0 copy-start.7
  147.2 0.0 copy-start.6
  147.2 1.9 multiply_convert_fusion.2
  149.1 0.0 copy-done.7
  149.1 0.3 fusion.8
  149.4 0.0 copy-done.6
  149.4 0.0 copy-start.3
  149.4 0.0 copy-start.9
  149.4 0.3 fusion.9
  149.8 55.5 %shard_map.86 = f32[16,256]{1,0:T(8,128)S(1)} custom-call(bf16[4,2,512,128]{3,2,1,0:T(8,128)(2,1)S(1)} %bitcast.90, bf16[128,256]{1,0:T(8,128)(2,1)S(1)} %pad_maximum_fusion.3.gp_ref), custom_call_target="tpu_custom_call" | custom-call | tf_op jit(solution)/shard_map/pallas_call | solution.py:235
  205.3 1.6 convolution_multiply_fusion
  206.9 0.0 copy-done.3
  206.9 0.0 copy-done.9
  206.9 1.2 fusion.5
  208.1 1.0 copy.56
  209.1 0.6 copy.66
  (6 shorter events, 0.1 us)
Async XLA Ops:
  0.6 5.0 %copy-start = (bf16[4096,256]{1,0:T(8,128)(2,1)S(1)}, bf16[4096,256]{1,0:T(8,128)(2,1)}, u32[]{:S(2)}) copy-start(bf16[4096,256]{1,0:T(8,128)(2,1)} %param.8) | copy-start | bytes 6291460
  4.1 3.4 %copy-start.4 = (bf16[1,128,2048]{1,2,0:T(8,128)(2,1)}, bf16[1,128,2048]{1,2,0:T(8,128)(2,1)S(1)}, u32[]{:S(2)}) copy-start(bf16[1,128,2048]{1,2,0:T(8,128)(2,1)S(1)} %copy.45) | copy-start | bytes 1572868
  5.6 2.1 %copy-start.1 = (bf16[1,128,2048]{1,2,0:T(8,128)(2,1)}, bf16[1,128,2048]{1,2,0:T(8,128)(2,1)S(1)}, u32[]{:S(2)}) copy-start(bf16[1,128,2048]{1,2,0:T(8,128)(2,1)S(1)} %copy.44) | copy-start | bytes 1572868
  10.4 66.7 %all-to-all-start = ((f32[32,2,72,128]{3,2,1,0:T(8,128)}), f32[32,2,72,128]{3,2,1,0:T(8,128)}, u32[]{:S(2)}, u32[]{:S(2)}) async-start(f32[32,2,72,128]{3,2,1,0:T(8,128)} %copy.47), calls=%async_computation | async-start | bytes 4718592 | tf_op jit(solution)/shard_map/all_to_all | solution.py:155
  91.9 55.3 %all-to-all-start.1 = ((f32[32,2,64,128]{3,2,1,0:T(8,128)}), f32[32,2,64,128]{3,2,1,0:T(8,128)}, u32[]{:S(2)}, u32[]{:S(2)}) async-start(f32[32,2,64,128]{3,2,1,0:T(8,128)} %copy.49), calls=%async_computation.1 | async-start | bytes 4194304 | tf_op jit(solution)/shard_map/all_to_all | solution.py:171
  98.4 1.9 copy-start.8
  100.3 2.6 %copy-start.2 = (bf16[1,128,2048]{1,2,0:T(8,128)(2,1)S(1)}, bf16[1,128,2048]{1,2,0:T(8,128)(2,1)}, u32[]{:S(2)}) copy-start(bf16[1,128,2048]{1,2,0:T(8,128)(2,1)} %copy-done.1) | copy-start | bytes 1572868
  100.3 2.6 %copy-start.5 = (bf16[1,128,2048]{1,2,0:T(8,128)(2,1)S(1)}, bf16[1,128,2048]{1,2,0:T(8,128)(2,1)}, u32[]{:S(2)}) copy-start(bf16[1,128,2048]{1,2,0:T(8,128)(2,1)} %copy-done.4) | copy-start | bytes 1572868
  147.2 1.9 copy-start.7
  147.2 2.2 %copy-start.6 = (bf16[128,32,64]{0,2,1:T(8,128)(2,1)S(1)}, bf16[128,32,64]{0,2,1:T(8,128)(2,1)}, u32[]{:S(2)}) copy-start(bf16[128,32,64]{0,2,1:T(8,128)(2,1)} %get-tuple-element.80) | copy-start | bytes 1572868
  149.4 57.5 %copy-start.3 = (bf16[1,128,2048]{1,2,0:T(8,128)(2,1)S(1)}, bf16[1,128,2048]{1,2,0:T(8,128)(2,1)}, u32[]{:S(2)}) copy-start(bf16[1,128,2048]{1,2,0:T(8,128)(2,1)} %copy-done.1) | copy-start | bytes 1572868
  149.4 57.5 %copy-start.9 = (f32[32]{0:T(128)S(1)}, f32[32]{0:T(128)}, u32[]{:S(2)}) copy-start(f32[32]{0:T(128)} %param.12) | copy-start | bytes 388

commit v6 on v5

--- a/solution.py
+++ b/solution.py
@@ -174,63 +174,93 @@
 
 def weight_grad_sum(tokens, grad_proj, scale):
     chips, cores = lax.axis_size("x"), lax.axis_size("core")
-    width = lax.axis_size("y")
-    count = lax.axis_size("z") * width
+    layers, width = lax.axis_size("z"), lax.axis_size("y")
+    count = layers * width
     length, depth = tokens.shape
     cols = grad_proj.shape[1]
+    half = cols // 2
     slab = depth // (chips * cores)
     piece = slab // count
     by_owner = tokens.T.reshape(chips, cores, slab, length)
-
-    def kernel(tok_ref, gp_ref, out_ref, send1, land1, acc1, land2, acc2, land3, sems):
+    mesh_id = pl.DeviceIdType.MESH
+    ring = count - 1
+
+    def kernel(tok_ref, gp_ref, out_ref, send1, land1, acc_a, acc_b, land_a, land_b,
+               sum_a, sum_b, fin_a, fin_b, sems):
         chip, core = lax.axis_index("x"), lax.axis_index("core")
         z, y = lax.axis_index("z"), lax.axis_index("y")
         me = z * width + y
+        spot = chip * layers + z
         other = 1 - core
         gp = gp_ref[...]
         for c in range(chips):
             send1[c] = jnp.dot(tok_ref[c, other], gp, preferred_element_type=jnp.float32)
         first = pltpu.make_async_remote_copy(
             src_ref=send1, dst_ref=land1, send_sem=sems.at[0, 0], recv_sem=sems.at[1, 0],
-            device_id=(chip, other, z, y), device_id_type=pl.DeviceIdType.MESH,
+            device_id=(chip, other, z, y), device_id_type=mesh_id,
         )
         first.start()
+        own = [jnp.dot(tok_ref[c, core], gp, preferred_element_type=jnp.float32) for c in range(chips)]
+        first.wait()
         for c in range(chips):
-            acc1[c] = jnp.dot(tok_ref[c, core], gp, preferred_element_type=jnp.float32)
-        first.wait()
-        acc1[...] = acc1[...] + land1[...]
+            summed = own[c] + land1[c]
+            acc_a[c] = summed[:, :half]
+            blocks = summed[:, half:].reshape(layers, width, piece, half)
+            for w in range(width):
+                acc_b[w, c] = blocks[:, w]
         second = []
         for step in range(1, chips):
             dest = (chip + step) % chips
-            copy = pltpu.make_async_remote_copy(
-                src_ref=acc1.at[dest], dst_ref=land2.at[step - 1], send_sem=sems.at[0, step],
-                recv_sem=sems.at[1, step], device_id=(dest, core, z, y),
-                device_id_type=pl.DeviceIdType.MESH,
-            )
+            second.append(pltpu.make_async_remote_copy(
+                src_ref=acc_a.at[dest], dst_ref=land_a.at[step - 1], send_sem=sems.at[0, step],
+                recv_sem=sems.at[1, step], device_id=(dest, core, z, y), device_id_type=mesh_id,
+            ))
+        for step in range(1, width):
+            dest = (y + step) % width
+            second.append(pltpu.make_async_remote_copy(
+                src_ref=acc_b.at[dest], dst_ref=land_b.at[step - 1], send_sem=sems.at[0, chips + step],
+                recv_sem=sems.at[1, chips + step], device_id=(chip, core, z, dest), device_id_type=mesh_id,
+            ))
+        for copy in second:
             copy.start()
-            second.append(copy)
         for copy in second:
             copy.wait()
-        total = acc1[chip]
+        total = acc_a[chip]
         for step in range(1, chips):
-            total = total + land2[step - 1]
-        acc2[...] = total.reshape(count, piece, cols)
+            total = total + land_a[step - 1]
+        sum_a[...] = total.reshape(count, piece, half)
+        total = acc_b[y]
+        for step in range(1, width):
+            total = total + land_b[step - 1]
+        sum_b[...] = total.reshape(chips * layers, piece, half)
+        base = chips + width
         third = []
         for step in range(1, count):
             dest = (me + step) % count
-            copy = pltpu.make_async_remote_copy(
-                src_ref=acc2.at[dest], dst_ref=land3.at[step - 1], send_sem=sems.at[0, chips + step],
-                recv_sem=sems.at[1, chips + step], device_id=(chip, core, dest // width, dest % width),
-                device_id_type=pl.DeviceIdType.MESH,
-            )
+            third.append(pltpu.make_async_remote_copy(
+                src_ref=sum_a.at[dest], dst_ref=fin_a.at[step - 1], send_sem=sems.at[0, base + step],
+                recv_sem=sems.at[1, base + step], device_id=(chip, core, dest // width, dest % width),
+                device_id_type=mesh_id,
+            ))
+        for step in range(1, chips * layers):
+            dest = (spot + step) % (chips * layers)
+            third.append(pltpu.make_async_remote_copy(
+                src_ref=sum_b.at[dest], dst_ref=fin_b.at[step - 1], send_sem=sems.at[0, base + ring + step],
+                recv_sem=sems.at[1, base + ring + step], device_id=(dest // layers, core, dest % layers, y),
+                device_id_type=mesh_id,
+            ))
+        for copy in third:
             copy.start()
-            third.append(copy)
         for copy in third:
             copy.wait()
-        total = acc2[me]
+        total = sum_a[me]
         for step in range(1, count):
-            total = total + land3[step - 1]
-        out_ref[...] = total * scale
+            total = total + fin_a[step - 1]
+        out_ref[:, :half] = total * scale
+        total = sum_b[spot]
+        for step in range(1, chips * layers):
+            total = total + fin_b[step - 1]
+        out_ref[:, half:] = total * scale
 
     return pl.pallas_call(
         kernel,
@@ -240,11 +270,15 @@
         scratch_shapes=[
             pltpu.VMEM((chips, slab, cols), jnp.float32),
             pltpu.VMEM((chips, slab, cols), jnp.float32),
-            pltpu.VMEM((chips, slab, cols), jnp.float32),
-            pltpu.VMEM((chips - 1, slab, cols), jnp.float32),
-            pltpu.VMEM((count, piece, cols), jnp.float32),
-            pltpu.VMEM((count - 1, piece, cols), jnp.float32),
-            pltpu.SemaphoreType.DMA((2, chips + count)),
+            pltpu.VMEM((chips, slab, half), jnp.float32),
+            pltpu.VMEM((width, chips, layers, piece, half), jnp.float32),
+            pltpu.VMEM((chips - 1, slab, half), jnp.float32),
+            pltpu.VMEM((width - 1, chips, layers, piece, half), jnp.float32),
+            pltpu.VMEM((count, piece, half), jnp.float32),
+            pltpu.VMEM((chips * layers, piece, half), jnp.float32),
+            pltpu.VMEM((count - 1, piece, half), jnp.float32),
+            pltpu.VMEM((chips * layers - 1, piece, half), jnp.float32),
+            pltpu.SemaphoreType.DMA((2, chips + width + count + chips * layers)),
         ],
         compiler_params=pltpu.CompilerParams(has_side_effects=True, vmem_limit_bytes=48 * 1024 * 1024),
     )(by_owner, grad_proj)

time: 214 us -> 203 us (0.949); the launches traced: 210 us -> 201 us
  Pallas kernels: 55.5 us -> 46.8 us
    pallas_call x1, Pallas kernels: 55.5 us -> 46.8 us  [weight_grad_sum(): pl.pallas_call(kernel, out_shape=jax.ShapeDtypeStruct((piece, cols), jnp....]
where the time goes in v6:
time: 203 us; the launch traced here: 201 us
  waiting for transfers between devices  98.3 us (48%)
  Pallas kernels  46.8 us (23%)
  starting transfers between devices  17.9 us (9%)
  local copies, waits for them, and re-layouts  17.6 us (9%)
  matrix products  13.2 us (7%)
  other arithmetic  6.17 us (3%)
    all_to_all x1, waiting for transfers between devices, exchange(): mine = lax.all_to_all(payload, ('z', 'y'), 0, 0, tiled=True)  55.3 us
    pallas_call x1, Pallas kernels, weight_grad_sum(): pl.pallas_call(kernel, out_shape=jax.ShapeDtypeStruct((piece, cols), jnp....  46.8 us
    all_to_all x1, waiting for transfers between devices, exchange(): back = lax.all_to_all(entries, ('z', 'y'), 0, 0, tiled=True)  43 us
    all_to_all x1, starting transfers between devices, exchange(): mine = lax.all_to_all(payload, ('z', 'y'), 0, 0, tiled=True)  11.4 us
    all_to_all x1, starting transfers between devices, exchange(): back = lax.all_to_all(entries, ('z', 'y'), 0, 0, tiled=True)  6.52 us
    unnamed x25, local copies, waits for them, and re-layouts  4.88 us
    dot_general x1, matrix products, exchange(): jnp.einsum('ktj,jkx->tkx', weights, ends, precision=lax.Precision.HIGHEST...  4.72 us
  transfers between devices with their start and end apart: 2, of which 2 were waited for; matrix products, arithmetic and copies ran while one was open for 3% of the time, Pallas kernels for 0%

profile of v6, /device:TPU:32, one launch (start us, length us, event | category | flops | bytes accessed | tf_op | source)
XLA Modules:
  0.0 201.1 jit_solution(5203073602731503592)
XLA Ops:
  0.6 0.0 copy-start
  0.6 1.1 reduce_window_sum.17
  1.8 0.2 slice_reduce_fusion.1
  2.0 0.8 multiply_bitcast_fusion
  2.8 1.3 copy.45
  4.1 0.0 copy-start.4
  4.1 1.5 copy.44
  5.6 0.0 copy-done
  5.6 0.0 copy-start.1
  5.7 1.9 convolution_convert_fusion
  7.5 0.0 copy-done.4
  7.5 0.2 fusion.13
  7.7 0.0 copy-done.1
  7.8 0.3 convolution_add_fusion.1
  8.0 0.3 convolution_add_fusion
  8.3 0.1 broadcast_in_dim.100
  8.4 0.2 fusion.6
  8.6 0.2 pad_maximum_fusion
  8.8 1.6 copy.47
  10.4 11.4 %all-to-all-start = ((f32[32,2,72,128]{3,2,1,0:T(8,128)}), f32[32,2,72,128]{3,2,1,0:T(8,128)}, u32[]{:S(2)}, u32[]{:S(2)}) async-start(f32[32,2,72,128]{3,2,1,0:T(8,128)} %copy.47), calls=%async_computation | async-start | bytes 4718592 | tf_op jit(solution)/shard_map/all_to_all | solution.py:155
  21.8 55.3 %all-to-all-done = f32[32,2,72,128]{3,2,1,0:T(8,128)} async-done(((f32[32,2,72,128]{3,2,1,0:T(8,128)}), f32[32,2,72,128]{3,2,1,0:T(8,128)}, u32[]{:S(2)}, u32[]{:S(2)}) %all-to-all-start) | async-done | bytes 2359328 | tf_op jit(solution)/shard_map/all_to_all | solution.py:155
  77.1 3.2 %slice.31 = f32[32,2,64,128]{3,2,1,0:T(8,128)} slice(f32[32,2,72,128]{3,2,1,0:T(8,128)} %all-to-all-done), slice={[0:32], [0:2], [0:64], [0:128]} | slice | bytes 4194304 | tf_op jit(solution)/shard_map/slice | solution.py:157
  80.3 3.4 %reshape.350 = f32[32,2,8192]{2,1,0:T(2,128)} reshape(f32[32,2,64,128]{3,2,1,0:T(8,128)} %slice.31) | data formatting | bytes 4194304 | tf_op jit(solution)/shard_map/reshape | solution.py:157
  83.7 1.2 slice_reduce_fusion
  85.0 0.3 select_reduce_fusion.1
  85.3 4.7 %fusion = f32[2,8192,32]{1,2,0:T(8,128)S(1)} fusion(f32[32,2,8192]{2,1,0:T(2,128)} %reshape.350, f32[1,32,32]{2,1,0:T(8,128)S(1)} %bitcast_select_fusion, f32[1,32,32]{2,1,0:T(8,128)S(1)} %bitcast_select_fusion.1), kind=kOutput, calls=%fused_computation.1 | convolution fusion | flops 201328640 | bytes 4202496 | tf_op jit(solution)/shard_map/ktj,jkx->tkx/dot_general | solution.py:167
  90.1 0.4 copy.62
  90.4 1.4 copy.49
  91.9 6.5 %all-to-all-start.1 = ((f32[32,2,64,128]{3,2,1,0:T(8,128)}), f32[32,2,64,128]{3,2,1,0:T(8,128)}, u32[]{:S(2)}, u32[]{:S(2)}) async-start(f32[32,2,64,128]{3,2,1,0:T(8,128)} %copy.49), calls=%async_computation.1 | async-start | bytes 4194304 | tf_op jit(solution)/shard_map/all_to_all | solution.py:171
  98.4 0.0 copy-start.8
  98.4 1.6 copy.50
  100.1 0.1 exponential_bitcast_fusion.1
  100.1 0.1 fusion.32
  100.3 0.0 copy-done.8
  100.3 0.0 copy-start.2
  100.3 0.0 copy-start.5
  100.3 2.2 %multiply_reduce_fusion = bf16[128,128]{1,0:T(8,128)(2,1)S(1)} fusion(bf16[128,32,64]{0,2,1:T(8,128)(2,1)} %bitcast.93, bf16[128,32,64]{0,2,1:T(8,128)(2,1)} %bitcast.96, f32[32,128]{1,0:T(8,128)S(1)} %bitcast.108, f32[32,128]{1,0:T(8,128)S(1)} %bitcast.106, pred[128,128]{1,0:T(8,128)(4,1)S(1)} %iota_compare_fusion), kind=kOutput, calls=%fused_computation.3 | convolution fusion | flops 69713920 | bytes 1130496 | tf_op jit(solution)/shard_map/while/body/eval_jaxpr/shp,jhp->hsj/dot_general | solution.py:79
  102.6 0.1 fusion.35
  102.7 0.2 fusion.29
  102.9 0.0 copy-done.2
  102.9 0.0 copy-done.5
  102.9 1.3 fusion.10
  104.2 43.0 %all-to-all-done.1 = f32[32,2,64,128]{3,2,1,0:T(8,128)} async-done(((f32[32,2,64,128]{3,2,1,0:T(8,128)}), f32[32,2,64,128]{3,2,1,0:T(8,128)}, u32[]{:S(2)}, u32[]{:S(2)}) %all-to-all-start.1) | async-done | bytes 2097184 | tf_op jit(solution)/shard_map/all_to_all | solution.py:171
  147.2 0.0 copy-start.7
  147.2 0.0 copy-start.6
  147.2 1.9 multiply_convert_fusion.2
  149.1 0.0 copy-done.7
  149.1 0.3 fusion.8
  149.4 0.0 copy-done.6
  149.4 0.0 copy-start.3
  149.4 0.0 copy-start.9
  149.4 0.3 fusion.9
  149.8 46.8 %shard_map.86 = f32[16,256]{1,0:T(8,128)S(1)} custom-call(bf16[4,2,512,128]{3,2,1,0:T(8,128)(2,1)S(1)} %bitcast.90, bf16[128,256]{1,0:T(8,128)(2,1)S(1)} %pad_maximum_fusion.3.gp_ref), custom_call_target="tpu_custom_call" | custom-call | tf_op jit(solution)/shard_map/pallas_call | solution.py:265
  196.7 1.6 convolution_multiply_fusion
  198.3 0.0 copy-done.3
  198.3 0.0 copy-done.9
  198.3 1.2 fusion.5
  199.4 1.0 copy.56
  200.5 0.6 copy.66
  (6 shorter events, 0.1 us)
Async XLA Ops:
  0.6 5.0 %copy-start = (bf16[4096,256]{1,0:T(8,128)(2,1)S(1)}, bf16[4096,256]{1,0:T(8,128)(2,1)}, u32[]{:S(2)}) copy-start(bf16[4096,256]{1,0:T(8,128)(2,1)} %param.8) | copy-start | bytes 6291460
  4.1 3.4 %copy-start.4 = (bf16[1,128,2048]{1,2,0:T(8,128)(2,1)}, bf16[1,128,2048]{1,2,0:T(8,128)(2,1)S(1)}, u32[]{:S(2)}) copy-start(bf16[1,128,2048]{1,2,0:T(8,128)(2,1)S(1)} %copy.45) | copy-start | bytes 1572868
  5.6 2.1 %copy-start.1 = (bf16[1,128,2048]{1,2,0:T(8,128)(2,1)}, bf16[1,128,2048]{1,2,0:T(8,128)(2,1)S(1)}, u32[]{:S(2)}) copy-start(bf16[1,128,2048]{1,2,0:T(8,128)(2,1)S(1)} %copy.44) | copy-start | bytes 1572868
  10.4 66.7 %all-to-all-start = ((f32[32,2,72,128]{3,2,1,0:T(8,128)}), f32[32,2,72,128]{3,2,1,0:T(8,128)}, u32[]{:S(2)}, u32[]{:S(2)}) async-start(f32[32,2,72,128]{3,2,1,0:T(8,128)} %copy.47), calls=%async_computation | async-start | bytes 4718592 | tf_op jit(solution)/shard_map/all_to_all | solution.py:155
  91.9 55.3 %all-to-all-start.1 = ((f32[32,2,64,128]{3,2,1,0:T(8,128)}), f32[32,2,64,128]{3,2,1,0:T(8,128)}, u32[]{:S(2)}, u32[]{:S(2)}) async-start(f32[32,2,64,128]{3,2,1,0:T(8,128)} %copy.49), calls=%async_computation.1 | async-start | bytes 4194304 | tf_op jit(solution)/shard_map/all_to_all | solution.py:171
  98.4 1.9 copy-start.8
  100.3 2.6 %copy-start.2 = (bf16[1,128,2048]{1,2,0:T(8,128)(2,1)S(1)}, bf16[1,128,2048]{1,2,0:T(8,128)(2,1)}, u32[]{:S(2)}) copy-start(bf16[1,128,2048]{1,2,0:T(8,128)(2,1)} %copy-done.1) | copy-start | bytes 1572868
  100.3 2.6 %copy-start.5 = (bf16[1,128,2048]{1,2,0:T(8,128)(2,1)S(1)}, bf16[1,128,2048]{1,2,0:T(8,128)(2,1)}, u32[]{:S(2)}) copy-start(bf16[1,128,2048]{1,2,0:T(8,128)(2,1)} %copy-done.4) | copy-start | bytes 1572868
  147.2 1.9 copy-start.7
  147.2 2.2 %copy-start.6 = (bf16[128,32,64]{0,2,1:T(8,128)(2,1)S(1)}, bf16[128,32,64]{0,2,1:T(8,128)(2,1)}, u32[]{:S(2)}) copy-start(bf16[128,32,64]{0,2,1:T(8,128)(2,1)} %get-tuple-element.80) | copy-start | bytes 1572868
  149.4 48.8 %copy-start.3 = (bf16[1,128,2048]{1,2,0:T(8,128)(2,1)S(1)}, bf16[1,128,2048]{1,2,0:T(8,128)(2,1)}, u32[]{:S(2)}) copy-start(bf16[1,128,2048]{1,2,0:T(8,128)(2,1)} %copy-done.1) | copy-start | bytes 1572868
  149.4 48.8 %copy-start.9 = (f32[32]{0:T(128)S(1)}, f32[32]{0:T(128)}, u32[]{:S(2)}) copy-start(f32[32]{0:T(128)} %param.12) | copy-start | bytes 388

commit v7 on v6

--- a/solution.py
+++ b/solution.py
@@ -141,35 +141,32 @@
     )(payload)
 
 
+def chain_kernel(ends_ref, out_ref):
+    count, _, _ = ends_ref.shape
+    rows = out_ref.shape[1] // 2
+    carry = jnp.zeros((rows, out_ref.shape[2]), jnp.float32)
+    for j in range(count):
+        out_ref[j, :rows] = carry
+        carry = jnp.exp(ends_ref[j, 2 * rows : 2 * rows + 1]) * carry + ends_ref[j, :rows]
+    carry = jnp.zeros_like(carry)
+    for j in reversed(range(count)):
+        out_ref[j, rows:] = carry
+        carry = jnp.exp(ends_ref[j, 2 * rows : 2 * rows + 1]) * carry + ends_ref[j, rows : 2 * rows]
+
+
 def exchange(own_state, own_grad, device_total):
-    count = lax.axis_size("z") * lax.axis_size("y")
     heads, rows, cols = own_state.shape
     marks = jnp.broadcast_to(device_total[:, None, None], (heads, 8, cols))
-    payload = jnp.stack(
-        [
-            jnp.concatenate([own_state, marks], axis=1),
-            jnp.concatenate([own_grad, marks], axis=1),
-        ],
-        axis=1,
-    )
+    payload = jnp.concatenate([own_state, own_grad, marks], axis=1)
     mine = lax.all_to_all(payload, ("z", "y"), 0, 0, tiled=True)
-    totals = mine[:, 0, rows, 0]
-    ends = mine[:, :, :rows, :].reshape(count, 2, rows * cols)
-    ids = jnp.arange(count)
-    target, source, between = ids[:, None, None], ids[None, :, None], ids[None, None, :]
-    fwd_span = (source < between) & (between < target)
-    bwd_span = (target < between) & (between < source)
-    fwd_log = jnp.sum(jnp.where(fwd_span, totals[None, None, :], 0.0), axis=2)
-    bwd_log = jnp.sum(jnp.where(bwd_span, totals[None, None, :], 0.0), axis=2)
-    fwd_w = jnp.where(ids[None, :] < ids[:, None], jnp.exp(fwd_log), 0.0)
-    bwd_w = jnp.where(ids[None, :] > ids[:, None], jnp.exp(bwd_log), 0.0)
-    weights = jnp.stack([fwd_w, bwd_w])
-    entries = jnp.einsum(
-        "ktj,jkx->tkx", weights, ends, precision=lax.Precision.HIGHEST,
-        preferred_element_type=jnp.float32,
-    ).reshape(count, 2, rows, cols)
+    entries = pl.pallas_call(
+        chain_kernel,
+        out_shape=jax.ShapeDtypeStruct((heads, 2 * rows, cols), jnp.float32),
+        in_specs=[pl.BlockSpec(memory_space=pltpu.VMEM)],
+        out_specs=pl.BlockSpec(memory_space=pltpu.VMEM),
+    )(mine)
     back = lax.all_to_all(entries, ("z", "y"), 0, 0, tiled=True)
-    return back[:, 0], back[:, 1]
+    return back[:, :rows], back[:, rows:]
 
 
 def weight_grad_sum(tokens, grad_proj, scale):

time: 203 us -> 188 us (0.926)
  blocking collectives: 0 us -> 65.7 us
  waiting for transfers between devices: 98.3 us -> 43.8 us
  starting transfers between devices: 17.9 us -> 5.56 us
  local copies, waits for them, and re-layouts: 17.6 us -> 6.35 us
  other arithmetic: 6.17 us -> 2.45 us
  Pallas kernels: 46.8 us -> 49.9 us
    all_to_all x0 -> x1, blocking collectives: none -> 65.7 us  [exchange(): mine = lax.all_to_all(payload, ('z', 'y'), 0, 0, tiled=True)]
    all_to_all x1 -> x0, waiting for transfers between devices: 55.3 us -> none  [exchange(): mine = lax.all_to_all(payload, ('z', 'y'), 0, 0, tiled=True)]
    all_to_all x1 -> x0, starting transfers between devices: 11.4 us -> none  [exchange(): mine = lax.all_to_all(payload, ('z', 'y'), 0, 0, tiled=True)]
    reshape x2 -> x0, local copies, waits for them, and re-layouts: 4.88 us -> none  [the longest x1 3.43 us: exchange(): ends = mine[:, :, :rows, :].reshape(count, 2, rows * cols)]
    dot_general x1 -> x0, matrix products: 4.72 us -> none  [exchange(): jnp.einsum('ktj,jkx->tkx', weights, ends, precision=lax.Precision.HIGHEST...]
    slice x2 -> x0, local copies, waits for them, and re-layouts: 4.43 us -> none  [the longest x1 3.2 us: exchange(): ends = mine[:, :, :rows, :].reshape(count, 2, rows * cols)]
    pallas_call x0 -> x1, Pallas kernels: none -> 3.12 us  [exchange(): pl.pallas_call(chain_kernel, out_shape=jax.ShapeDtypeStruct((heads, 2 * r...]
    unnamed x25 -> x16, local copies, waits for them, and re-layouts: 4.88 us -> 4.46 us
  transfers between devices with their start and end apart: 2 -> 1, of which waited for: 2 -> 1; matrix products, arithmetic and copies ran while one was open for 3% -> 2% of each run, Pallas kernels for 0% -> 0%
where the time goes in v7:
time: 188 us; the launch traced here: 186 us
  blocking collectives  65.7 us (35%)
  Pallas kernels  49.9 us (27%)
  waiting for transfers between devices  43.8 us (23%)
  matrix products  11.4 us (6%)
  local copies, waits for them, and re-layouts  6.35 us (3%)
  starting transfers between devices  5.56 us (3%)
  other arithmetic  2.45 us (1%)
    all_to_all x1, blocking collectives, exchange(): mine = lax.all_to_all(payload, ('z', 'y'), 0, 0, tiled=True)  65.7 us
    pallas_call x1, Pallas kernels, weight_grad_sum(): pl.pallas_call(kernel, out_shape=jax.ShapeDtypeStruct((piece, cols), jnp....  46.8 us
    all_to_all x1, waiting for transfers between devices, exchange(): back = lax.all_to_all(entries, ('z', 'y'), 0, 0, tiled=True)  43.8 us
    all_to_all x1, starting transfers between devices, exchange(): back = lax.all_to_all(entries, ('z', 'y'), 0, 0, tiled=True)  5.56 us
    unnamed x16, local copies, waits for them, and re-layouts  4.46 us
  transfers between devices with their start and end apart: 1, of which 1 were waited for; matrix products, arithmetic and copies ran while one was open for 2% of the time, Pallas kernels for 0%

profile of v7, /device:TPU:32, one launch (start us, length us, event | category | flops | bytes accessed | tf_op | source)
XLA Modules:
  0.0 186.2 jit_solution(4986941338464358677)
XLA Ops:
  0.6 0.0 copy-start
  0.6 1.1 reduce_window_sum.17
  1.8 0.2 slice_reduce_fusion
  2.0 0.8 multiply_bitcast_fusion
  2.8 1.3 copy.22
  4.1 0.0 copy-start.1
  4.1 1.5 copy.23
  5.6 0.0 copy-done
  5.6 0.0 copy-start.3
  5.7 1.9 convolution_convert_fusion
  7.5 0.0 copy-done.1
  7.5 0.2 fusion.9
  7.7 0.0 copy-done.3
  7.8 0.3 convolution_add_fusion
  8.0 0.3 convolution_add_fusion.1
  8.3 0.1 broadcast_in_dim.72
  8.4 0.2 pad_maximum_fusion
  8.6 65.7 %all_to_all.10.ends_ref = f32[32,136,128]{2,1,0:T(8,128)} all-to-all(f32[32,136,128]{2,1,0:T(8,128)S(1)} %pad_maximum_fusion), channel_id=1, replica_groups=mesh['x'=4,'core'=2,'z'=8,'y'=4] {'z','y'}, dimensions={0} | all-to-all | bytes 4456448 | tf_op jit(solution)/shard_map/all_to_all | solution.py:161
  74.3 3.1 %shard_map.86 = f32[32,128,128]{2,1,0:T(8,128)} custom-call(f32[32,136,128]{2,1,0:T(8,128)} %all_to_all.10.ends_ref), custom_call_target="tpu_custom_call" | custom-call | tf_op jit(solution)/shard_map/pallas_call | solution.py:162
  77.4 5.6 %all-to-all-start.1 = ((f32[32,128,128]{2,1,0:T(8,128)}), f32[32,128,128]{2,1,0:T(8,128)}, u32[]{:S(2)}, u32[]{:S(2)}) async-start(f32[32,128,128]{2,1,0:T(8,128)} %shard_map.86), calls=%async_computation.1 | async-start | bytes 4194304 | tf_op jit(solution)/shard_map/all_to_all | solution.py:168
  83.0 0.0 copy-start.4
  83.0 1.6 copy.25
  84.7 0.1 exponential_bitcast_fusion.1
  84.8 0.1 fusion.27
  84.9 0.0 copy-done.4
  84.9 2.2 %multiply_reduce_fusion = bf16[128,128]{1,0:T(8,128)(2,1)S(1)} fusion(bf16[128,32,64]{0,2,1:T(8,128)(2,1)} %bitcast.65, bf16[128,32,64]{0,2,1:T(8,128)(2,1)} %bitcast.68, f32[32,128]{1,0:T(8,128)S(1)} %bitcast.76, f32[32,128]{1,0:T(8,128)S(1)} %bitcast.74, pred[128,128]{1,0:T(8,128)(4,1)S(1)} %iota_compare_fusion), kind=kOutput, calls=%fused_computation.1 | convolution fusion | flops 69713920 | bytes 1130496 | tf_op jit(solution)/shard_map/while/body/eval_jaxpr/shp,jhp->hsj/dot_general | solution.py:79
  87.1 43.8 %all-to-all-done.1 = f32[32,128,128]{2,1,0:T(8,128)} async-done(((f32[32,128,128]{2,1,0:T(8,128)}), f32[32,128,128]{2,1,0:T(8,128)}, u32[]{:S(2)}, u32[]{:S(2)}) %all-to-all-start.1) | async-done | bytes 2097184 | tf_op jit(solution)/shard_map/all_to_all | solution.py:168
  130.9 1.8 convolution_bitcast_fusion.2
  132.7 0.2 fusion.4
  132.9 1.8 convolution_bitcast_fusion.1
  134.8 0.0 copy-start.2
  134.8 0.0 copy-start.5
  134.8 0.1 fusion.5
  134.9 46.8 %shard_map.87 = f32[16,256]{1,0:T(8,128)S(1)} custom-call(bf16[4,2,512,128]{3,2,1,0:T(8,128)(2,1)S(1)} %bitcast.64, bf16[128,256]{1,0:T(8,128)(2,1)S(1)} %pad_maximum_fusion.1.gp_ref), custom_call_target="tpu_custom_call" | custom-call | tf_op jit(solution)/shard_map/pallas_call | solution.py:262
  181.8 1.6 convolution_multiply_fusion
  183.4 0.0 copy-done.2
  183.4 0.0 copy-done.5
  183.4 1.2 fusion.3
  184.5 1.0 copy.31
  185.5 0.6 copy.39
  (3 shorter events, 0.0 us)
Async XLA Ops:
  0.6 5.0 %copy-start = (bf16[4096,256]{1,0:T(8,128)(2,1)S(1)}, bf16[4096,256]{1,0:T(8,128)(2,1)}, u32[]{:S(2)}) copy-start(bf16[4096,256]{1,0:T(8,128)(2,1)} %param.8) | copy-start | bytes 6291460
  4.1 3.4 %copy-start.1 = (bf16[1,128,2048]{1,2,0:T(8,128)(2,1)}, bf16[1,128,2048]{1,2,0:T(8,128)(2,1)S(1)}, u32[]{:S(2)}) copy-start(bf16[1,128,2048]{1,2,0:T(8,128)(2,1)S(1)} %copy.22) | copy-start | bytes 1572868
  5.6 2.1 %copy-start.3 = (bf16[1,128,2048]{1,2,0:T(8,128)(2,1)}, bf16[1,128,2048]{1,2,0:T(8,128)(2,1)S(1)}, u32[]{:S(2)}) copy-start(bf16[1,128,2048]{1,2,0:T(8,128)(2,1)S(1)} %copy.23) | copy-start | bytes 1572868
  77.4 53.5 %all-to-all-start.1 = ((f32[32,128,128]{2,1,0:T(8,128)}), f32[32,128,128]{2,1,0:T(8,128)}, u32[]{:S(2)}, u32[]{:S(2)}) async-start(f32[32,128,128]{2,1,0:T(8,128)} %shard_map.86), calls=%async_computation.1 | async-start | bytes 4194304 | tf_op jit(solution)/shard_map/all_to_all | solution.py:168
  83.0 1.9 %copy-start.4 = (f32[1,32,128]{2,1,0:T(8,128)S(1)}, f32[1,32,128]{2,1,0:T(8,128)}, u32[]{:S(2)}) copy-start(f32[1,32,128]{2,1,0:T(8,128)} %param.10) | copy-start | bytes 49156
  134.8 48.6 %copy-start.2 = (bf16[1,128,2048]{1,2,0:T(8,128)(2,1)S(1)}, bf16[1,128,2048]{1,2,0:T(8,128)(2,1)}, u32[]{:S(2)}) copy-start(bf16[1,128,2048]{1,2,0:T(8,128)(2,1)} %copy-done.1) | copy-start | bytes 1572868
  134.8 48.6 %copy-start.5 = (f32[32]{0:T(128)S(1)}, f32[32]{0:T(128)}, u32[]{:S(2)}) copy-start(f32[32]{0:T(128)} %param.12) | copy-start | bytes 388

commit v8 on v7

--- a/solution.py
+++ b/solution.py
@@ -141,31 +141,133 @@
     )(payload)
 
 
-def chain_kernel(ends_ref, out_ref):
-    count, _, _ = ends_ref.shape
-    rows = out_ref.shape[1] // 2
-    carry = jnp.zeros((rows, out_ref.shape[2]), jnp.float32)
-    for j in range(count):
-        out_ref[j, :rows] = carry
-        carry = jnp.exp(ends_ref[j, 2 * rows : 2 * rows + 1]) * carry + ends_ref[j, :rows]
-    carry = jnp.zeros_like(carry)
-    for j in reversed(range(count)):
-        out_ref[j, rows:] = carry
-        carry = jnp.exp(ends_ref[j, 2 * rows : 2 * rows + 1]) * carry + ends_ref[j, rows : 2 * rows]
+def tiered_exchange(payload):
+    width, layers = lax.axis_size("y"), lax.axis_size("z")
+    heads, span, cols = payload.shape
+    rows = (span - 8) // 2
+    group = heads // width
+    mesh_id = pl.DeviceIdType.MESH
+
+    def kernel(pay, out_ref, land1, agg, land2, res, land3, out4, land4, sems, local):
+        chip, core = lax.axis_index("x"), lax.axis_index("core")
+        z, y = lax.axis_index("z"), lax.axis_index("y")
+
+        def run(copies):
+            for copy in copies:
+                copy.start()
+            for copy in copies:
+                copy.wait()
+
+        mine = pltpu.make_async_copy(pay.at[pl.ds(y * group, group)], land1.at[y], local.at[0])
+        mine.start()
+        first = []
+        for step in range(1, width):
+            dest = (y + step) % width
+            first.append(pltpu.make_async_remote_copy(
+                src_ref=pay.at[pl.ds(dest * group, group)], dst_ref=land1.at[y],
+                send_sem=sems.at[0, step - 1], recv_sem=sems.at[1, step - 1],
+                device_id=(chip, core, z, dest), device_id_type=mesh_id,
+            ))
+        run(first)
+        mine.wait()
+        for k in range(group):
+            fwd = jnp.zeros((rows, cols), jnp.float32)
+            bwd = jnp.zeros((rows, cols), jnp.float32)
+            total = jnp.zeros((1, cols), jnp.float32)
+            for w in range(width):
+                mark = land1[w, k, 2 * rows : 2 * rows + 1]
+                fwd = jnp.exp(mark) * fwd + land1[w, k, :rows]
+                total = total + mark
+            for w in reversed(range(width)):
+                mark = land1[w, k, 2 * rows : 2 * rows + 1]
+                bwd = jnp.exp(mark) * bwd + land1[w, k, rows : 2 * rows]
+            agg[k, :rows] = fwd
+            agg[k, rows : 2 * rows] = bwd
+            agg[k, 2 * rows :] = jnp.broadcast_to(total, (8, cols))
+        mine = pltpu.make_async_copy(agg.at[z], land2.at[z], local.at[1])
+        mine.start()
+        base = width - 1
+        second = []
+        for step in range(1, layers):
+            dest = (z + step) % layers
+            second.append(pltpu.make_async_remote_copy(
+                src_ref=agg.at[dest], dst_ref=land2.at[z],
+                send_sem=sems.at[0, base + step - 1], recv_sem=sems.at[1, base + step - 1],
+                device_id=(chip, core, dest, y), device_id_type=mesh_id,
+            ))
+        run(second)
+        mine.wait()
+        carry = jnp.zeros((rows, cols), jnp.float32)
+        for r in range(layers):
+            res[r, :rows] = carry
+            carry = jnp.exp(land2[r, 2 * rows : 2 * rows + 1]) * carry + land2[r, :rows]
+        carry = jnp.zeros((rows, cols), jnp.float32)
+        for r in reversed(range(layers)):
+            res[r, rows:] = carry
+            carry = jnp.exp(land2[r, 2 * rows : 2 * rows + 1]) * carry + land2[r, rows : 2 * rows]
+        mine = pltpu.make_async_copy(res.at[z], land3.at[z], local.at[2])
+        mine.start()
+        base = width - 1 + layers - 1
+        third = []
+        for step in range(1, layers):
+            dest = (z + step) % layers
+            third.append(pltpu.make_async_remote_copy(
+                src_ref=res.at[dest], dst_ref=land3.at[z],
+                send_sem=sems.at[0, base + step - 1], recv_sem=sems.at[1, base + step - 1],
+                device_id=(chip, core, dest, y), device_id_type=mesh_id,
+            ))
+        run(third)
+        mine.wait()
+        for k in range(group):
+            carry = land3[k, :rows]
+            for w in range(width):
+                out4[w, k, :rows] = carry
+                carry = jnp.exp(land1[w, k, 2 * rows : 2 * rows + 1]) * carry + land1[w, k, :rows]
+            carry = land3[k, rows:]
+            for w in reversed(range(width)):
+                out4[w, k, rows:] = carry
+                carry = jnp.exp(land1[w, k, 2 * rows : 2 * rows + 1]) * carry + land1[w, k, rows : 2 * rows]
+        mine = pltpu.make_async_copy(out4.at[y], land4.at[y], local.at[3])
+        mine.start()
+        base = width - 1 + 2 * (layers - 1)
+        fourth = []
+        for step in range(1, width):
+            dest = (y + step) % width
+            fourth.append(pltpu.make_async_remote_copy(
+                src_ref=out4.at[dest], dst_ref=land4.at[y],
+                send_sem=sems.at[0, base + step - 1], recv_sem=sems.at[1, base + step - 1],
+                device_id=(chip, core, z, dest), device_id_type=mesh_id,
+            ))
+        run(fourth)
+        mine.wait()
+        out_ref[...] = land4[...].reshape(heads, 2 * rows, cols)
+
+    links = 2 * (width - 1) + 2 * (layers - 1)
+    return pl.pallas_call(
+        kernel,
+        out_shape=jax.ShapeDtypeStruct((heads, 2 * rows, cols), jnp.float32),
+        in_specs=[pl.BlockSpec(memory_space=pltpu.VMEM)],
+        out_specs=pl.BlockSpec(memory_space=pltpu.VMEM),
+        scratch_shapes=[
+            pltpu.VMEM((width, group, span, cols), jnp.float32),
+            pltpu.VMEM((group, span, cols), jnp.float32),
+            pltpu.VMEM((layers, span, cols), jnp.float32),
+            pltpu.VMEM((layers, 2 * rows, cols), jnp.float32),
+            pltpu.VMEM((layers, 2 * rows, cols), jnp.float32),
+            pltpu.VMEM((width, group, 2 * rows, cols), jnp.float32),
+            pltpu.VMEM((width, group, 2 * rows, cols), jnp.float32),
+            pltpu.SemaphoreType.DMA((2, links)),
+            pltpu.SemaphoreType.DMA((4,)),
+        ],
+        compiler_params=pltpu.CompilerParams(has_side_effects=True, vmem_limit_bytes=48 * 1024 * 1024),
+    )(payload)
 
 
 def exchange(own_state, own_grad, device_total):
     heads, rows, cols = own_state.shape
     marks = jnp.broadcast_to(device_total[:, None, None], (heads, 8, cols))
     payload = jnp.concatenate([own_state, own_grad, marks], axis=1)
-    mine = lax.all_to_all(payload, ("z", "y"), 0, 0, tiled=True)
-    entries = pl.pallas_call(
-        chain_kernel,
-        out_shape=jax.ShapeDtypeStruct((heads, 2 * rows, cols), jnp.float32),
-        in_specs=[pl.BlockSpec(memory_space=pltpu.VMEM)],
-        out_specs=pl.BlockSpec(memory_space=pltpu.VMEM),
-    )(mine)
-    back = lax.all_to_all(entries, ("z", "y"), 0, 0, tiled=True)
+    back = tiered_exchange(payload)
     return back[:, :rows], back[:, rows:]
 
 

time: 188 us -> 162 us (0.86)
  Pallas kernels: 49.9 us -> 144 us
  blocking collectives: 65.7 us -> 0 us
  waiting for transfers between devices: 43.8 us -> 0 us
  starting transfers between devices: 5.56 us -> 0 us
  matrix products: 11.4 us -> 6.18 us
    pallas_call x1, Pallas kernels: 3.12 us -> 94.3 us  [tiered_exchange(): pl.pallas_call(kernel, out_shape=jax.ShapeDtypeStruct((heads, 2 * rows, c...]
    all_to_all x1 -> x0, blocking collectives: 65.7 us -> none  [exchange(): mine = lax.all_to_all(payload, ('z', 'y'), 0, 0, tiled=True)]
    all_to_all x1 -> x0, waiting for transfers between devices: 43.8 us -> none  [exchange(): back = lax.all_to_all(entries, ('z', 'y'), 0, 0, tiled=True)]
    all_to_all x1 -> x0, starting transfers between devices: 5.56 us -> none  [exchange(): back = lax.all_to_all(entries, ('z', 'y'), 0, 0, tiled=True)]
    pallas_call x1, Pallas kernels: 46.8 us -> 49.5 us  [weight_grad_sum(): pl.pallas_call(kernel, out_shape=jax.ShapeDtypeStruct((piece, cols), jnp....]
    unnamed x16 -> x18, local copies, waits for them, and re-layouts: 4.46 us -> 5.47 us
  transfers between devices with their start and end apart: 1 -> 0, of which waited for: 1 -> 0; matrix products, arithmetic and copies ran while one was open for 2% -> 0% of each run, Pallas kernels for 0% -> 0%
where the time goes in v8:
time: 162 us; the launch traced here: 161 us
  Pallas kernels  144 us (89%)
  local copies, waits for them, and re-layouts  7.35 us (5%)
  matrix products  6.18 us (4%)
  other arithmetic  2.44 us (2%)
    pallas_call x1, Pallas kernels, tiered_exchange(): pl.pallas_call(kernel, out_shape=jax.ShapeDtypeStruct((heads, 2 * rows, c...  94.3 us
    pallas_call x1, Pallas kernels, weight_grad_sum(): pl.pallas_call(kernel, out_shape=jax.ShapeDtypeStruct((piece, cols), jnp....  49.5 us
    unnamed x18, local copies, waits for them, and re-layouts  5.47 us

profile of v8, /device:TPU:32, one launch (start us, length us, event | category | flops | bytes accessed | tf_op | source)
XLA Modules:
  0.0 160.6 jit_solution(9796146703190971849)
XLA Ops:
  0.6 0.0 copy-start
  0.6 1.1 reduce_window_sum.17
  1.8 0.2 slice_reduce_fusion
  2.0 0.8 multiply_bitcast_fusion
  2.8 1.3 copy.22
  4.1 0.0 copy-start.2
  4.1 1.5 copy.23
  5.6 0.0 copy-start.4
  5.6 0.2 fusion.7
  5.9 0.0 copy-done
  5.9 1.0 copy-done.4
  6.8 0.4 convolution_convert_fusion
  7.3 0.3 convolution_add_fusion
  7.6 0.3 convolution_add_fusion.1
  7.9 0.1 broadcast_in_dim.72
  8.0 0.2 pad_maximum_fusion.pay
  8.1 0.0 copy-start.5
  8.2 94.3 %shard_map.86 = f32[32,128,128]{2,1,0:T(8,128)S(1)} custom-call(f32[32,136,128]{2,1,0:T(8,128)S(1)} %pad_maximum_fusion.pay), custom_call_target="tpu_custom_call" | custom-call | tf_op jit(solution)/shard_map/pallas_call | solution.py:246
  102.4 0.0 copy-start.1
  102.4 0.4 convolution_bitcast_fusion.2
  102.9 0.0 copy-done.5
  102.9 1.1 multiply_reduce_fusion
  104.0 0.2 fusion.4
  104.2 0.0 copy-done.2
  104.2 0.0 copy-done.1
  104.3 0.4 convolution_bitcast_fusion.1
  104.7 0.1 fusion.5
  104.9 1.6 %copy.25 = bf16[4096,128]{1,0:T(8,128)(2,1)S(1)} copy(bf16[4096,128]{0,1:T(8,128)(2,1)} %bitcast.70) | data formatting | bytes 2097152 | tf_op jit(solution)/shard_map/transpose | solution.py:283
  106.5 0.0 copy-start.3
  106.5 0.0 copy-start.6
  106.5 49.5 %shard_map.87 = f32[16,256]{1,0:T(8,128)S(1)} custom-call(bf16[4,2,512,128]{3,2,1,0:T(8,128)(2,1)S(1)} %bitcast.64, bf16[128,256]{1,0:T(8,128)(2,1)S(1)} %pad_maximum_fusion.1.gp_ref), custom_call_target="tpu_custom_call" | custom-call | tf_op jit(solution)/shard_map/pallas_call | solution.py:364
  156.0 0.1 exponential_bitcast_fusion.1
  156.1 1.6 convolution_multiply_fusion
  157.7 0.1 fusion.24
  157.8 0.0 copy-done.3
  157.8 0.0 copy-done.6
  157.9 1.2 fusion.3
  159.0 1.0 copy.31
  160.0 0.6 copy.39
  (3 shorter events, 0.0 us)
Async XLA Ops:
  0.6 5.2 %copy-start = (bf16[4096,256]{1,0:T(8,128)(2,1)S(1)}, bf16[4096,256]{1,0:T(8,128)(2,1)}, u32[]{:S(2)}) copy-start(bf16[4096,256]{1,0:T(8,128)(2,1)} %param.8) | copy-start | bytes 6291460
  4.1 100.1 %copy-start.2 = (bf16[1,128,2048]{1,2,0:T(8,128)(2,1)}, bf16[1,128,2048]{1,2,0:T(8,128)(2,1)S(1)}, u32[]{:S(2)}) copy-start(bf16[1,128,2048]{1,2,0:T(8,128)(2,1)S(1)} %copy.22) | copy-start | bytes 1572868
  5.6 1.2 copy-start.4
  8.1 94.8 %copy-start.5 = (f32[1,32,128]{2,1,0:T(8,128)S(1)}, f32[1,32,128]{2,1,0:T(8,128)}, u32[]{:S(2)}) copy-start(f32[1,32,128]{2,1,0:T(8,128)} %param.10) | copy-start | bytes 49156
  102.4 1.8 %copy-start.1 = (f32[32,128,128]{2,1,0:T(8,128)}, f32[32,128,128]{2,1,0:T(8,128)S(1)}, u32[]{:S(2)}) copy-start(f32[32,128,128]{2,1,0:T(8,128)S(1)} %shard_map.86) | copy-start | bytes 6291460
  106.5 51.3 %copy-start.3 = (bf16[1,128,2048]{1,2,0:T(8,128)(2,1)S(1)}, bf16[1,128,2048]{1,2,0:T(8,128)(2,1)}, u32[]{:S(2)}) copy-start(bf16[1,128,2048]{1,2,0:T(8,128)(2,1)} %copy-done.2) | copy-start | bytes 1572868
  106.5 51.4 %copy-start.6 = (f32[32]{0:T(128)S(1)}, f32[32]{0:T(128)}, u32[]{:S(2)}) copy-start(f32[32]{0:T(128)} %param.12) | copy-start | bytes 388

commit v9 on v8

--- a/solution.py
+++ b/solution.py
@@ -151,6 +151,12 @@
     def kernel(pay, out_ref, land1, agg, land2, res, land3, out4, land4, sems, local):
         chip, core = lax.axis_index("x"), lax.axis_index("core")
         z, y = lax.axis_index("z"), lax.axis_index("y")
+        barrier = pltpu.get_barrier_semaphore()
+        for step in range(1, width):
+            pl.semaphore_signal(barrier, inc=1, device_id=(chip, core, z, (y + step) % width), device_id_type=mesh_id)
+        for step in range(1, layers):
+            pl.semaphore_signal(barrier, inc=1, device_id=(chip, core, (z + step) % layers, y), device_id_type=mesh_id)
+        pl.semaphore_wait(barrier, width - 1 + layers - 1)
 
         def run(copies):
             for copy in copies:
@@ -259,7 +265,9 @@
             pltpu.SemaphoreType.DMA((2, links)),
             pltpu.SemaphoreType.DMA((4,)),
         ],
-        compiler_params=pltpu.CompilerParams(has_side_effects=True, vmem_limit_bytes=48 * 1024 * 1024),
+        compiler_params=pltpu.CompilerParams(
+            collective_id=0, has_side_effects=True, vmem_limit_bytes=48 * 1024 * 1024
+        ),
     )(payload)
 
 
@@ -291,6 +299,15 @@
         me = z * width + y
         spot = chip * layers + z
         other = 1 - core
+        barrier = pltpu.get_barrier_semaphore()
+        pl.semaphore_signal(barrier, inc=1, device_id=(chip, other, z, y), device_id_type=mesh_id)
+        for step in range(1, count):
+            dest = (me + step) % count
+            pl.semaphore_signal(barrier, inc=1, device_id=(chip, core, dest // width, dest % width), device_id_type=mesh_id)
+        for step in range(1, chips * layers):
+            dest = (spot + step) % (chips * layers)
+            pl.semaphore_signal(barrier, inc=1, device_id=(dest // layers, core, dest % layers, y), device_id_type=mesh_id)
+        pl.semaphore_wait(barrier, count + chips * layers - 1)
         gp = gp_ref[...]
         for c in range(chips):
             send1[c] = jnp.dot(tok_ref[c, other], gp, preferred_element_type=jnp.float32)
@@ -379,7 +396,9 @@
             pltpu.VMEM((chips * layers - 1, piece, half), jnp.float32),
             pltpu.SemaphoreType.DMA((2, chips + width + count + chips * layers)),
         ],
-        compiler_params=pltpu.CompilerParams(has_side_effects=True, vmem_limit_bytes=48 * 1024 * 1024),
+        compiler_params=pltpu.CompilerParams(
+            collective_id=1, has_side_effects=True, vmem_limit_bytes=48 * 1024 * 1024
+        ),
     )(by_owner, grad_proj)
 
 

time: 162 us -> 145 us (0.90)
  Pallas kernels: 144 us -> 128 us
    pallas_call x1, Pallas kernels: 94.3 us -> 85.2 us  [tiered_exchange(): pl.pallas_call(kernel, out_shape=jax.ShapeDtypeStruct((heads, 2 * rows, c...]
    pallas_call x1, Pallas kernels: 49.5 us -> 42.7 us  [weight_grad_sum(): pl.pallas_call(kernel, out_shape=jax.ShapeDtypeStruct((piece, cols), jnp....]
where the time goes in v9:
time: 145 us
  Pallas kernels  128 us (88%)
  local copies, waits for them, and re-layouts  7.35 us (5%)
  matrix products  6.18 us (4%)
  other arithmetic  2.44 us (2%)
    pallas_call x1, Pallas kernels, tiered_exchange(): pl.pallas_call(kernel, out_shape=jax.ShapeDtypeStruct((heads, 2 * rows, c...  85.2 us
    pallas_call x1, Pallas kernels, weight_grad_sum(): pl.pallas_call(kernel, out_shape=jax.ShapeDtypeStruct((piece, cols), jnp....  42.7 us
    unnamed x18, local copies, waits for them, and re-layouts  5.47 us

profile of v9, /device:TPU:32, one launch (start us, length us, event | category | flops | bytes accessed | tf_op | source)
XLA Modules:
  0.0 144.8 jit_solution(782286885063919613)
XLA Ops:
  0.6 0.0 copy-start
  0.6 1.1 reduce_window_sum.17
  1.8 0.2 slice_reduce_fusion
  2.0 0.8 multiply_bitcast_fusion
  2.8 1.3 copy.22
  4.1 0.0 copy-start.2
  4.1 1.5 %copy.23 = bf16[1,128,2048]{1,2,0:T(8,128)(2,1)S(1)} copy(bf16[1,128,2048]{2,1,0:T(8,128)(2,1)} %param.9) | data formatting | bytes 1048576 | tf_op args[2]
  5.6 0.0 copy-start.4
  5.6 0.2 fusion.7
  5.9 0.0 copy-done
  5.9 1.0 copy-done.4
  6.8 0.4 convolution_convert_fusion
  7.3 0.3 convolution_add_fusion
  7.6 0.3 convolution_add_fusion.1
  7.9 0.1 broadcast_in_dim.72
  8.0 0.2 pad_maximum_fusion.pay
  8.1 0.0 copy-start.5
  8.2 85.2 %shard_map.86 = f32[32,128,128]{2,1,0:T(8,128)S(1)} custom-call(f32[32,136,128]{2,1,0:T(8,128)S(1)} %pad_maximum_fusion.pay), custom_call_target="tpu_custom_call" | custom-call | tf_op jit(solution)/shard_map/pallas_call | solution.py:252
  93.4 0.0 copy-start.1
  93.4 0.4 convolution_bitcast_fusion.2
  93.8 0.0 copy-done.5
  93.9 1.1 multiply_reduce_fusion
  95.0 0.2 fusion.4
  95.2 0.0 copy-done.2
  95.2 0.0 copy-done.1
  95.2 0.4 convolution_bitcast_fusion.1
  95.6 0.1 fusion.5
  95.8 1.6 %copy.25 = bf16[4096,128]{1,0:T(8,128)(2,1)S(1)} copy(bf16[4096,128]{0,1:T(8,128)(2,1)} %bitcast.70) | data formatting | bytes 2097152 | tf_op jit(solution)/shard_map/transpose | solution.py:291
  97.4 0.0 copy-start.3
  97.4 0.0 copy-start.6
  97.4 42.7 %shard_map.87 = f32[16,256]{1,0:T(8,128)S(1)} custom-call(bf16[4,2,512,128]{3,2,1,0:T(8,128)(2,1)S(1)} %bitcast.64, bf16[128,256]{1,0:T(8,128)(2,1)S(1)} %pad_maximum_fusion.1.gp_ref), custom_call_target="tpu_custom_call" | custom-call | tf_op jit(solution)/shard_map/pallas_call | solution.py:381
  140.2 0.1 exponential_bitcast_fusion.1
  140.3 1.6 %convolution_multiply_fusion = f32[128,32,64]{0,2,1:T(8,128)S(1)} fusion(f32[128,32]{0,1:T(8,128)S(1)} %exponential_bitcast_fusion.1, bf16[128,256]{1,0:T(8,128)(2,1)S(1)} %convolution_convert_fusion, f32[32,128,128]{2,1,0:T(8,128)} %copy-done.1, f32[32]{0:T(128)S(1)} %get-tuple-element.53), kind=kOutput, calls=%fused_computation.8 | convolution fusion | flops 67895296 | bytes 2146816 | tf_op jit(solution)/shard_map/while/body/eval_jaxpr/hpn,jn->jhp/dot_general | solution.py:74
  141.9 0.1 fusion.24
  142.0 0.0 copy-done.3
  142.0 0.0 copy-done.6
  142.0 1.2 fusion.3
  143.2 1.0 copy.31
  144.2 0.6 copy.39
  (3 shorter events, 0.0 us)
Async XLA Ops:
  0.6 5.2 %copy-start = (bf16[4096,256]{1,0:T(8,128)(2,1)S(1)}, bf16[4096,256]{1,0:T(8,128)(2,1)}, u32[]{:S(2)}) copy-start(bf16[4096,256]{1,0:T(8,128)(2,1)} %param.8) | copy-start | bytes 6291460
  4.1 91.1 %copy-start.2 = (bf16[1,128,2048]{1,2,0:T(8,128)(2,1)}, bf16[1,128,2048]{1,2,0:T(8,128)(2,1)S(1)}, u32[]{:S(2)}) copy-start(bf16[1,128,2048]{1,2,0:T(8,128)(2,1)S(1)} %copy.22) | copy-start | bytes 1572868
  5.6 1.2 copy-start.4
  8.1 85.7 %copy-start.5 = (f32[1,32,128]{2,1,0:T(8,128)S(1)}, f32[1,32,128]{2,1,0:T(8,128)}, u32[]{:S(2)}) copy-start(f32[1,32,128]{2,1,0:T(8,128)} %param.10) | copy-start | bytes 49156
  93.4 1.8 %copy-start.1 = (f32[32,128,128]{2,1,0:T(8,128)}, f32[32,128,128]{2,1,0:T(8,128)S(1)}, u32[]{:S(2)}) copy-start(f32[32,128,128]{2,1,0:T(8,128)S(1)} %shard_map.86) | copy-start | bytes 6291460
  97.4 44.6 %copy-start.3 = (bf16[1,128,2048]{1,2,0:T(8,128)(2,1)S(1)}, bf16[1,128,2048]{1,2,0:T(8,128)(2,1)}, u32[]{:S(2)}) copy-start(bf16[1,128,2048]{1,2,0:T(8,128)(2,1)} %copy-done.2) | copy-start | bytes 1572868
  97.4 44.6 %copy-start.6 = (f32[32]{0:T(128)S(1)}, f32[32]{0:T(128)}, u32[]{:S(2)}) copy-start(f32[32]{0:T(128)} %param.12) | copy-start | bytes 388

commit v10 on v9

--- a/solution.py
+++ b/solution.py
@@ -148,7 +148,7 @@
     group = heads // width
     mesh_id = pl.DeviceIdType.MESH
 
-    def kernel(pay, out_ref, land1, agg, land2, res, land3, out4, land4, sems, local):
+    def kernel(pay, out_ref, land1, agg, land2, res, land3, out4, land4, relay1, relay4, sems, local):
         chip, core = lax.axis_index("x"), lax.axis_index("core")
         z, y = lax.axis_index("z"), lax.axis_index("y")
         barrier = pltpu.get_barrier_semaphore()
@@ -164,17 +164,48 @@
             for copy in copies:
                 copy.wait()
 
+        def across_row(src_of, land, relay, base):
+            near, far = (y + 1) % width, (y + width - 1) % width
+            opposite = (y + 2) % width
+            cut = group // 2
+            direct = []
+            for step, dest in ((1, near), (width - 1, far)):
+                direct.append(pltpu.make_async_remote_copy(
+                    src_ref=src_of(dest), dst_ref=land.at[y], send_sem=sems.at[0, base + step - 1],
+                    recv_sem=sems.at[1, base + step - 1], device_id=(chip, core, z, dest), device_id_type=mesh_id,
+                ))
+            hop = [
+                pltpu.make_async_remote_copy(
+                    src_ref=src_of(opposite).at[pl.ds(0, cut)], dst_ref=relay.at[0], send_sem=sems.at[0, base + 1],
+                    recv_sem=sems.at[1, base + 1], device_id=(chip, core, z, near), device_id_type=mesh_id,
+                ),
+                pltpu.make_async_remote_copy(
+                    src_ref=src_of(opposite).at[pl.ds(cut, cut)], dst_ref=relay.at[1], send_sem=sems.at[0, base + 3],
+                    recv_sem=sems.at[1, base + 3], device_id=(chip, core, z, far), device_id_type=mesh_id,
+                ),
+            ]
+            for copy in direct + hop:
+                copy.start()
+            for copy in hop:
+                copy.wait()
+            onward = [
+                pltpu.make_async_remote_copy(
+                    src_ref=relay.at[0], dst_ref=land.at[far, pl.ds(0, cut)], send_sem=sems.at[0, base + 4],
+                    recv_sem=sems.at[1, base + 4], device_id=(chip, core, z, near), device_id_type=mesh_id,
+                ),
+                pltpu.make_async_remote_copy(
+                    src_ref=relay.at[1], dst_ref=land.at[near, pl.ds(cut, cut)], send_sem=sems.at[0, base + 5],
+                    recv_sem=sems.at[1, base + 5], device_id=(chip, core, z, far), device_id_type=mesh_id,
+                ),
+            ]
+            for copy in onward:
+                copy.start()
+            for copy in direct + onward:
+                copy.wait()
+
         mine = pltpu.make_async_copy(pay.at[pl.ds(y * group, group)], land1.at[y], local.at[0])
         mine.start()
-        first = []
-        for step in range(1, width):
-            dest = (y + step) % width
-            first.append(pltpu.make_async_remote_copy(
-                src_ref=pay.at[pl.ds(dest * group, group)], dst_ref=land1.at[y],
-                send_sem=sems.at[0, step - 1], recv_sem=sems.at[1, step - 1],
-                device_id=(chip, core, z, dest), device_id_type=mesh_id,
-            ))
-        run(first)
+        across_row(lambda m: pay.at[pl.ds(m * group, group)], land1, relay1, 0)
         mine.wait()
         for k in range(group):
             fwd = jnp.zeros((rows, cols), jnp.float32)
@@ -192,7 +223,7 @@
             agg[k, 2 * rows :] = jnp.broadcast_to(total, (8, cols))
         mine = pltpu.make_async_copy(agg.at[z], land2.at[z], local.at[1])
         mine.start()
-        base = width - 1
+        base = 6
         second = []
         for step in range(1, layers):
             dest = (z + step) % layers
@@ -213,7 +244,7 @@
             carry = jnp.exp(land2[r, 2 * rows : 2 * rows + 1]) * carry + land2[r, rows : 2 * rows]
         mine = pltpu.make_async_copy(res.at[z], land3.at[z], local.at[2])
         mine.start()
-        base = width - 1 + layers - 1
+        base = 6 + layers - 1
         third = []
         for step in range(1, layers):
             dest = (z + step) % layers
@@ -235,20 +266,11 @@
                 carry = jnp.exp(land1[w, k, 2 * rows : 2 * rows + 1]) * carry + land1[w, k, rows : 2 * rows]
         mine = pltpu.make_async_copy(out4.at[y], land4.at[y], local.at[3])
         mine.start()
-        base = width - 1 + 2 * (layers - 1)
-        fourth = []
-        for step in range(1, width):
-            dest = (y + step) % width
-            fourth.append(pltpu.make_async_remote_copy(
-                src_ref=out4.at[dest], dst_ref=land4.at[y],
-                send_sem=sems.at[0, base + step - 1], recv_sem=sems.at[1, base + step - 1],
-                device_id=(chip, core, z, dest), device_id_type=mesh_id,
-            ))
-        run(fourth)
+        across_row(lambda m: out4.at[m], land4, relay4, 6 + 2 * (layers - 1))
         mine.wait()
         out_ref[...] = land4[...].reshape(heads, 2 * rows, cols)
 
-    links = 2 * (width - 1) + 2 * (layers - 1)
+    links = 12 + 2 * (layers - 1)
     return pl.pallas_call(
         kernel,
         out_shape=jax.ShapeDtypeStruct((heads, 2 * rows, cols), jnp.float32),
@@ -262,6 +284,8 @@
             pltpu.VMEM((layers, 2 * rows, cols), jnp.float32),
             pltpu.VMEM((width, group, 2 * rows, cols), jnp.float32),
             pltpu.VMEM((width, group, 2 * rows, cols), jnp.float32),
+            pltpu.VMEM((2, group // 2, span, cols), jnp.float32),
+            pltpu.VMEM((2, group // 2, 2 * rows, cols), jnp.float32),
             pltpu.SemaphoreType.DMA((2, links)),
             pltpu.SemaphoreType.DMA((4,)),
         ],

time: 145 us -> 147 us (1.014)
  Pallas kernels: 128 us -> 130 us
    pallas_call x1, Pallas kernels: 42.7 us -> 45.8 us  [weight_grad_sum(): pl.pallas_call(kernel, out_shape=jax.ShapeDtypeStruct((piece, cols), jnp....]
where the time goes in v10:
time: 147 us
  Pallas kernels  130 us (88%)
  local copies, waits for them, and re-layouts  7.35 us (5%)
  matrix products  6.17 us (4%)
  other arithmetic  2.44 us (2%)
    pallas_call x1, Pallas kernels, tiered_exchange(): pl.pallas_call(kernel, out_shape=jax.ShapeDtypeStruct((heads, 2 * rows, c...  83.9 us
    pallas_call x1, Pallas kernels, weight_grad_sum(): pl.pallas_call(kernel, out_shape=jax.ShapeDtypeStruct((piece, cols), jnp....  45.8 us
    unnamed x18, local copies, waits for them, and re-layouts  5.47 us

profile of v10, /device:TPU:32, one launch (start us, length us, event | category | flops | bytes accessed | tf_op | source)
XLA Modules:
  0.0 146.6 jit_solution(14622470718400919615)
XLA Ops:
  0.6 0.0 copy-start
  0.6 1.1 reduce_window_sum.17
  1.8 0.2 slice_reduce_fusion
  2.0 0.8 multiply_bitcast_fusion
  2.8 1.3 copy.22
  4.1 0.0 copy-start.2
  4.1 1.5 %copy.23 = bf16[1,128,2048]{1,2,0:T(8,128)(2,1)S(1)} copy(bf16[1,128,2048]{2,1,0:T(8,128)(2,1)} %param.9) | data formatting | bytes 1048576 | tf_op args[2]
  5.6 0.0 copy-start.4
  5.6 0.2 fusion.7
  5.9 0.0 copy-done
  5.9 1.0 copy-done.4
  6.8 0.4 convolution_convert_fusion
  7.3 0.3 convolution_add_fusion
  7.6 0.3 convolution_add_fusion.1
  7.9 0.1 broadcast_in_dim.72
  8.0 0.2 pad_maximum_fusion.pay
  8.1 0.0 copy-start.5
  8.2 83.9 %shard_map.86 = f32[32,128,128]{2,1,0:T(8,128)S(1)} custom-call(f32[32,136,128]{2,1,0:T(8,128)S(1)} %pad_maximum_fusion.pay), custom_call_target="tpu_custom_call" | custom-call | tf_op jit(solution)/shard_map/pallas_call | solution.py:274
  92.1 0.0 copy-start.1
  92.1 0.4 convolution_bitcast_fusion.2
  92.6 0.0 copy-done.5
  92.6 1.1 multiply_reduce_fusion
  93.7 0.2 fusion.4
  93.9 0.0 copy-done.2
  93.9 0.0 copy-done.1
  93.9 0.4 convolution_bitcast_fusion.1
  94.4 0.1 fusion.5
  94.5 1.6 %copy.25 = bf16[4096,128]{1,0:T(8,128)(2,1)S(1)} copy(bf16[4096,128]{0,1:T(8,128)(2,1)} %bitcast.70) | data formatting | bytes 2097152 | tf_op jit(solution)/shard_map/transpose | solution.py:315
  96.1 0.0 copy-start.3
  96.2 0.0 copy-start.6
  96.2 45.8 %shard_map.87 = f32[16,256]{1,0:T(8,128)S(1)} custom-call(bf16[4,2,512,128]{3,2,1,0:T(8,128)(2,1)S(1)} %bitcast.64, bf16[128,256]{1,0:T(8,128)(2,1)S(1)} %pad_maximum_fusion.1.gp_ref), custom_call_target="tpu_custom_call" | custom-call | tf_op jit(solution)/shard_map/pallas_call | solution.py:405
  142.0 0.1 exponential_bitcast_fusion.1
  142.1 1.6 %convolution_multiply_fusion = f32[128,32,64]{0,2,1:T(8,128)S(1)} fusion(f32[128,32]{0,1:T(8,128)S(1)} %exponential_bitcast_fusion.1, bf16[128,256]{1,0:T(8,128)(2,1)S(1)} %convolution_convert_fusion, f32[32,128,128]{2,1,0:T(8,128)} %copy-done.1, f32[32]{0:T(128)S(1)} %get-tuple-element.53), kind=kOutput, calls=%fused_computation.8 | convolution fusion | flops 67895296 | bytes 2146816 | tf_op jit(solution)/shard_map/while/body/eval_jaxpr/hpn,jn->jhp/dot_general | solution.py:74
  143.7 0.1 fusion.24
  143.8 0.0 copy-done.3
  143.8 0.0 copy-done.6
  143.8 1.2 fusion.3
  145.0 1.0 copy.31
  146.0 0.6 copy.39
  (3 shorter events, 0.0 us)
Async XLA Ops:
  0.6 5.2 %copy-start = (bf16[4096,256]{1,0:T(8,128)(2,1)S(1)}, bf16[4096,256]{1,0:T(8,128)(2,1)}, u32[]{:S(2)}) copy-start(bf16[4096,256]{1,0:T(8,128)(2,1)} %param.8) | copy-start | bytes 6291460
  4.1 89.8 %copy-start.2 = (bf16[1,128,2048]{1,2,0:T(8,128)(2,1)}, bf16[1,128,2048]{1,2,0:T(8,128)(2,1)S(1)}, u32[]{:S(2)}) copy-start(bf16[1,128,2048]{1,2,0:T(8,128)(2,1)S(1)} %copy.22) | copy-start | bytes 1572868
  5.6 1.2 copy-start.4
  8.1 84.4 %copy-start.5 = (f32[1,32,128]{2,1,0:T(8,128)S(1)}, f32[1,32,128]{2,1,0:T(8,128)}, u32[]{:S(2)}) copy-start(f32[1,32,128]{2,1,0:T(8,128)} %param.10) | copy-start | bytes 49156
  92.1 1.8 %copy-start.1 = (f32[32,128,128]{2,1,0:T(8,128)}, f32[32,128,128]{2,1,0:T(8,128)S(1)}, u32[]{:S(2)}) copy-start(f32[32,128,128]{2,1,0:T(8,128)S(1)} %shard_map.86) | copy-start | bytes 6291460
  96.1 47.7 %copy-start.3 = (bf16[1,128,2048]{1,2,0:T(8,128)(2,1)S(1)}, bf16[1,128,2048]{1,2,0:T(8,128)(2,1)}, u32[]{:S(2)}) copy-start(bf16[1,128,2048]{1,2,0:T(8,128)(2,1)} %copy-done.2) | copy-start | bytes 1572868
  96.2 47.7 %copy-start.6 = (f32[32]{0:T(128)S(1)}, f32[32]{0:T(128)}, u32[]{:S(2)}) copy-start(f32[32]{0:T(128)} %param.12) | copy-start | bytes 388

commit v11 on v7

--- a/solution.py
+++ b/solution.py
@@ -141,31 +141,120 @@
     )(payload)
 
 
-def chain_kernel(ends_ref, out_ref):
-    count, _, _ = ends_ref.shape
-    rows = out_ref.shape[1] // 2
-    carry = jnp.zeros((rows, out_ref.shape[2]), jnp.float32)
-    for j in range(count):
-        out_ref[j, :rows] = carry
-        carry = jnp.exp(ends_ref[j, 2 * rows : 2 * rows + 1]) * carry + ends_ref[j, :rows]
-    carry = jnp.zeros_like(carry)
-    for j in reversed(range(count)):
-        out_ref[j, rows:] = carry
-        carry = jnp.exp(ends_ref[j, 2 * rows : 2 * rows + 1]) * carry + ends_ref[j, rows : 2 * rows]
+def tiered_exchange(payload):
+    width, layers = lax.axis_size("y"), lax.axis_size("z")
+    heads, span, cols = payload.shape
+    rows = (span - 8) // 2
+    group = heads // width
+    mesh_id = pl.DeviceIdType.MESH
+    per_wave = 2 * (width - 1) + 2 * (layers - 1)
+
+    def kernel(pay, out_ref, land1, agg, land2, res, land3, out4, land4, sems, local):
+        chip, core = lax.axis_index("x"), lax.axis_index("core")
+        z, y = lax.axis_index("z"), lax.axis_index("y")
+        barrier = pltpu.get_barrier_semaphore()
+        for step in range(1, width):
+            pl.semaphore_signal(barrier, inc=1, device_id=(chip, core, z, (y + step) % width), device_id_type=mesh_id)
+        for step in range(1, layers):
+            pl.semaphore_signal(barrier, inc=1, device_id=(chip, core, (z + step) % layers, y), device_id_type=mesh_id)
+        pl.semaphore_wait(barrier, width - 1 + layers - 1)
+
+        def tier(src_of, dst, size, where, place, wave, base, slot):
+            first = pltpu.make_async_copy(src_of(where), dst, local.at[wave, slot])
+            copies = [first]
+            for step in range(1, size):
+                dest = (where + step) % size
+                copies.append(pltpu.make_async_remote_copy(
+                    src_ref=src_of(dest), dst_ref=dst, send_sem=sems.at[0, wave, base + step - 1],
+                    recv_sem=sems.at[1, wave, base + step - 1], device_id=place(dest), device_id_type=mesh_id,
+                ))
+            for copy in copies:
+                copy.start()
+            return copies
+
+        def finish(copies):
+            for copy in copies:
+                copy.wait()
+
+        row_place = lambda m: (chip, core, z, m)
+        col_place = lambda m: (chip, core, m, y)
+        lo = (0, rows)
+        n = (rows + 8, rows)
+        t1 = [
+            tier(lambda m, w=w: pay.at[pl.ds(m * group, group), w], land1.at[w, y], width, y, row_place, w, 0, 0)
+            for w in range(2)
+        ]
+        for w in range(2):
+            finish(t1[w])
+            for k in range(group):
+                carry = jnp.zeros((rows, cols), jnp.float32)
+                total = jnp.zeros((1, cols), jnp.float32)
+                order = range(width) if w == 0 else reversed(range(width))
+                for m in order:
+                    mark = land1[0, m, k, rows : rows + 1]
+                    carry = jnp.exp(mark) * carry + land1[w, m, k, :rows]
+                    total = total + mark
+                agg[w, k, :rows] = carry
+                agg[w, k, rows:] = jnp.broadcast_to(total * (1 - w), (8, cols))
+            t2 = tier(lambda m, w=w: agg.at[w, m], land2.at[w, z], layers, z, col_place, w, width - 1, 1)
+            if w == 0:
+                t2_first = t2
+        finish(t2_first)
+        finish(t2)
+        for w in range(2):
+            carry = jnp.zeros((rows, cols), jnp.float32)
+            order = range(layers) if w == 0 else reversed(range(layers))
+            for r in order:
+                res[w, r] = carry
+                carry = jnp.exp(land2[0, r, rows : rows + 1]) * carry + land2[w, r, :rows]
+            t3 = tier(lambda m, w=w: res.at[w, m], land3.at[w, z], layers, z, col_place, w, width + layers - 2, 2)
+            if w == 0:
+                t3_first = t3
+        t4 = []
+        for w, t3w in ((0, t3_first), (1, t3)):
+            finish(t3w)
+            for k in range(group):
+                carry = land3[w, k]
+                order = range(width) if w == 0 else reversed(range(width))
+                for m in order:
+                    out4[w, m, k] = carry
+                    carry = jnp.exp(land1[0, m, k, rows : rows + 1]) * carry + land1[w, m, k, :rows]
+            t4.append(tier(lambda m, w=w: out4.at[w, m], land4.at[w, y], width, y, row_place, w, width + 2 * layers - 3, 3))
+        for copies in t4:
+            finish(copies)
+        out_ref[:, :rows] = land4[0].reshape(heads, rows, cols)
+        out_ref[:, rows:] = land4[1].reshape(heads, rows, cols)
+
+    fwd = jnp.concatenate([payload[:, :rows], payload[:, 2 * rows :]], axis=1)
+    bwd = jnp.pad(payload[:, rows : 2 * rows], ((0, 0), (0, 8), (0, 0)))
+    body = jnp.stack([fwd, bwd], axis=1)
+    return pl.pallas_call(
+        kernel,
+        out_shape=jax.ShapeDtypeStruct((heads, 2 * rows, cols), jnp.float32),
+        in_specs=[pl.BlockSpec(memory_space=pltpu.VMEM)],
+        out_specs=pl.BlockSpec(memory_space=pltpu.VMEM),
+        scratch_shapes=[
+            pltpu.VMEM((2, width, group, rows + 8, cols), jnp.float32),
+            pltpu.VMEM((2, group, rows + 8, cols), jnp.float32),
+            pltpu.VMEM((2, layers, rows + 8, cols), jnp.float32),
+            pltpu.VMEM((2, layers, rows, cols), jnp.float32),
+            pltpu.VMEM((2, layers, rows, cols), jnp.float32),
+            pltpu.VMEM((2, width, group, rows, cols), jnp.float32),
+            pltpu.VMEM((2, width, group, rows, cols), jnp.float32),
+            pltpu.SemaphoreType.DMA((2, 2, per_wave)),
+            pltpu.SemaphoreType.DMA((2, 4)),
+        ],
+        compiler_params=pltpu.CompilerParams(
+            collective_id=0, has_side_effects=True, vmem_limit_bytes=48 * 1024 * 1024
+        ),
+    )(body)
 
 
 def exchange(own_state, own_grad, device_total):
     heads, rows, cols = own_state.shape
     marks = jnp.broadcast_to(device_total[:, None, None], (heads, 8, cols))
     payload = jnp.concatenate([own_state, own_grad, marks], axis=1)
-    mine = lax.all_to_all(payload, ("z", "y"), 0, 0, tiled=True)
-    entries = pl.pallas_call(
-        chain_kernel,
-        out_shape=jax.ShapeDtypeStruct((heads, 2 * rows, cols), jnp.float32),
-        in_specs=[pl.BlockSpec(memory_space=pltpu.VMEM)],
-        out_specs=pl.BlockSpec(memory_space=pltpu.VMEM),
-    )(mine)
-    back = lax.all_to_all(entries, ("z", "y"), 0, 0, tiled=True)
+    back = tiered_exchange(payload)
     return back[:, :rows], back[:, rows:]
 
 
@@ -189,6 +278,15 @@
         me = z * width + y
         spot = chip * layers + z
         other = 1 - core
+        barrier = pltpu.get_barrier_semaphore()
+        pl.semaphore_signal(barrier, inc=1, device_id=(chip, other, z, y), device_id_type=mesh_id)
+        for step in range(1, count):
+            dest = (me + step) % count
+            pl.semaphore_signal(barrier, inc=1, device_id=(chip, core, dest // width, dest % width), device_id_type=mesh_id)
+        for step in range(1, chips * layers):
+            dest = (spot + step) % (chips * layers)
+            pl.semaphore_signal(barrier, inc=1, device_id=(dest // layers, core, dest % layers, y), device_id_type=mesh_id)
+        pl.semaphore_wait(barrier, count + chips * layers - 1)
         gp = gp_ref[...]
         for c in range(chips):
             send1[c] = jnp.dot(tok_ref[c, other], gp, preferred_element_type=jnp.float32)
@@ -277,7 +375,9 @@
             pltpu.VMEM((chips * layers - 1, piece, half), jnp.float32),
             pltpu.SemaphoreType.DMA((2, chips + width + count + chips * layers)),
         ],
-        compiler_params=pltpu.CompilerParams(has_side_effects=True, vmem_limit_bytes=48 * 1024 * 1024),
+        compiler_params=pltpu.CompilerParams(
+            collective_id=1, has_side_effects=True, vmem_limit_bytes=48 * 1024 * 1024
+        ),
     )(by_owner, grad_proj)
 
 

time: 188 us -> 135 us (0.72)
  Pallas kernels: 49.9 us -> 117 us
  blocking collectives: 65.7 us -> 0 us
  waiting for transfers between devices: 43.8 us -> 0 us
  starting transfers between devices: 5.56 us -> 0 us
  matrix products: 11.4 us -> 6.18 us
    pallas_call x1, Pallas kernels: 3.12 us -> 75.5 us  [tiered_exchange(): pl.pallas_call(kernel, out_shape=jax.ShapeDtypeStruct((heads, 2 * rows, c...]
    all_to_all x1 -> x0, blocking collectives: 65.7 us -> none  [exchange(): mine = lax.all_to_all(payload, ('z', 'y'), 0, 0, tiled=True)]
    all_to_all x1 -> x0, waiting for transfers between devices: 43.8 us -> none  [exchange(): back = lax.all_to_all(entries, ('z', 'y'), 0, 0, tiled=True)]
    all_to_all x1 -> x0, starting transfers between devices: 5.56 us -> none  [exchange(): back = lax.all_to_all(entries, ('z', 'y'), 0, 0, tiled=True)]
    pallas_call x1, Pallas kernels: 46.8 us -> 41.5 us  [weight_grad_sum(): pl.pallas_call(kernel, out_shape=jax.ShapeDtypeStruct((piece, cols), jnp....]
    unnamed x16 -> x18, local copies, waits for them, and re-layouts: 4.46 us -> 5.47 us
  transfers between devices with their start and end apart: 1 -> 0, of which waited for: 1 -> 0; matrix products, arithmetic and copies ran while one was open for 2% -> 0% of each run, Pallas kernels for 0% -> 0%
where the time goes in v11:
time: 135 us; the launch traced here: 134 us
  Pallas kernels  117 us (87%)
  local copies, waits for them, and re-layouts  7.43 us (6%)
  matrix products  6.18 us (5%)
  other arithmetic  2.66 us (2%)
    pallas_call x1, Pallas kernels, tiered_exchange(): pl.pallas_call(kernel, out_shape=jax.ShapeDtypeStruct((heads, 2 * rows, c...  75.5 us
    pallas_call x1, Pallas kernels, weight_grad_sum(): pl.pallas_call(kernel, out_shape=jax.ShapeDtypeStruct((piece, cols), jnp....  41.5 us
    unnamed x18, local copies, waits for them, and re-layouts  5.47 us

profile of v11, /device:TPU:32, one launch (start us, length us, event | category | flops | bytes accessed | tf_op | source)
XLA Modules:
  0.0 134.1 jit_solution(17856391608733022122)
XLA Ops:
  0.6 0.0 copy-start
  0.6 1.1 reduce_window_sum.17
  1.8 0.2 slice_reduce_fusion
  2.0 0.8 multiply_bitcast_fusion
  2.8 1.3 copy.23
  4.1 0.0 copy-start.2
  4.1 1.5 %copy.24 = bf16[1,128,2048]{1,2,0:T(8,128)(2,1)S(1)} copy(bf16[1,128,2048]{2,1,0:T(8,128)(2,1)} %param.9) | data formatting | bytes 1048576 | tf_op args[2]
  5.6 0.0 copy-start.4
  5.6 0.2 fusion.7
  5.9 0.0 copy-done
  5.9 1.0 copy-done.4
  6.8 0.4 convolution_convert_fusion
  7.3 0.3 convolution_add_fusion.1
  7.6 0.1 broadcast_in_dim.72
  7.7 0.1 maximum_bitcast_fusion
  7.8 0.3 convolution_add_fusion
  8.1 0.1 pad_bitcast_fusion
  8.2 0.3 pad_maximum_fusion.pay
  8.5 0.0 copy-start.5
  8.5 75.5 %shard_map.86 = f32[32,128,128]{2,1,0:T(8,128)S(1)} custom-call(f32[32,2,72,128]{3,2,1,0:T(8,128)S(1)} %pad_maximum_fusion.pay), custom_call_target="tpu_custom_call" | custom-call | tf_op jit(solution)/shard_map/pallas_call | solution.py:231
  83.9 0.0 copy-start.1
  84.0 0.4 convolution_bitcast_fusion.2
  84.4 0.0 copy-done.5
  84.4 1.1 multiply_reduce_fusion
  85.5 0.2 fusion.4
  85.7 0.0 copy-done.2
  85.8 0.0 copy-done.1
  85.8 0.4 convolution_bitcast_fusion.1
  86.2 0.1 fusion.5
  86.4 1.6 %copy.27 = bf16[4096,128]{1,0:T(8,128)(2,1)S(1)} copy(bf16[4096,128]{0,1:T(8,128)(2,1)} %bitcast.76) | data formatting | bytes 2097152 | tf_op jit(solution)/shard_map/transpose | solution.py:270
  88.0 0.0 copy-start.3
  88.0 0.0 copy-start.6
  88.0 41.5 %shard_map.87 = f32[16,256]{1,0:T(8,128)S(1)} custom-call(bf16[4,2,512,128]{3,2,1,0:T(8,128)(2,1)S(1)} %bitcast.70, bf16[128,256]{1,0:T(8,128)(2,1)S(1)} %pad_maximum_fusion.1.gp_ref), custom_call_target="tpu_custom_call" | custom-call | tf_op jit(solution)/shard_map/pallas_call | solution.py:360
  129.5 0.1 exponential_bitcast_fusion.1
  129.6 1.6 %convolution_multiply_fusion = f32[128,32,64]{0,2,1:T(8,128)S(1)} fusion(f32[128,32]{0,1:T(8,128)S(1)} %exponential_bitcast_fusion.1, bf16[128,256]{1,0:T(8,128)(2,1)S(1)} %convolution_convert_fusion, f32[32,128,128]{2,1,0:T(8,128)} %copy-done.1, f32[32]{0:T(128)S(1)} %get-tuple-element.53), kind=kOutput, calls=%fused_computation.8 | convolution fusion | flops 67895296 | bytes 2146816 | tf_op jit(solution)/shard_map/while/body/eval_jaxpr/hpn,jn->jhp/dot_general | solution.py:74
  131.2 0.1 fusion.24
  131.3 0.0 copy-done.3
  131.3 0.0 copy-done.6
  131.3 1.2 fusion.3
  132.5 1.0 copy.33
  133.5 0.6 copy.41
  (3 shorter events, 0.0 us)
Async XLA Ops:
  0.6 5.2 %copy-start = (bf16[4096,256]{1,0:T(8,128)(2,1)S(1)}, bf16[4096,256]{1,0:T(8,128)(2,1)}, u32[]{:S(2)}) copy-start(bf16[4096,256]{1,0:T(8,128)(2,1)} %param.8) | copy-start | bytes 6291460
  4.1 81.6 %copy-start.2 = (bf16[1,128,2048]{1,2,0:T(8,128)(2,1)}, bf16[1,128,2048]{1,2,0:T(8,128)(2,1)S(1)}, u32[]{:S(2)}) copy-start(bf16[1,128,2048]{1,2,0:T(8,128)(2,1)S(1)} %copy.23) | copy-start | bytes 1572868
  5.6 1.2 copy-start.4
  8.5 76.0 %copy-start.5 = (f32[1,32,128]{2,1,0:T(8,128)S(1)}, f32[1,32,128]{2,1,0:T(8,128)}, u32[]{:S(2)}) copy-start(f32[1,32,128]{2,1,0:T(8,128)} %param.10) | copy-start | bytes 49156
  83.9 1.8 %copy-start.1 = (f32[32,128,128]{2,1,0:T(8,128)}, f32[32,128,128]{2,1,0:T(8,128)S(1)}, u32[]{:S(2)}) copy-start(f32[32,128,128]{2,1,0:T(8,128)S(1)} %shard_map.86) | copy-start | bytes 6291460
  88.0 43.3 %copy-start.3 = (bf16[1,128,2048]{1,2,0:T(8,128)(2,1)S(1)}, bf16[1,128,2048]{1,2,0:T(8,128)(2,1)}, u32[]{:S(2)}) copy-start(bf16[1,128,2048]{1,2,0:T(8,128)(2,1)} %copy-done.2) | copy-start | bytes 1572868
  88.0 43.3 %copy-start.6 = (f32[32]{0:T(128)S(1)}, f32[32]{0:T(128)}, u32[]{:S(2)}) copy-start(f32[32]{0:T(128)} %param.12) | copy-start | bytes 388

commit v12 on v11

--- a/solution.py
+++ b/solution.py
@@ -180,12 +180,14 @@
         col_place = lambda m: (chip, core, m, y)
         lo = (0, rows)
         n = (rows + 8, rows)
-        t1 = [
-            tier(lambda m, w=w: pay.at[pl.ds(m * group, group), w], land1.at[w, y], width, y, row_place, w, 0, 0)
-            for w in range(2)
-        ]
+        def row_tier(w):
+            return tier(lambda m: pay.at[pl.ds(m * group, group), w], land1.at[w, y], width, y, row_place, w, 0, 0)
+
+        t1 = [row_tier(0)]
         for w in range(2):
             finish(t1[w])
+            if w == 0:
+                t1.append(row_tier(1))
             for k in range(group):
                 carry = jnp.zeros((rows, cols), jnp.float32)
                 total = jnp.zeros((1, cols), jnp.float32)
@@ -207,12 +209,13 @@
             for r in order:
                 res[w, r] = carry
                 carry = jnp.exp(land2[0, r, rows : rows + 1]) * carry + land2[w, r, :rows]
-            t3 = tier(lambda m, w=w: res.at[w, m], land3.at[w, z], layers, z, col_place, w, width + layers - 2, 2)
             if w == 0:
-                t3_first = t3
+                t3 = [tier(lambda m: res.at[0, m], land3.at[0, z], layers, z, col_place, 0, width + layers - 2, 2)]
         t4 = []
-        for w, t3w in ((0, t3_first), (1, t3)):
-            finish(t3w)
+        for w in range(2):
+            finish(t3[w])
+            if w == 0:
+                t3.append(tier(lambda m: res.at[1, m], land3.at[1, z], layers, z, col_place, 1, width + layers - 2, 2))
             for k in range(group):
                 carry = land3[w, k]
                 order = range(width) if w == 0 else reversed(range(width))

time: 135 us -> 138 us (1.022)
  Pallas kernels: 117 us -> 120 us
    pallas_call x1, Pallas kernels: 75.5 us -> 77.4 us  [tiered_exchange(): pl.pallas_call(kernel, out_shape=jax.ShapeDtypeStruct((heads, 2 * rows, c...]
where the time goes in v12:
time: 138 us; the launch traced here: 137 us
  Pallas kernels  120 us (87%)
  local copies, waits for them, and re-layouts  7.43 us (5%)
  matrix products  6.18 us (4%)
  other arithmetic  2.66 us (2%)
    pallas_call x1, Pallas kernels, tiered_exchange(): pl.pallas_call(kernel, out_shape=jax.ShapeDtypeStruct((heads, 2 * rows, c...  77.4 us
    pallas_call x1, Pallas kernels, weight_grad_sum(): pl.pallas_call(kernel, out_shape=jax.ShapeDtypeStruct((piece, cols), jnp....  42.2 us
    unnamed x18, local copies, waits for them, and re-layouts  5.47 us

profile of v12, /device:TPU:32, one launch (start us, length us, event | category | flops | bytes accessed | tf_op | source)
XLA Modules:
  0.0 136.8 jit_solution(13309025094169047283)
XLA Ops:
  0.6 0.0 copy-start
  0.6 1.1 reduce_window_sum.17
  1.8 0.2 slice_reduce_fusion
  2.0 0.8 multiply_bitcast_fusion
  2.8 1.3 copy.23
  4.1 0.0 copy-start.2
  4.1 1.5 %copy.24 = bf16[1,128,2048]{1,2,0:T(8,128)(2,1)S(1)} copy(bf16[1,128,2048]{2,1,0:T(8,128)(2,1)} %param.9) | data formatting | bytes 1048576 | tf_op args[2]
  5.6 0.0 copy-start.4
  5.6 0.2 fusion.7
  5.9 0.0 copy-done
  5.9 1.0 copy-done.4
  6.8 0.4 convolution_convert_fusion
  7.3 0.3 convolution_add_fusion.1
  7.6 0.1 broadcast_in_dim.72
  7.7 0.1 maximum_bitcast_fusion
  7.8 0.3 convolution_add_fusion
  8.1 0.1 pad_bitcast_fusion
  8.2 0.3 pad_maximum_fusion.pay
  8.5 0.0 copy-start.5
  8.5 77.4 %shard_map.86 = f32[32,128,128]{2,1,0:T(8,128)S(1)} custom-call(f32[32,2,72,128]{3,2,1,0:T(8,128)S(1)} %pad_maximum_fusion.pay), custom_call_target="tpu_custom_call" | custom-call | tf_op jit(solution)/shard_map/pallas_call | solution.py:234
  85.9 0.0 copy-start.1
  85.9 0.4 convolution_bitcast_fusion.2
  86.4 0.0 copy-done.5
  86.4 1.1 multiply_reduce_fusion
  87.5 0.2 fusion.4
  87.7 0.0 copy-done.2
  87.7 0.0 copy-done.1
  87.7 0.4 convolution_bitcast_fusion.1
  88.2 0.1 fusion.5
  88.3 1.6 %copy.27 = bf16[4096,128]{1,0:T(8,128)(2,1)S(1)} copy(bf16[4096,128]{0,1:T(8,128)(2,1)} %bitcast.76) | data formatting | bytes 2097152 | tf_op jit(solution)/shard_map/transpose | solution.py:273
  89.9 0.0 copy-start.3
  89.9 0.0 copy-start.6
  90.0 42.2 %shard_map.87 = f32[16,256]{1,0:T(8,128)S(1)} custom-call(bf16[4,2,512,128]{3,2,1,0:T(8,128)(2,1)S(1)} %bitcast.70, bf16[128,256]{1,0:T(8,128)(2,1)S(1)} %pad_maximum_fusion.1.gp_ref), custom_call_target="tpu_custom_call" | custom-call | tf_op jit(solution)/shard_map/pallas_call | solution.py:363
  132.2 0.1 exponential_bitcast_fusion.1
  132.3 1.6 %convolution_multiply_fusion = f32[128,32,64]{0,2,1:T(8,128)S(1)} fusion(f32[128,32]{0,1:T(8,128)S(1)} %exponential_bitcast_fusion.1, bf16[128,256]{1,0:T(8,128)(2,1)S(1)} %convolution_convert_fusion, f32[32,128,128]{2,1,0:T(8,128)} %copy-done.1, f32[32]{0:T(128)S(1)} %get-tuple-element.53), kind=kOutput, calls=%fused_computation.8 | convolution fusion | flops 67895296 | bytes 2146816 | tf_op jit(solution)/shard_map/while/body/eval_jaxpr/hpn,jn->jhp/dot_general | solution.py:74
  133.9 0.1 fusion.24
  134.0 0.0 copy-done.3
  134.0 0.0 copy-done.6
  134.0 1.2 fusion.3
  135.2 1.0 copy.33
  136.2 0.6 copy.41
  (3 shorter events, 0.0 us)
Async XLA Ops:
  0.6 5.2 %copy-start = (bf16[4096,256]{1,0:T(8,128)(2,1)S(1)}, bf16[4096,256]{1,0:T(8,128)(2,1)}, u32[]{:S(2)}) copy-start(bf16[4096,256]{1,0:T(8,128)(2,1)} %param.8) | copy-start | bytes 6291460
  4.1 83.6 %copy-start.2 = (bf16[1,128,2048]{1,2,0:T(8,128)(2,1)}, bf16[1,128,2048]{1,2,0:T(8,128)(2,1)S(1)}, u32[]{:S(2)}) copy-start(bf16[1,128,2048]{1,2,0:T(8,128)(2,1)S(1)} %copy.23) | copy-start | bytes 1572868
  5.6 1.2 copy-start.4
  8.5 77.9 %copy-start.5 = (f32[1,32,128]{2,1,0:T(8,128)S(1)}, f32[1,32,128]{2,1,0:T(8,128)}, u32[]{:S(2)}) copy-start(f32[1,32,128]{2,1,0:T(8,128)} %param.10) | copy-start | bytes 49156
  85.9 1.8 %copy-start.1 = (f32[32,128,128]{2,1,0:T(8,128)}, f32[32,128,128]{2,1,0:T(8,128)S(1)}, u32[]{:S(2)}) copy-start(f32[32,128,128]{2,1,0:T(8,128)S(1)} %shard_map.86) | copy-start | bytes 6291460
  89.9 44.1 %copy-start.3 = (bf16[1,128,2048]{1,2,0:T(8,128)(2,1)S(1)}, bf16[1,128,2048]{1,2,0:T(8,128)(2,1)}, u32[]{:S(2)}) copy-start(bf16[1,128,2048]{1,2,0:T(8,128)(2,1)} %copy-done.2) | copy-start | bytes 1572868
  89.9 44.1 %copy-start.6 = (f32[32]{0:T(128)S(1)}, f32[32]{0:T(128)}, u32[]{:S(2)}) copy-start(f32[32]{0:T(128)} %param.12) | copy-start | bytes 388

commit v13 on v11

--- a/solution.py
+++ b/solution.py
@@ -146,6 +146,8 @@
     heads, span, cols = payload.shape
     rows = (span - 8) // 2
     group = heads // width
+    part = rows // 2
+    waves = 4
     mesh_id = pl.DeviceIdType.MESH
     per_wave = 2 * (width - 1) + 2 * (layers - 1)
 
@@ -178,71 +180,71 @@
 
         row_place = lambda m: (chip, core, z, m)
         col_place = lambda m: (chip, core, m, y)
-        lo = (0, rows)
-        n = (rows + 8, rows)
         t1 = [
             tier(lambda m, w=w: pay.at[pl.ds(m * group, group), w], land1.at[w, y], width, y, row_place, w, 0, 0)
-            for w in range(2)
+            for w in range(waves)
         ]
-        for w in range(2):
+        t2 = []
+        for w in range(waves):
             finish(t1[w])
             for k in range(group):
-                carry = jnp.zeros((rows, cols), jnp.float32)
+                carry = jnp.zeros((part, cols), jnp.float32)
                 total = jnp.zeros((1, cols), jnp.float32)
-                order = range(width) if w == 0 else reversed(range(width))
+                order = range(width) if w < 2 else reversed(range(width))
                 for m in order:
-                    mark = land1[0, m, k, rows : rows + 1]
-                    carry = jnp.exp(mark) * carry + land1[w, m, k, :rows]
+                    mark = land1[0, m, k, part : part + 1]
+                    carry = jnp.exp(mark) * carry + land1[w, m, k, :part]
                     total = total + mark
-                agg[w, k, :rows] = carry
-                agg[w, k, rows:] = jnp.broadcast_to(total * (1 - w), (8, cols))
-            t2 = tier(lambda m, w=w: agg.at[w, m], land2.at[w, z], layers, z, col_place, w, width - 1, 1)
-            if w == 0:
-                t2_first = t2
-        finish(t2_first)
-        finish(t2)
-        for w in range(2):
-            carry = jnp.zeros((rows, cols), jnp.float32)
-            order = range(layers) if w == 0 else reversed(range(layers))
+                agg[w, k, :part] = carry
+                agg[w, k, part:] = jnp.broadcast_to(total * (1 if w == 0 else 0), (8, cols))
+            t2.append(tier(lambda m, w=w: agg.at[w, m], land2.at[w, z], layers, z, col_place, w, width - 1, 1))
+        t3 = []
+        for w in range(waves):
+            finish(t2[w])
+            carry = jnp.zeros((part, cols), jnp.float32)
+            order = range(layers) if w < 2 else reversed(range(layers))
             for r in order:
                 res[w, r] = carry
-                carry = jnp.exp(land2[0, r, rows : rows + 1]) * carry + land2[w, r, :rows]
-            t3 = tier(lambda m, w=w: res.at[w, m], land3.at[w, z], layers, z, col_place, w, width + layers - 2, 2)
-            if w == 0:
-                t3_first = t3
+                carry = jnp.exp(land2[0, r, part : part + 1]) * carry + land2[w, r, :part]
+            t3.append(tier(lambda m, w=w: res.at[w, m], land3.at[w, z], layers, z, col_place, w, width + layers - 2, 2))
         t4 = []
-        for w, t3w in ((0, t3_first), (1, t3)):
-            finish(t3w)
+        for w in range(waves):
+            finish(t3[w])
             for k in range(group):
                 carry = land3[w, k]
-                order = range(width) if w == 0 else reversed(range(width))
+                order = range(width) if w < 2 else reversed(range(width))
                 for m in order:
                     out4[w, m, k] = carry
-                    carry = jnp.exp(land1[0, m, k, rows : rows + 1]) * carry + land1[w, m, k, :rows]
+                    carry = jnp.exp(land1[0, m, k, part : part + 1]) * carry + land1[w, m, k, :part]
             t4.append(tier(lambda m, w=w: out4.at[w, m], land4.at[w, y], width, y, row_place, w, width + 2 * layers - 3, 3))
-        for copies in t4:
-            finish(copies)
-        out_ref[:, :rows] = land4[0].reshape(heads, rows, cols)
-        out_ref[:, rows:] = land4[1].reshape(heads, rows, cols)
-
-    fwd = jnp.concatenate([payload[:, :rows], payload[:, 2 * rows :]], axis=1)
-    bwd = jnp.pad(payload[:, rows : 2 * rows], ((0, 0), (0, 8), (0, 0)))
-    body = jnp.stack([fwd, bwd], axis=1)
+        for w in range(waves):
+            finish(t4[w])
+            out_ref[:, w * part : (w + 1) * part] = land4[w].reshape(heads, part, cols)
+
+    marks = payload[:, 2 * rows :]
+    blank = jnp.zeros_like(marks)
+    body = jnp.stack(
+        [
+            jnp.concatenate([payload[:, w * part : (w + 1) * part], marks if w == 0 else blank], axis=1)
+            for w in range(waves)
+        ],
+        axis=1,
+    )
     return pl.pallas_call(
         kernel,
         out_shape=jax.ShapeDtypeStruct((heads, 2 * rows, cols), jnp.float32),
         in_specs=[pl.BlockSpec(memory_space=pltpu.VMEM)],
         out_specs=pl.BlockSpec(memory_space=pltpu.VMEM),
         scratch_shapes=[
-            pltpu.VMEM((2, width, group, rows + 8, cols), jnp.float32),
-            pltpu.VMEM((2, group, rows + 8, cols), jnp.float32),
-            pltpu.VMEM((2, layers, rows + 8, cols), jnp.float32),
-            pltpu.VMEM((2, layers, rows, cols), jnp.float32),
-            pltpu.VMEM((2, layers, rows, cols), jnp.float32),
-            pltpu.VMEM((2, width, group, rows, cols), jnp.float32),
-            pltpu.VMEM((2, width, group, rows, cols), jnp.float32),
-            pltpu.SemaphoreType.DMA((2, 2, per_wave)),
-            pltpu.SemaphoreType.DMA((2, 4)),
+            pltpu.VMEM((waves, width, group, part + 8, cols), jnp.float32),
+            pltpu.VMEM((waves, group, part + 8, cols), jnp.float32),
+            pltpu.VMEM((waves, layers, part + 8, cols), jnp.float32),
+            pltpu.VMEM((waves, layers, part, cols), jnp.float32),
+            pltpu.VMEM((waves, layers, part, cols), jnp.float32),
+            pltpu.VMEM((waves, width, group, part, cols), jnp.float32),
+            pltpu.VMEM((waves, width, group, part, cols), jnp.float32),
+            pltpu.SemaphoreType.DMA((2, waves, per_wave)),
+            pltpu.SemaphoreType.DMA((waves, 4)),
         ],
         compiler_params=pltpu.CompilerParams(
             collective_id=0, has_side_effects=True, vmem_limit_bytes=48 * 1024 * 1024

time: 135 us -> 134 us (level); the launches traced: 134 us -> 131 us
  Pallas kernels: 117 us -> 114 us
    pallas_call x1, Pallas kernels: 75.5 us -> 70.8 us  [tiered_exchange(): pl.pallas_call(kernel, out_shape=jax.ShapeDtypeStruct((heads, 2 * rows, c...]
    pallas_call x1, Pallas kernels: 41.5 us -> 42.9 us  [weight_grad_sum(): pl.pallas_call(kernel, out_shape=jax.ShapeDtypeStruct((piece, cols), jnp....]
    unnamed x18 -> x20, local copies, waits for them, and re-layouts: 5.47 us -> 5.73 us
where the time goes in v13:
time: 134 us; the launch traced here: 131 us
  Pallas kernels  114 us (85%)
  local copies, waits for them, and re-layouts  7.82 us (6%)
  matrix products  6.18 us (5%)
  other arithmetic  2.61 us (2%)
    pallas_call x1, Pallas kernels, tiered_exchange(): pl.pallas_call(kernel, out_shape=jax.ShapeDtypeStruct((heads, 2 * rows, c...  70.8 us
    pallas_call x1, Pallas kernels, weight_grad_sum(): pl.pallas_call(kernel, out_shape=jax.ShapeDtypeStruct((piece, cols), jnp....  42.9 us
    unnamed x20, local copies, waits for them, and re-layouts  5.73 us

profile of v13, /device:TPU:32, one launch (start us, length us, event | category | flops | bytes accessed | tf_op | source)
XLA Modules:
  0.0 131.3 jit_solution(16908248876000089980)
XLA Ops:
  0.6 0.0 copy-start
  0.6 1.1 reduce_window_sum.17
  1.8 0.2 slice_reduce_fusion
  2.0 0.8 multiply_bitcast_fusion
  2.8 1.3 copy.25
  4.1 0.0 copy-start.2
  4.1 1.5 %copy.26 = bf16[1,128,2048]{1,2,0:T(8,128)(2,1)S(1)} copy(bf16[1,128,2048]{2,1,0:T(8,128)(2,1)} %param.9) | data formatting | bytes 1048576 | tf_op args[2]
  5.6 0.0 copy-start.4
  5.6 0.2 fusion.7
  5.9 0.0 copy-done
  5.9 1.0 copy-done.4
  6.8 0.4 convolution_convert_fusion
  7.3 0.3 convolution_add_fusion.1
  7.6 0.1 fusion.34
  7.7 0.1 broadcast_in_dim.73
  7.9 0.0 copy-start.6
  7.9 0.3 convolution_add_fusion
  8.3 0.3 copy-done.6
  8.5 0.1 fusion.15
  8.7 0.2 pad_maximum_fusion.pay
  8.8 0.0 copy-start.5
  8.8 70.8 %shard_map.86 = f32[32,128,128]{2,1,0:T(8,128)S(1)} custom-call(f32[32,4,40,128]{3,2,1,0:T(8,128)S(1)} %pad_maximum_fusion.pay), custom_call_target="tpu_custom_call" | custom-call | tf_op jit(solution)/shard_map/pallas_call | solution.py:233
  79.6 0.0 copy-start.1
  79.6 0.4 convolution_bitcast_fusion.2
  80.1 0.0 copy-done.5
  80.1 1.1 multiply_reduce_fusion
  81.2 0.2 fusion.4
  81.4 0.0 copy-done.2
  81.4 0.0 copy-done.1
  81.5 0.4 convolution_bitcast_fusion.1
  81.9 0.1 fusion.5
  82.1 1.6 %copy.31 = bf16[4096,128]{1,0:T(8,128)(2,1)S(1)} copy(bf16[4096,128]{0,1:T(8,128)(2,1)} %bitcast.84) | data formatting | bytes 2097152 | tf_op jit(solution)/shard_map/transpose | solution.py:272
  83.7 0.0 copy-start.3
  83.7 0.0 copy-start.7
  83.7 42.9 %shard_map.87 = f32[16,256]{1,0:T(8,128)S(1)} custom-call(bf16[4,2,512,128]{3,2,1,0:T(8,128)(2,1)S(1)} %bitcast.78, bf16[128,256]{1,0:T(8,128)(2,1)S(1)} %pad_maximum_fusion.1.gp_ref), custom_call_target="tpu_custom_call" | custom-call | tf_op jit(solution)/shard_map/pallas_call | solution.py:362
  126.7 0.1 exponential_bitcast_fusion.1
  126.7 1.6 %convolution_multiply_fusion = f32[128,32,64]{0,2,1:T(8,128)S(1)} fusion(f32[128,32]{0,1:T(8,128)S(1)} %exponential_bitcast_fusion.1, bf16[128,256]{1,0:T(8,128)(2,1)S(1)} %convolution_convert_fusion, f32[32,128,128]{2,1,0:T(8,128)} %copy-done.1, f32[32]{0:T(128)S(1)} %get-tuple-element.70), kind=kOutput, calls=%fused_computation.8 | convolution fusion | flops 67895296 | bytes 2146816 | tf_op jit(solution)/shard_map/while/body/eval_jaxpr/hpn,jn->jhp/dot_general | solution.py:74
  128.3 0.1 fusion.25
  128.5 0.0 copy-done.3
  128.5 0.0 copy-done.7
  128.5 1.2 fusion.3
  129.6 1.0 copy.37
  130.7 0.6 copy.45
  (7 shorter events, 0.2 us)
Async XLA Ops:
  0.6 5.2 %copy-start = (bf16[4096,256]{1,0:T(8,128)(2,1)S(1)}, bf16[4096,256]{1,0:T(8,128)(2,1)}, u32[]{:S(2)}) copy-start(bf16[4096,256]{1,0:T(8,128)(2,1)} %param.8) | copy-start | bytes 6291460
  4.1 77.3 %copy-start.2 = (bf16[1,128,2048]{1,2,0:T(8,128)(2,1)}, bf16[1,128,2048]{1,2,0:T(8,128)(2,1)S(1)}, u32[]{:S(2)}) copy-start(bf16[1,128,2048]{1,2,0:T(8,128)(2,1)S(1)} %copy.25) | copy-start | bytes 1572868
  5.6 1.2 copy-start.4
  7.9 0.7 copy-start.6
  8.8 71.3 %copy-start.5 = (f32[1,32,128]{2,1,0:T(8,128)S(1)}, f32[1,32,128]{2,1,0:T(8,128)}, u32[]{:S(2)}) copy-start(f32[1,32,128]{2,1,0:T(8,128)} %param.10) | copy-start | bytes 49156
  79.6 1.8 %copy-start.1 = (f32[32,128,128]{2,1,0:T(8,128)}, f32[32,128,128]{2,1,0:T(8,128)S(1)}, u32[]{:S(2)}) copy-start(f32[32,128,128]{2,1,0:T(8,128)S(1)} %shard_map.86) | copy-start | bytes 6291460
  83.7 44.8 %copy-start.3 = (bf16[1,128,2048]{1,2,0:T(8,128)(2,1)S(1)}, bf16[1,128,2048]{1,2,0:T(8,128)(2,1)}, u32[]{:S(2)}) copy-start(bf16[1,128,2048]{1,2,0:T(8,128)(2,1)} %copy-done.2) | copy-start | bytes 1572868
  83.7 44.8 %copy-start.7 = (f32[32]{0:T(128)S(1)}, f32[32]{0:T(128)}, u32[]{:S(2)}) copy-start(f32[32]{0:T(128)} %param.12) | copy-start | bytes 388

commit v14 on v13

--- a/solution.py
+++ b/solution.py
@@ -180,8 +180,14 @@
 
         row_place = lambda m: (chip, core, z, m)
         col_place = lambda m: (chip, core, m, y)
+        def span_of(w):
+            return pl.ds(0, part + 8 if w == 0 else part)
+
         t1 = [
-            tier(lambda m, w=w: pay.at[pl.ds(m * group, group), w], land1.at[w, y], width, y, row_place, w, 0, 0)
+            tier(
+                lambda m, w=w: pay.at[pl.ds(m * group, group), w, span_of(w)],
+                land1.at[w, y, :, span_of(w)], width, y, row_place, w, 0, 0,
+            )
             for w in range(waves)
         ]
         t2 = []
@@ -197,7 +203,9 @@
                     total = total + mark
                 agg[w, k, :part] = carry
                 agg[w, k, part:] = jnp.broadcast_to(total * (1 if w == 0 else 0), (8, cols))
-            t2.append(tier(lambda m, w=w: agg.at[w, m], land2.at[w, z], layers, z, col_place, w, width - 1, 1))
+            t2.append(tier(
+                lambda m, w=w: agg.at[w, m, span_of(w)], land2.at[w, z, span_of(w)], layers, z, col_place, w, width - 1, 1,
+            ))
         t3 = []
         for w in range(waves):
             finish(t2[w])

time: 134 us -> 128 us (0.955)
  Pallas kernels: 114 us -> 109 us
    pallas_call x1, Pallas kernels: 70.8 us -> 65.7 us  [tiered_exchange(): pl.pallas_call(kernel, out_shape=jax.ShapeDtypeStruct((heads, 2 * rows, c...]
where the time goes in v14:
time: 128 us; the launch traced here: 126 us
  Pallas kernels  109 us (85%)
  local copies, waits for them, and re-layouts  7.82 us (6%)
  matrix products  6.18 us (5%)
  other arithmetic  2.61 us (2%)
    pallas_call x1, Pallas kernels, tiered_exchange(): pl.pallas_call(kernel, out_shape=jax.ShapeDtypeStruct((heads, 2 * rows, c...  65.7 us
    pallas_call x1, Pallas kernels, weight_grad_sum(): pl.pallas_call(kernel, out_shape=jax.ShapeDtypeStruct((piece, cols), jnp....  43.3 us
    unnamed x20, local copies, waits for them, and re-layouts  5.73 us

profile of v14, /device:TPU:32, one launch (start us, length us, event | category | flops | bytes accessed | tf_op | source)
XLA Modules:
  0.0 126.5 jit_solution(6306343141803079541)
XLA Ops:
  0.6 0.0 copy-start
  0.6 1.1 reduce_window_sum.17
  1.8 0.2 slice_reduce_fusion
  2.0 0.8 multiply_bitcast_fusion
  2.8 1.3 %copy.25 = bf16[1,128,2048]{1,2,0:T(8,128)(2,1)S(1)} copy(bf16[1,128,2048]{2,1,0:T(8,128)(2,1)} %param.13) | data formatting | bytes 1048576 | tf_op args[6]
  4.1 0.0 copy-start.2
  4.1 1.5 %copy.26 = bf16[1,128,2048]{1,2,0:T(8,128)(2,1)S(1)} copy(bf16[1,128,2048]{2,1,0:T(8,128)(2,1)} %param.9) | data formatting | bytes 1048576 | tf_op args[2]
  5.6 0.0 copy-start.4
  5.6 0.2 fusion.7
  5.9 0.0 copy-done
  5.9 1.0 copy-done.4
  6.8 0.4 convolution_convert_fusion
  7.3 0.3 convolution_add_fusion.1
  7.6 0.1 fusion.34
  7.7 0.1 broadcast_in_dim.73
  7.9 0.0 copy-start.6
  7.9 0.3 convolution_add_fusion
  8.3 0.3 copy-done.6
  8.5 0.1 fusion.15
  8.7 0.2 pad_maximum_fusion.pay
  8.8 0.0 copy-start.5
  8.8 65.7 %shard_map.86 = f32[32,128,128]{2,1,0:T(8,128)S(1)} custom-call(f32[32,4,40,128]{3,2,1,0:T(8,128)S(1)} %pad_maximum_fusion.pay), custom_call_target="tpu_custom_call" | custom-call | tf_op jit(solution)/shard_map/pallas_call | solution.py:241
  74.5 0.0 copy-start.1
  74.5 0.4 convolution_bitcast_fusion.2
  75.0 0.0 copy-done.5
  75.0 1.1 multiply_reduce_fusion
  76.1 0.2 fusion.4
  76.3 0.0 copy-done.2
  76.3 0.0 copy-done.1
  76.3 0.4 convolution_bitcast_fusion.1
  76.8 0.1 fusion.5
  76.9 1.6 %copy.31 = bf16[4096,128]{1,0:T(8,128)(2,1)S(1)} copy(bf16[4096,128]{0,1:T(8,128)(2,1)} %bitcast.84) | data formatting | bytes 2097152 | tf_op jit(solution)/shard_map/transpose | solution.py:280
  78.6 0.0 copy-start.3
  78.6 0.0 copy-start.7
  78.6 43.3 %shard_map.87 = f32[16,256]{1,0:T(8,128)S(1)} custom-call(bf16[4,2,512,128]{3,2,1,0:T(8,128)(2,1)S(1)} %bitcast.78, bf16[128,256]{1,0:T(8,128)(2,1)S(1)} %pad_maximum_fusion.1.gp_ref), custom_call_target="tpu_custom_call" | custom-call | tf_op jit(solution)/shard_map/pallas_call | solution.py:370
  121.9 0.1 exponential_bitcast_fusion.1
  122.0 1.6 %convolution_multiply_fusion = f32[128,32,64]{0,2,1:T(8,128)S(1)} fusion(f32[128,32]{0,1:T(8,128)S(1)} %exponential_bitcast_fusion.1, bf16[128,256]{1,0:T(8,128)(2,1)S(1)} %convolution_convert_fusion, f32[32,128,128]{2,1,0:T(8,128)} %copy-done.1, f32[32]{0:T(128)S(1)} %get-tuple-element.70), kind=kOutput, calls=%fused_computation.8 | convolution fusion | flops 67895296 | bytes 2146816 | tf_op jit(solution)/shard_map/while/body/eval_jaxpr/hpn,jn->jhp/dot_general | solution.py:74
  123.6 0.1 fusion.25
  123.7 0.0 copy-done.3
  123.7 0.0 copy-done.7
  123.7 1.2 fusion.3
  124.9 1.0 copy.37
  125.9 0.6 copy.45
  (7 shorter events, 0.2 us)
Async XLA Ops:
  0.6 5.2 %copy-start = (bf16[4096,256]{1,0:T(8,128)(2,1)S(1)}, bf16[4096,256]{1,0:T(8,128)(2,1)}, u32[]{:S(2)}) copy-start(bf16[4096,256]{1,0:T(8,128)(2,1)} %param.8) | copy-start | bytes 6291460
  4.1 72.2 %copy-start.2 = (bf16[1,128,2048]{1,2,0:T(8,128)(2,1)}, bf16[1,128,2048]{1,2,0:T(8,128)(2,1)S(1)}, u32[]{:S(2)}) copy-start(bf16[1,128,2048]{1,2,0:T(8,128)(2,1)S(1)} %copy.25) | copy-start | bytes 1572868
  5.6 1.2 copy-start.4
  7.9 0.7 copy-start.6
  8.8 66.2 %copy-start.5 = (f32[1,32,128]{2,1,0:T(8,128)S(1)}, f32[1,32,128]{2,1,0:T(8,128)}, u32[]{:S(2)}) copy-start(f32[1,32,128]{2,1,0:T(8,128)} %param.10) | copy-start | bytes 49156
  74.5 1.8 %copy-start.1 = (f32[32,128,128]{2,1,0:T(8,128)}, f32[32,128,128]{2,1,0:T(8,128)S(1)}, u32[]{:S(2)}) copy-start(f32[32,128,128]{2,1,0:T(8,128)S(1)} %shard_map.86) | copy-start | bytes 6291460
  78.6 45.1 %copy-start.3 = (bf16[1,128,2048]{1,2,0:T(8,128)(2,1)S(1)}, bf16[1,128,2048]{1,2,0:T(8,128)(2,1)}, u32[]{:S(2)}) copy-start(bf16[1,128,2048]{1,2,0:T(8,128)(2,1)} %copy-done.2) | copy-start | bytes 1572868
  78.6 45.1 %copy-start.7 = (f32[32]{0:T(128)S(1)}, f32[32]{0:T(128)}, u32[]{:S(2)}) copy-start(f32[32]{0:T(128)} %param.12) | copy-start | bytes 388

commit v15 on v14

--- a/solution.py
+++ b/solution.py
@@ -328,40 +328,47 @@
             ))
         for copy in second:
             copy.start()
-        for copy in second:
+        base = chips + width
+        third_a = []
+        for copy in second[: chips - 1]:
             copy.wait()
         total = acc_a[chip]
         for step in range(1, chips):
             total = total + land_a[step - 1]
         sum_a[...] = total.reshape(count, piece, half)
+        for step in range(1, count):
+            dest = (me + step) % count
+            third_a.append(pltpu.make_async_remote_copy(
+                src_ref=sum_a.at[dest], dst_ref=fin_a.at[step - 1], send_sem=sems.at[0, base + step],
+                recv_sem=sems.at[1, base + step], device_id=(chip, core, dest // width, dest % width),
+                device_id_type=mesh_id,
+            ))
+        for copy in third_a:
+            copy.start()
+        third_b = []
+        for copy in second[chips - 1 :]:
+            copy.wait()
         total = acc_b[y]
         for step in range(1, width):
             total = total + land_b[step - 1]
         sum_b[...] = total.reshape(chips * layers, piece, half)
-        base = chips + width
-        third = []
-        for step in range(1, count):
-            dest = (me + step) % count
-            third.append(pltpu.make_async_remote_copy(
-                src_ref=sum_a.at[dest], dst_ref=fin_a.at[step - 1], send_sem=sems.at[0, base + step],
-                recv_sem=sems.at[1, base + step], device_id=(chip, core, dest // width, dest % width),
-                device_id_type=mesh_id,
-            ))
         for step in range(1, chips * layers):
             dest = (spot + step) % (chips * layers)
-            third.append(pltpu.make_async_remote_copy(
+            third_b.append(pltpu.make_async_remote_copy(
                 src_ref=sum_b.at[dest], dst_ref=fin_b.at[step - 1], send_sem=sems.at[0, base + ring + step],
                 recv_sem=sems.at[1, base + ring + step], device_id=(dest // layers, core, dest % layers, y),
                 device_id_type=mesh_id,
             ))
-        for copy in third:
+        for copy in third_b:
             copy.start()
-        for copy in third:
+        for copy in third_a:
             copy.wait()
         total = sum_a[me]
         for step in range(1, count):
             total = total + fin_a[step - 1]
         out_ref[:, :half] = total * scale
+        for copy in third_b:
+            copy.wait()
         total = sum_b[spot]
         for step in range(1, chips * layers):
             total = total + fin_b[step - 1]

time: 128 us -> 128 us (level)
  no operation moved by 1% of the time
where the time goes in v15:
time: 128 us; the launch traced here: 126 us
  Pallas kernels  108 us (84%)
  local copies, waits for them, and re-layouts  7.82 us (6%)
  matrix products  6.18 us (5%)
  other arithmetic  2.61 us (2%)
    pallas_call x1, Pallas kernels, tiered_exchange(): pl.pallas_call(kernel, out_shape=jax.ShapeDtypeStruct((heads, 2 * rows, c...  65.7 us
    pallas_call x1, Pallas kernels, weight_grad_sum(): pl.pallas_call(kernel, out_shape=jax.ShapeDtypeStruct((piece, cols), jnp....  42.6 us
    unnamed x20, local copies, waits for them, and re-layouts  5.73 us

profile of v15, /device:TPU:32, one launch (start us, length us, event | category | flops | bytes accessed | tf_op | source)
XLA Modules:
  0.0 125.8 jit_solution(6833784034848327473)
XLA Ops:
  0.6 0.0 copy-start
  0.6 1.1 reduce_window_sum.17
  1.8 0.2 slice_reduce_fusion
  2.0 0.8 multiply_bitcast_fusion
  2.8 1.3 %copy.25 = bf16[1,128,2048]{1,2,0:T(8,128)(2,1)S(1)} copy(bf16[1,128,2048]{2,1,0:T(8,128)(2,1)} %param.13) | data formatting | bytes 1048576 | tf_op args[6]
  4.1 0.0 copy-start.2
  4.1 1.5 %copy.26 = bf16[1,128,2048]{1,2,0:T(8,128)(2,1)S(1)} copy(bf16[1,128,2048]{2,1,0:T(8,128)(2,1)} %param.9) | data formatting | bytes 1048576 | tf_op args[2]
  5.6 0.0 copy-start.4
  5.6 0.2 fusion.7
  5.9 0.0 copy-done
  5.9 1.0 copy-done.4
  6.8 0.4 convolution_convert_fusion
  7.3 0.3 convolution_add_fusion.1
  7.6 0.1 fusion.34
  7.7 0.1 broadcast_in_dim.73
  7.9 0.0 copy-start.6
  7.9 0.3 convolution_add_fusion
  8.3 0.3 copy-done.6
  8.5 0.1 fusion.15
  8.7 0.2 pad_maximum_fusion.pay
  8.8 0.0 copy-start.5
  8.8 65.7 %shard_map.86 = f32[32,128,128]{2,1,0:T(8,128)S(1)} custom-call(f32[32,4,40,128]{3,2,1,0:T(8,128)S(1)} %pad_maximum_fusion.pay), custom_call_target="tpu_custom_call" | custom-call | tf_op jit(solution)/shard_map/pallas_call | solution.py:241
  74.5 0.0 copy-start.1
  74.5 0.4 convolution_bitcast_fusion.2
  75.0 0.0 copy-done.5
  75.0 1.1 multiply_reduce_fusion
  76.1 0.2 fusion.4
  76.3 0.0 copy-done.2
  76.3 0.0 copy-done.1
  76.3 0.4 convolution_bitcast_fusion.1
  76.8 0.1 fusion.5
  76.9 1.6 %copy.31 = bf16[4096,128]{1,0:T(8,128)(2,1)S(1)} copy(bf16[4096,128]{0,1:T(8,128)(2,1)} %bitcast.84) | data formatting | bytes 2097152 | tf_op jit(solution)/shard_map/transpose | solution.py:280
  78.6 0.0 copy-start.3
  78.6 0.0 copy-start.7
  78.6 42.6 %shard_map.87 = f32[16,256]{1,0:T(8,128)S(1)} custom-call(bf16[4,2,512,128]{3,2,1,0:T(8,128)(2,1)S(1)} %bitcast.78, bf16[128,256]{1,0:T(8,128)(2,1)S(1)} %pad_maximum_fusion.1.gp_ref), custom_call_target="tpu_custom_call" | custom-call | tf_op jit(solution)/shard_map/pallas_call | solution.py:377
  121.2 0.1 exponential_bitcast_fusion.1
  121.3 1.6 %convolution_multiply_fusion = f32[128,32,64]{0,2,1:T(8,128)S(1)} fusion(f32[128,32]{0,1:T(8,128)S(1)} %exponential_bitcast_fusion.1, bf16[128,256]{1,0:T(8,128)(2,1)S(1)} %convolution_convert_fusion, f32[32,128,128]{2,1,0:T(8,128)} %copy-done.1, f32[32]{0:T(128)S(1)} %get-tuple-element.70), kind=kOutput, calls=%fused_computation.8 | convolution fusion | flops 67895296 | bytes 2146816 | tf_op jit(solution)/shard_map/while/body/eval_jaxpr/hpn,jn->jhp/dot_general | solution.py:74
  122.9 0.1 fusion.25
  123.0 0.0 copy-done.3
  123.0 0.0 copy-done.7
  123.0 1.2 fusion.3
  124.2 1.0 copy.37
  125.2 0.6 copy.45
  (7 shorter events, 0.2 us)
Async XLA Ops:
  0.6 5.2 %copy-start = (bf16[4096,256]{1,0:T(8,128)(2,1)S(1)}, bf16[4096,256]{1,0:T(8,128)(2,1)}, u32[]{:S(2)}) copy-start(bf16[4096,256]{1,0:T(8,128)(2,1)} %param.8) | copy-start | bytes 6291460
  4.1 72.2 %copy-start.2 = (bf16[1,128,2048]{1,2,0:T(8,128)(2,1)}, bf16[1,128,2048]{1,2,0:T(8,128)(2,1)S(1)}, u32[]{:S(2)}) copy-start(bf16[1,128,2048]{1,2,0:T(8,128)(2,1)S(1)} %copy.25) | copy-start | bytes 1572868
  5.6 1.2 copy-start.4
  7.9 0.7 copy-start.6
  8.8 66.2 %copy-start.5 = (f32[1,32,128]{2,1,0:T(8,128)S(1)}, f32[1,32,128]{2,1,0:T(8,128)}, u32[]{:S(2)}) copy-start(f32[1,32,128]{2,1,0:T(8,128)} %param.10) | copy-start | bytes 49156
  74.5 1.8 %copy-start.1 = (f32[32,128,128]{2,1,0:T(8,128)}, f32[32,128,128]{2,1,0:T(8,128)S(1)}, u32[]{:S(2)}) copy-start(f32[32,128,128]{2,1,0:T(8,128)S(1)} %shard_map.86) | copy-start | bytes 6291460
  78.6 44.5 %copy-start.3 = (bf16[1,128,2048]{1,2,0:T(8,128)(2,1)S(1)}, bf16[1,128,2048]{1,2,0:T(8,128)(2,1)}, u32[]{:S(2)}) copy-start(bf16[1,128,2048]{1,2,0:T(8,128)(2,1)} %copy-done.2) | copy-start | bytes 1572868
  78.6 44.5 %copy-start.7 = (f32[32]{0:T(128)S(1)}, f32[32]{0:T(128)}, u32[]{:S(2)}) copy-start(f32[32]{0:T(128)} %param.12) | copy-start | bytes 388

commit v16 on v15

--- a/solution.py
+++ b/solution.py
@@ -146,8 +146,8 @@
     heads, span, cols = payload.shape
     rows = (span - 8) // 2
     group = heads // width
-    part = rows // 2
-    waves = 4
+    waves = 8
+    part = rows * 2 // waves
     mesh_id = pl.DeviceIdType.MESH
     per_wave = 2 * (width - 1) + 2 * (layers - 1)
 
@@ -196,7 +196,7 @@
             for k in range(group):
                 carry = jnp.zeros((part, cols), jnp.float32)
                 total = jnp.zeros((1, cols), jnp.float32)
-                order = range(width) if w < 2 else reversed(range(width))
+                order = range(width) if w < waves // 2 else reversed(range(width))
                 for m in order:
                     mark = land1[0, m, k, part : part + 1]
                     carry = jnp.exp(mark) * carry + land1[w, m, k, :part]
@@ -210,7 +210,7 @@
         for w in range(waves):
             finish(t2[w])
             carry = jnp.zeros((part, cols), jnp.float32)
-            order = range(layers) if w < 2 else reversed(range(layers))
+            order = range(layers) if w < waves // 2 else reversed(range(layers))
             for r in order:
                 res[w, r] = carry
                 carry = jnp.exp(land2[0, r, part : part + 1]) * carry + land2[w, r, :part]
@@ -220,7 +220,7 @@
             finish(t3[w])
             for k in range(group):
                 carry = land3[w, k]
-                order = range(width) if w < 2 else reversed(range(width))
+                order = range(width) if w < waves // 2 else reversed(range(width))
                 for m in order:
                     out4[w, m, k] = carry
                     carry = jnp.exp(land1[0, m, k, part : part + 1]) * carry + land1[w, m, k, :part]

time: 128 us -> 126 us (0.984)
    unnamed x20 -> x25, local copies, waits for them, and re-layouts: 5.73 us -> 5.86 us
where the time goes in v16:
time: 126 us; the launch traced here: 125 us
  Pallas kernels  107 us (85%)
  local copies, waits for them, and re-layouts  7.93 us (6%)
  matrix products  6.17 us (5%)
  other arithmetic  2.4 us (2%)
    pallas_call x1, Pallas kernels, tiered_exchange(): pl.pallas_call(kernel, out_shape=jax.ShapeDtypeStruct((heads, 2 * rows, c...  65.7 us
    pallas_call x1, Pallas kernels, weight_grad_sum(): pl.pallas_call(kernel, out_shape=jax.ShapeDtypeStruct((piece, cols), jnp....  41.6 us
    unnamed x25, local copies, waits for them, and re-layouts  5.86 us

profile of v16, /device:TPU:32, one launch (start us, length us, event | category | flops | bytes accessed | tf_op | source)
XLA Modules:
  0.0 124.7 jit_solution(4303427962402450832)
XLA Ops:
  0.6 0.0 copy-start
  0.6 1.1 reduce_window_sum.17
  1.8 0.2 slice_reduce_fusion
  2.0 0.8 exponential_bitcast_fusion
  2.8 1.3 %copy.29 = bf16[1,128,2048]{1,2,0:T(8,128)(2,1)S(1)} copy(bf16[1,128,2048]{2,1,0:T(8,128)(2,1)} %param.13) | data formatting | bytes 1048576 | tf_op args[6]
  4.1 0.0 copy-start.2
  4.1 1.5 %copy.30 = bf16[1,128,2048]{1,2,0:T(8,128)(2,1)S(1)} copy(bf16[1,128,2048]{2,1,0:T(8,128)(2,1)} %param.9) | data formatting | bytes 1048576 | tf_op args[2]
  5.6 0.0 copy-start.4
  5.6 0.2 fusion.7
  5.9 0.0 copy-done
  5.9 1.0 copy-done.4
  6.8 0.4 convolution_convert_fusion
  7.3 0.3 convolution_add_fusion.1
  7.6 0.1 fusion.37
  7.7 0.1 broadcast_in_dim.73
  7.8 0.0 copy-start.6
  8.0 0.3 convolution_add_fusion
  8.3 0.2 copy-done.6
  8.4 0.1 fusion.20
  8.6 0.1 fusion.36
  8.8 0.0 copy-start.5
  8.8 65.7 %shard_map.86 = f32[32,128,128]{2,1,0:T(8,128)S(1)} custom-call(f32[32,8,24,128]{3,2,1,0:T(8,128)S(1)} %bitcast_dynamic-update-slice_fusion.5.pay), custom_call_target="tpu_custom_call" | custom-call | tf_op jit(solution)/shard_map/pallas_call | solution.py:241
  74.4 0.0 copy-start.1
  74.5 0.4 convolution_bitcast_fusion.2
  74.9 0.0 copy-done.5
  74.9 1.1 multiply_reduce_fusion
  76.1 0.2 fusion.4
  76.2 0.0 copy-done.2
  76.3 0.0 copy-done.1
  76.3 0.4 convolution_bitcast_fusion.1
  76.7 0.1 fusion.5
  76.9 1.6 %copy.39 = bf16[4096,128]{1,0:T(8,128)(2,1)S(1)} copy(bf16[4096,128]{0,1:T(8,128)(2,1)} %bitcast.104) | data formatting | bytes 2097152 | tf_op jit(solution)/shard_map/transpose | solution.py:280
  78.5 0.0 copy-start.3
  78.5 0.0 copy-start.7
  78.5 41.6 %shard_map.87 = f32[16,256]{1,0:T(8,128)S(1)} custom-call(bf16[4,2,512,128]{3,2,1,0:T(8,128)(2,1)S(1)} %bitcast.98, bf16[128,256]{1,0:T(8,128)(2,1)S(1)} %pad_maximum_fusion.gp_ref), custom_call_target="tpu_custom_call" | custom-call | tf_op jit(solution)/shard_map/pallas_call | solution.py:377
  120.1 0.1 exponential_bitcast_fusion.1
  120.2 1.6 %convolution_multiply_fusion = f32[128,32,64]{0,2,1:T(8,128)S(1)} fusion(f32[128,32]{0,1:T(8,128)S(1)} %exponential_bitcast_fusion.1, bf16[128,256]{1,0:T(8,128)(2,1)S(1)} %convolution_convert_fusion, f32[32,128,128]{2,1,0:T(8,128)} %copy-done.1, f32[32]{0:T(128)S(1)} %get-tuple-element.75), kind=kOutput, calls=%fused_computation.7 | convolution fusion | flops 67895296 | bytes 2146816 | tf_op jit(solution)/shard_map/while/body/eval_jaxpr/hpn,jn->jhp/dot_general | solution.py:74
  121.8 0.1 fusion.27
  121.9 0.0 copy-done.3
  121.9 0.0 copy-done.7
  121.9 1.2 fusion.3
  123.1 1.0 copy.45
  124.1 0.6 copy.60
  (10 shorter events, 0.3 us)
Async XLA Ops:
  0.6 5.2 %copy-start = (bf16[4096,256]{1,0:T(8,128)(2,1)S(1)}, bf16[4096,256]{1,0:T(8,128)(2,1)}, u32[]{:S(2)}) copy-start(bf16[4096,256]{1,0:T(8,128)(2,1)} %param.8) | copy-start | bytes 6291460
  4.1 72.1 %copy-start.2 = (bf16[1,128,2048]{1,2,0:T(8,128)(2,1)}, bf16[1,128,2048]{1,2,0:T(8,128)(2,1)S(1)}, u32[]{:S(2)}) copy-start(bf16[1,128,2048]{1,2,0:T(8,128)(2,1)S(1)} %copy.29) | copy-start | bytes 1572868
  5.6 1.2 copy-start.4
  7.8 0.7 copy-start.6
  8.8 66.2 %copy-start.5 = (f32[1,32,128]{2,1,0:T(8,128)S(1)}, f32[1,32,128]{2,1,0:T(8,128)}, u32[]{:S(2)}) copy-start(f32[1,32,128]{2,1,0:T(8,128)} %param.10) | copy-start | bytes 49156
  74.4 1.8 %copy-start.1 = (f32[32,128,128]{2,1,0:T(8,128)}, f32[32,128,128]{2,1,0:T(8,128)S(1)}, u32[]{:S(2)}) copy-start(f32[32,128,128]{2,1,0:T(8,128)S(1)} %shard_map.86) | copy-start | bytes 6291460
  78.5 43.4 %copy-start.3 = (bf16[1,128,2048]{1,2,0:T(8,128)(2,1)S(1)}, bf16[1,128,2048]{1,2,0:T(8,128)(2,1)}, u32[]{:S(2)}) copy-start(bf16[1,128,2048]{1,2,0:T(8,128)(2,1)} %copy-done.2) | copy-start | bytes 1572868
  78.5 43.4 %copy-start.7 = (f32[32]{0:T(128)S(1)}, f32[32]{0:T(128)}, u32[]{:S(2)}) copy-start(f32[32]{0:T(128)} %param.12) | copy-start | bytes 388
